TPU v7x, 32 devices: a whole 2x2x4 slice. The times are simulated.
32 devices in a mesh: dp: 4 (over y, x), expert: 8 (over z, core).
Axes of the slice: x: 2, y: 2, z: 4, core: 2. Of those that a mesh axis runs over, the one named last changes fastest.
Arguments:
- tokens: bfloat16 [4, 32, 64, 1024], P('dp', 'expert'), may hold values from -6 to 6
- route_ids: int32 [4, 32, 64, 2], P('dp', 'expert'), may hold values from 0 to 7, as said below
- slot_ids: int32 [4, 32, 64, 2], P('dp', 'expert'), may hold values from 0 to 95, as said below
- router: float32 [1024, 8], replicated, may hold values from -0.1875 to 0.1875
- expert_in: bfloat16 [8, 4096, 1024], P('expert'), may hold values from -0.1875 to 0.1875
- expert_out: bfloat16 [8, 4096, 1024], P('expert'), may hold values from -0.09375 to 0.09375
- conv_weight: bfloat16 [3, 3, 1024, 512], P(None, None, 'dp', 'expert'), may hold values from -0.0625 to 0.0625
Outputs:
- joined: bfloat16 [4, 32, 64, 512], P('dp', 'expert')
Inputs may be any that keep to these rules, and one draw needn't show every extreme that they name: `route_ids`: the two experts of a patch differ. In each routing block (its 256 patches) no expert is named by more than 96 patches, and every expert is named in every block. `slot_ids`: within a routing block the pairs (expert, slot) of all patches and both routes are distinct. In every block one expert has all 96 slots in use, the same expert in all blocks of one image group.
All inputs are finite; a program needn't handle non-finite values.
Results may differ from a plain program's by a relative error of at most 0.0056.
Values may be sent and summed in bfloat16 or wider, within the bound.
No kernel may reach another device: no remote copies, remote signals or barrier semaphores. Data moves between devices by JAX's collectives and lax.ppermute only.
A program may use at most 128 MiB of HBM per device.

v0:
```python
import jax
import jax.numpy as jnp
from jax import lax
from jax.experimental import pallas as pl
from jax.experimental.pallas import tpu as pltpu
from jax.sharding import PartitionSpec as P


F32 = jnp.float32
BF16 = jnp.bfloat16
VM = pl.BlockSpec(memory_space=pltpu.VMEM)
SM = pl.BlockSpec(memory_space=pltpu.SMEM)
ANY = pl.BlockSpec(memory_space=pl.ANY)
PARAMS = pltpu.CompilerParams(vmem_limit_bytes=24 * 2**20)


def prologue(tok, cells, experts, cap):
    count, width = tok.shape

    def kernel(tok_ref, cells_ref, normed_ref, *blocks):
        x = tok_ref[...].astype(F32)
        centred = x - jnp.mean(x, axis=-1, keepdims=True)
        var = jnp.mean(centred * centred, axis=-1, keepdims=True)
        normed = (centred * lax.rsqrt(var + 1e-06)).astype(BF16)
        normed_ref[...] = normed
        first, second = cells_ref[0:1, :], cells_ref[1:2, :]
        for k in range(experts):
            rows = lax.broadcasted_iota(jnp.int32, (cap, count), 0) + k * cap
            hot = ((rows == first) | (rows == second)).astype(F32).astype(BF16)
            blocks[k][...] = jnp.dot(hot, normed, preferred_element_type=F32).astype(BF16)

    outs = [jax.ShapeDtypeStruct((count, width), BF16)]
    outs += [jax.ShapeDtypeStruct((cap, width), BF16)] * experts
    res = pl.pallas_call(
        kernel, out_shape=outs, in_specs=[VM, VM], out_specs=[VM] * len(outs),
        compiler_params=PARAMS, name="prologue",
    )(tok, cells)
    return res[0], res[1:]


def mlp(blocks, w_in, w_out, step=512):
    n, (cap, width) = len(blocks), blocks[0].shape
    steps = w_in.shape[0] // step

    def kernel(*refs):
        xs, (wi, wo), outs, (x_scr, acc) = refs[:n], refs[n : n + 2], refs[n + 2 : 2 * n + 2], refs[2 * n + 2 :]
        for k in range(n):
            x_scr[k * cap : (k + 1) * cap, :] = xs[k][...]
        acc[...] = jnp.zeros_like(acc)

        def body(i, carry):
            rows = pl.ds(pl.multiple_of(i * step, step), step)
            h = lax.dot_general(x_scr[...], wi[rows, :], (((1,), (1,)), ((), ())), preferred_element_type=F32)
            act = (0.5 * h * (1.0 + lax.erf(h * 0.7071067811865476))).astype(BF16)
            acc[...] += jnp.dot(act, wo[rows, :], preferred_element_type=F32)
            return carry

        lax.fori_loop(0, steps, body, 0)
        for k in range(n):
            outs[k][...] = acc[k * cap : (k + 1) * cap, :].astype(BF16)

    return pl.pallas_call(
        kernel, in_specs=[VM] * (n + 2), out_specs=[VM] * n,
        out_shape=[jax.ShapeDtypeStruct((cap, width), BF16)] * n,
        scratch_shapes=[pltpu.VMEM((n * cap, width), BF16), pltpu.VMEM((n * cap, width), F32)],
        compiler_params=pltpu.CompilerParams(vmem_limit_bytes=16 * 2**20),
    )(*blocks, w_in, w_out)


def combine(tok, gates, cells, results, edge):
    count, width = tok.shape
    n, cap = len(results), results[0].shape[0]

    def kernel(tok_ref, gates_ref, cells_ref, *refs):
        res, (mixed_ref, low_ref, high_ref, scr) = refs[:n], refs[n:]
        for k in range(n):
            scr[k * cap : (k + 1) * cap, :] = res[k][...]
        cols = lax.broadcasted_iota(jnp.int32, (count, n * cap), 1)
        total = jnp.zeros((count, width), F32)
        for k in range(2):
            hot = (cols == cells_ref[:, k : k + 1]).astype(F32).astype(BF16)
            picked = jnp.dot(hot, scr[...], preferred_element_type=F32)
            total = total + picked * gates_ref[:, k : k + 1]
        mixed = (tok_ref[...].astype(F32) + total).astype(BF16)
        mixed_ref[...] = mixed
        low_ref[...] = mixed[:edge, :]
        high_ref[...] = mixed[count - edge :, :]

    outs = [jax.ShapeDtypeStruct((r, width), BF16) for r in (count, edge, edge)]
    return pl.pallas_call(
        kernel, out_shape=outs, in_specs=[VM] * (3 + n), out_specs=[VM] * 3,
        scratch_shapes=[pltpu.VMEM((n * cap, width), BF16)],
        compiler_params=PARAMS, name="combine",
    )(tok, gates, cells, *results)


def assemble(place, own, ups, downs, lanes):
    rows, packed = own.shape
    fold, n = packed // lanes, len(ups) + 1

    def kernel(place_ref, *refs):
        z, out = place_ref[0], refs[-1]
        share = [refs[0][...]] + [r[...] for r in refs[1:-1]]
        for p in range(n):
            piece = share[0]
            for k in range(1, n):
                if p >= k:
                    piece = jnp.where(z == p - k, share[n - 1 + k], piece)
                if p + k < n:
                    piece = jnp.where(z == p + k, share[k], piece)
            for f in range(fold):
                out[f * rows : (f + 1) * rows, p * lanes : (p + 1) * lanes] = piece[:, f * lanes : (f + 1) * lanes]

    return pl.pallas_call(
        kernel, out_shape=jax.ShapeDtypeStruct((rows * fold, lanes * n), BF16),
        in_specs=[SM] + [VM] * (2 * n - 1), out_specs=VM, compiler_params=PARAMS, name="assemble",
    )(place, own, *ups, *downs)


def conv(place, mixed, top, bottom, mine, theirs, lanes):
    count, _ = mixed.shape
    edge = top.shape[0]
    quarters = len(mine)
    chans, cols = mine[0].shape[0] // 9, mine[0].shape[1]
    n = cols // lanes

    def kernel(place_ref, mixed_ref, top_ref, bottom_ref, *refs):
        weights, (out, x_scr, w_scr, sems) = refs[: 2 * quarters], refs[2 * quarters :]
        copies = [pltpu.make_async_copy(w, w_scr.at[i], sems.at[i]) for i, w in enumerate(weights)]
        for c in copies:
            c.start()
        for q in range(quarters):
            x_scr[q, 0:edge, :] = top_ref[:, q * chans : (q + 1) * chans]
            x_scr[q, edge : edge + count, :] = mixed_ref[:, q * chans : (q + 1) * chans]
            x_scr[q, edge + count :, :] = bottom_ref[:, q * chans : (q + 1) * chans]
        col = lax.broadcasted_iota(jnp.int32, (count, cols), 0) % edge
        accs = [[jnp.zeros((count, cols), F32) for _ in range(3)] for _ in range(2)]
        for k in range(quarters):
            for r in range(2):
                i = 2 * k + r
                copies[i].wait()
                for a in range(3):
                    x = x_scr[place_ref[1] ^ k, a * edge : a * edge + count, :]
                    for b in range(3):
                        t = 3 * a + b
                        accs[r][b] += jnp.dot(
                            x, w_scr[i, t * chans : (t + 1) * chans, :], preferred_element_type=F32
                        )
        halves = []
        for r in range(2):
            left = jnp.where(col == 0, 0.0, pltpu.roll(accs[r][0], 1, 0))
            right = jnp.where(col == edge - 1, 0.0, pltpu.roll(accs[r][2], count - 1, 0))
            halves.append((left + accs[r][1] + right))
        even = jnp.where(place_ref[2] == 0, halves[0], halves[1]).astype(BF16)
        odd = jnp.where(place_ref[2] == 0, halves[1], halves[0]).astype(BF16)
        for p in range(n):
            out[:, 2 * p * lanes : (2 * p + 1) * lanes] = even[:, p * lanes : (p + 1) * lanes]
            out[:, (2 * p + 1) * lanes : (2 * p + 2) * lanes] = odd[:, p * lanes : (p + 1) * lanes]

    weights = [w for pair in zip(mine, theirs) for w in pair]
    return pl.pallas_call(
        kernel, out_shape=jax.ShapeDtypeStruct((count, 2 * cols), BF16),
        in_specs=[SM, VM, VM, VM] + [ANY] * (2 * quarters), out_specs=VM,
        scratch_shapes=[
            pltpu.VMEM((quarters, count + 2 * edge, chans), BF16),
            pltpu.VMEM((2 * quarters, 9 * chans, cols), BF16),
            pltpu.SemaphoreType.DMA((2 * quarters,)),
        ],
        compiler_params=PARAMS, name="conv",
    )(place, mixed, top, bottom, *weights)


def flip(value, axis, k):
    return lax.ppermute(value, axis, [(i, i ^ k) for i in range(lax.axis_size(axis))])


def gather_filters(conv_weight, place):
    chans, lanes = conv_weight.shape[2:]
    size, groups = lax.axis_size("expert"), lax.axis_size("dp")
    fold = 128 // lanes
    rows = 9 * chans // fold
    flat = conv_weight.reshape(9 * chans, lanes)
    own = jnp.concatenate([flat[f * rows : (f + 1) * rows] for f in range(fold)], axis=1)
    up, down = own, own
    ups, downs = [], []
    for _ in range(1, size // 2):
        up = lax.ppermute(up, "expert", [(i, i + 2) for i in range(size - 2)])
        down = lax.ppermute(down, "expert", [(i + 2, i) for i in range(size - 2)])
        ups.append(up)
        downs.append(down)
    column = assemble(place, own, ups, downs, lanes)
    if groups == 4:
        x, y = flip(column, "dp", 1), flip(column, "dp", 2)
        half = column.shape[0] // 2
        across = [flip(y[:half], "dp", 1), flip(x[half:], "dp", 2)]
        mine = [column, x, y, jnp.concatenate(across, axis=0)]
    else:
        mine = [column] + [flip(column, "dp", k) for k in range(1, groups)]
    theirs = [flip(w, "expert", 1) for w in mine]
    return mine, theirs


def shards(tokens, route_ids, slot_ids, router, expert_in, expert_out, conv_weight):
    images, strip_rows, span_cols, width = tokens.shape
    count = images * strip_rows * span_cols
    experts = router.shape[1]
    cap = 3 * count // experts
    me = lax.axis_index("expert")
    place = jnp.stack([me // 2, lax.axis_index("dp"), me % 2]).astype(jnp.int32)
    tok = tokens.reshape(count, width)
    routes = route_ids.reshape(count, 2)
    cells = (routes ^ me) * cap + slot_ids.reshape(count, 2)
    normed, blocks = prologue(tok, cells.T, experts, cap)
    received = [blocks[0]] + [flip(blocks[k], "expert", k) for k in range(1, experts)]
    mine, theirs = gather_filters(conv_weight, place)
    half = experts // 2
    produced = list(mlp(received[:half], expert_in[0], expert_out[0]))
    produced += list(mlp(received[half:], expert_in[0], expert_out[0]))
    returned = [produced[0]] + [flip(produced[k], "expert", k) for k in range(1, experts)]
    logits = jnp.dot(normed.astype(F32), router, precision=lax.Precision.HIGHEST)
    matches = routes[:, :, None] == lax.broadcasted_iota(jnp.int32, (1, 1, experts), 2)
    gates = jax.nn.sigmoid(jnp.sum(jnp.where(matches, logits[:, None, :], 0.0), axis=2))
    mixed, low, high = combine(tok, gates, cells, returned, span_cols)
    top = lax.ppermute(high, "expert", [(i, i + 1) for i in range(experts - 1)])
    bottom = lax.ppermute(low, "expert", [(i + 1, i) for i in range(experts - 1)])
    out = conv(place, mixed, top, bottom, mine, theirs, conv_weight.shape[3])
    return out.reshape(images, strip_rows, span_cols, out.shape[1])


def solution(mesh):
    placed = (
        P("dp", "expert", None, None),
        P("dp", "expert", None, None),
        P("dp", "expert", None, None),
        P(),
        P("expert", None, None),
        P("expert", None, None),
        P(None, None, "dp", "expert"),
    )

    return jax.shard_map(shards, mesh=mesh, in_specs=placed, out_specs=P("dp", "expert", None, None), check_vma=False)
```

profile of v0, /device:TPU:1, one launch (start us, length us, event | category | flops | bytes accessed | tf_op | source)
XLA Modules:
  0.0 193.9 jit_solution(10890028392907558934)
XLA Ops:
  1.5 4.0 %collective-permute-start.16 = (bf16[1152,128]{1,0:T(8,128)(2,1)S(1)}, bf16[1152,128]{1,0:T(8,128)(2,1)S(1)}, u32[]{:S(2)}, u32[]{:S(2)}) collective-permute-start(bf16[1152,128]{1,0:T(8,128)(2,1)S(1)} %pad_maximum_fusion.refs_0_), channel_id=1, source_target_pairs={{0,2},{1,3},{2,4},{3,5},{4,6},{5,7},{8,10},{9,11},{10,12},{11,13},... | collective-permute-start | bytes 884744 | tf_op jit(solution)/shard_map/ppermute | solution.py:187
  6.9 4.4 %collective-permute-done.16.refs_1_ = bf16[1152,128]{1,0:T(8,128)(2,1)S(1)} collective-permute-done((bf16[1152,128]{1,0:T(8,128)(2,1)S(1)}, bf16[1152,128]{1,0:T(8,128)(2,1)S(1)}, u32[]{:S(2)}, u32[]{:S(2)}) %collective-permute-start.16) | collective-permute-done | bytes 294944 | tf_op jit(solution)/shard_map/ppermute | solution.py:187
  11.2 4.1 %collective-permute-start.17 = (bf16[1152,128]{1,0:T(8,128)(2,1)S(1)}, bf16[1152,128]{1,0:T(8,128)(2,1)S(1)}, u32[]{:S(2)}, u32[]{:S(2)}) collective-permute-start(bf16[1152,128]{1,0:T(8,128)(2,1)S(1)} %collective-permute-done.16.refs_1_), channel_id=1, source_target_pairs={{0,2},{1,3},{2,4},{3,5},{4,6},{5,7},{8,10},{9,11},{10,12},{11,13},... | collective-permute-start | bytes 884744 | tf_op jit(solution)/shard_map/ppermute | solution.py:187
  16.6 3.5 %collective-permute-done.17.refs_2_ = bf16[1152,128]{1,0:T(8,128)(2,1)S(1)} collective-permute-done((bf16[1152,128]{1,0:T(8,128)(2,1)S(1)}, bf16[1152,128]{1,0:T(8,128)(2,1)S(1)}, u32[]{:S(2)}, u32[]{:S(2)}) %collective-permute-start.17) | collective-permute-done | bytes 294944 | tf_op jit(solution)/shard_map/ppermute | solution.py:187
  20.1 4.1 %collective-permute-start.18 = (bf16[1152,128]{1,0:T(8,128)(2,1)S(1)}, bf16[1152,128]{1,0:T(8,128)(2,1)S(1)}, u32[]{:S(2)}, u32[]{:S(2)}) collective-permute-start(bf16[1152,128]{1,0:T(8,128)(2,1)S(1)} %collective-permute-done.17.refs_2_), channel_id=1, source_target_pairs={{0,2},{1,3},{2,4},{3,5},{4,6},{5,7},{8,10},{9,11},{10,12},{11,13},... | collective-permute-start | bytes 884744 | tf_op jit(solution)/shard_map/ppermute | solution.py:187
  25.7 2.5 %collective-permute-done.18.refs_3_ = bf16[1152,128]{1,0:T(8,128)(2,1)S(1)} collective-permute-done((bf16[1152,128]{1,0:T(8,128)(2,1)S(1)}, bf16[1152,128]{1,0:T(8,128)(2,1)S(1)}, u32[]{:S(2)}, u32[]{:S(2)}) %collective-permute-start.18) | collective-permute-done | bytes 294944 | tf_op jit(solution)/shard_map/ppermute | solution.py:187
  28.2 3.9 %collective-permute-done.21.refs_6_ = bf16[1152,128]{1,0:T(8,128)(2,1)S(1)} collective-permute-done((bf16[1152,128]{1,0:T(8,128)(2,1)S(1)}, bf16[1152,128]{1,0:T(8,128)(2,1)S(1)}, u32[]{:S(2)}, u32[]{:S(2)}) %collective-permute-start.21) | collective-permute-done | bytes 294944 | tf_op jit(solution)/shard_map/ppermute | solution.py:188
  36.2 21.4 %collective-permute-done.25.refs_4_ = bf16[2304,256]{1,0:T(8,128)(2,1)S(1)} collective-permute-done((bf16[2304,256]{1,0:T(8,128)(2,1)S(1)}, bf16[2304,256]{1,0:T(8,128)(2,1)S(1)}, u32[]{:S(2)}, u32[]{:S(2)}) %collective-permute-start.25) | collective-permute-done | bytes 1179680 | tf_op jit(solution)/shard_map/ppermute | solution.py:174
  60.9 4.6 %collective-permute-start = (bf16[96,1024]{1,0:T(8,128)(2,1)S(1)}, bf16[96,1024]{1,0:T(8,128)(2,1)S(1)}, u32[]{:S(2)}, u32[]{:S(2)}) collective-permute-start(bf16[96,1024]{1,0:T(8,128)(2,1)S(1)} %get-tuple-element.27), channel_id=1, source_target_pairs={{0,1},{1,0},{2,3},{3,2},{4,5},{5,4},{6,7},{7,6},{8,9},{9,8},{10,11... | collective-permute-start | bytes 589832 | tf_op jit(solution)/shard_map/ppermute | solution.py:174
  67.2 2.3 %collective-permute-start.6 = (bf16[96,1024]{1,0:T(8,128)(2,1)S(1)}, bf16[96,1024]{1,0:T(8,128)(2,1)S(1)}, u32[]{:S(2)}, u32[]{:S(2)}) collective-permute-start(bf16[96,1024]{1,0:T(8,128)(2,1)S(1)} %get-tuple-element.34), channel_id=1, source_target_pairs={{0,4},{1,5},{2,6},{3,7},{4,0},{5,1},{6,2},{7,3},{8,12},{9,13},{10,... | collective-permute-start | bytes 589832 | tf_op jit(solution)/shard_map/ppermute | solution.py:174
  71.9 4.2 %collective-permute-done.1.refs_2_ = bf16[96,1024]{1,0:T(8,128)(2,1)S(1)} collective-permute-done((bf16[96,1024]{1,0:T(8,128)(2,1)S(1)}, bf16[96,1024]{1,0:T(8,128)(2,1)S(1)}, u32[]{:S(2)}, u32[]{:S(2)}) %collective-permute-start.1) | collective-permute-done | bytes 196640 | tf_op jit(solution)/shard_map/ppermute | solution.py:174
  77.3 3.6 %collective-permute-done.2.refs_3_ = bf16[96,1024]{1,0:T(8,128)(2,1)S(1)} collective-permute-done((bf16[96,1024]{1,0:T(8,128)(2,1)S(1)}, bf16[96,1024]{1,0:T(8,128)(2,1)S(1)}, u32[]{:S(2)}, u32[]{:S(2)}) %collective-permute-start.2) | collective-permute-done | bytes 196640 | tf_op jit(solution)/shard_map/ppermute | solution.py:174
  80.9 2.0 %collective-permute-start.8 = (bf16[96,1024]{1,0:T(8,128)(2,1)S(1)}, bf16[96,1024]{1,0:T(8,128)(2,1)S(1)}, u32[]{:S(2)}, u32[]{:S(2)}) collective-permute-start(bf16[96,1024]{1,0:T(8,128)(2,1)S(1)} %get-tuple-element.36), channel_id=1, source_target_pairs={{0,6},{1,7},{2,4},{3,5},{4,2},{5,3},{6,0},{7,1},{8,14},{9,15},{10,... | collective-permute-start | bytes 589832 | tf_op jit(solution)/shard_map/ppermute | solution.py:174
  84.1 3.4 %copy-done.1 = bf16[1,4096,1024]{2,1,0:T(8,128)(2,1)S(1)} copy-done((bf16[1,4096,1024]{2,1,0:T(8,128)(2,1)S(1)}, bf16[1,4096,1024]{2,1,0:T(8,128)(2,1)}, u32[]{:S(2)}) %copy-start.1) | copy-done | bytes 8388632
  87.5 3.4 %copy-done.3 = bf16[1,4096,1024]{2,1,0:T(8,128)(2,1)S(1)} copy-done((bf16[1,4096,1024]{2,1,0:T(8,128)(2,1)S(1)}, bf16[1,4096,1024]{2,1,0:T(8,128)(2,1)}, u32[]{:S(2)}) %copy-start.3) | copy-done | bytes 8388632
  90.9 9.2 %shard_map.73 = (bf16[96,1024]{1,0:T(8,128)(2,1)S(1)}, bf16[96,1024]{1,0:T(8,128)(2,1)S(1)}, bf16[96,1024]{1,0:T(8,128)(2,1)S(1)}, bf16[96,1024]{1,0:T(8,128)(2,1)S(1)}) custom-call(bf16[96,1024]{1,0:T(8,128)(2,1)S(1)} %get-tuple-element.26.refs_0_, bf16[96,1024]{1,0:T(8,128)(2,1)S(1)} %collective-permute-done.refs_1_, ...), custom_call_target="tpu_custom_call" | custom-call | tf_op jit(solution)/shard_map/pallas_call | solution.py:62
  100.6 3.5 %collective-permute-start.4 = (bf16[96,1024]{1,0:T(8,128)(2,1)S(1)}, bf16[96,1024]{1,0:T(8,128)(2,1)S(1)}, u32[]{:S(2)}, u32[]{:S(2)}) collective-permute-start(bf16[96,1024]{1,0:T(8,128)(2,1)S(1)} %get-tuple-element.32), channel_id=1, source_target_pairs={{0,2},{1,3},{2,0},{3,1},{4,6},{5,7},{6,4},{7,5},{8,10},{9,11},{10,... | collective-permute-start | bytes 589832 | tf_op jit(solution)/shard_map/ppermute | solution.py:174
  104.1 4.6 %collective-permute-start.5 = (bf16[96,1024]{1,0:T(8,128)(2,1)S(1)}, bf16[96,1024]{1,0:T(8,128)(2,1)S(1)}, u32[]{:S(2)}, u32[]{:S(2)}) collective-permute-start(bf16[96,1024]{1,0:T(8,128)(2,1)S(1)} %get-tuple-element.33), channel_id=1, source_target_pairs={{0,3},{1,2},{2,1},{3,0},{4,7},{5,6},{6,5},{7,4},{8,11},{9,10},{10,... | collective-permute-start | bytes 589832 | tf_op jit(solution)/shard_map/ppermute | solution.py:174
  108.7 3.4 %copy-done.2 = bf16[1,4096,1024]{2,1,0:T(8,128)(2,1)S(1)} copy-done((bf16[1,4096,1024]{2,1,0:T(8,128)(2,1)S(1)}, bf16[1,4096,1024]{2,1,0:T(8,128)(2,1)}, u32[]{:S(2)}) %copy-start.2) | copy-done | bytes 8388632
  112.1 3.4 %copy-done.4 = bf16[1,4096,1024]{2,1,0:T(8,128)(2,1)S(1)} copy-done((bf16[1,4096,1024]{2,1,0:T(8,128)(2,1)S(1)}, bf16[1,4096,1024]{2,1,0:T(8,128)(2,1)}, u32[]{:S(2)}) %copy-start.4) | copy-done | bytes 8388632
  115.5 9.8 %shard_map.74 = (bf16[96,1024]{1,0:T(8,128)(2,1)S(1)}, bf16[96,1024]{1,0:T(8,128)(2,1)S(1)}, bf16[96,1024]{1,0:T(8,128)(2,1)}, bf16[96,1024]{1,0:T(8,128)(2,1)S(1)}) custom-call(bf16[96,1024]{1,0:T(8,128)(2,1)S(1)} %collective-permute-done.6.refs_0_, bf16[96,1024]{1,0:T(8,128)(2,1)S(1)} %collective-permute-done.7.refs_1_, ...), custom_call_target="tpu_custom_call" | custom-call | tf_op jit(solution)/shard_map/pallas_call | solution.py:62
  125.3 2.0 %constant_dynamic-update-slice_fusion.1 = bf16[2304,256]{1,0:T(8,128)(2,1)} fusion(bf16[1152,256]{1,0:T(8,128)(2,1)} %collective-permute-done.27), kind=kLoop, calls=%fused_computation.6 | loop fusion | bytes 1179648
  129.2 7.4 %collective-permute-done.10.refs_4_ = bf16[96,1024]{1,0:T(8,128)(2,1)S(1)} collective-permute-done((bf16[96,1024]{1,0:T(8,128)(2,1)S(1)}, bf16[96,1024]{1,0:T(8,128)(2,1)S(1)}, u32[]{:S(2)}, u32[]{:S(2)}) %collective-permute-start.10) | collective-permute-done | bytes 196640 | tf_op jit(solution)/shard_map/ppermute | solution.py:174
  137.3 11.2 %collective-permute-done.11.refs_5_ = bf16[96,1024]{1,0:T(8,128)(2,1)S(1)} collective-permute-done((bf16[96,1024]{1,0:T(8,128)(2,1)S(1)}, bf16[96,1024]{1,0:T(8,128)(2,1)S(1)}, u32[]{:S(2)}, u32[]{:S(2)}) %collective-permute-start.11) | collective-permute-done | bytes 196640 | tf_op jit(solution)/shard_map/ppermute | solution.py:174
  153.3 4.1 %collective-permute-done.12.refs_6_ = bf16[96,1024]{1,0:T(8,128)(2,1)} collective-permute-done((bf16[96,1024]{1,0:T(8,128)(2,1)}, bf16[96,1024]{1,0:T(8,128)(2,1)}, u32[]{:S(2)}, u32[]{:S(2)}) %collective-permute-start.12) | collective-permute-done | bytes 196640 | tf_op jit(solution)/shard_map/ppermute | solution.py:174
  157.4 2.9 %collective-permute-start.13 = (bf16[96,1024]{1,0:T(8,128)(2,1)}, bf16[96,1024]{1,0:T(8,128)(2,1)S(1)}, u32[]{:S(2)}, u32[]{:S(2)}) collective-permute-start(bf16[96,1024]{1,0:T(8,128)(2,1)} %copy-done.14), channel_id=1, source_target_pairs={{0,7},{1,6},{2,5},{3,4},{4,3},{5,2},{6,1},{7,0},{8,15},{9,14},{10,... | collective-permute-start | bytes 589832 | tf_op jit(solution)/shard_map/ppermute | solution.py:174
  161.3 5.1 %collective-permute-done.13.refs_7_ = bf16[96,1024]{1,0:T(8,128)(2,1)S(1)} collective-permute-done((bf16[96,1024]{1,0:T(8,128)(2,1)}, bf16[96,1024]{1,0:T(8,128)(2,1)S(1)}, u32[]{:S(2)}, u32[]{:S(2)}) %collective-permute-start.13) | collective-permute-done | bytes 196640 | tf_op jit(solution)/shard_map/ppermute | solution.py:174
  170.1 2.0 %combine.1 = (bf16[256,1024]{1,0:T(8,128)(2,1)S(1)}, bf16[64,1024]{1,0:T(8,128)(2,1)S(1)}, bf16[64,1024]{1,0:T(8,128)(2,1)S(1)}) custom-call(bf16[256,1024]{1,0:T(8,128)(2,1)S(1)} %bitcast.20, f32[256,2]{1,0:T(8,128)S(1)} %add_divide_fusion.gates_ref, s32[256,2]{1,0:T(8,128)S(1)} %bitcast_add_fusion.cells_ref, ...), custom_call_target="tpu_custom_call" | custom-call | tf_op jit(solution)/shard_map/combine/pallas_call | solution.py:90
  172.1 6.5 %collective-permute-start.14 = (bf16[64,1024]{1,0:T(8,128)(2,1)S(1)}, bf16[64,1024]{1,0:T(8,128)(2,1)S(1)}, u32[]{:S(2)}, u32[]{:S(2)}) collective-permute-start(bf16[64,1024]{1,0:T(8,128)(2,1)S(1)} %get-tuple-element.43), channel_id=1, source_target_pairs={{0,1},{1,2},{2,3},{3,4},{4,5},{5,6},{6,7},{8,9},{9,10},{10,11},{11... | collective-permute-start | bytes 393224 | tf_op jit(solution)/shard_map/ppermute | solution.py:224
  178.6 1.9 collective-permute-done.14.top_ref
  182.4 5.1 %collective-permute-done.15.bottom_ref = bf16[64,1024]{1,0:T(8,128)(2,1)S(1)} collective-permute-done((bf16[64,1024]{1,0:T(8,128)(2,1)S(1)}, bf16[64,1024]{1,0:T(8,128)(2,1)S(1)}, u32[]{:S(2)}, u32[]{:S(2)}) %collective-permute-start.15) | collective-permute-done | bytes 131104 | tf_op jit(solution)/shard_map/ppermute | solution.py:225
  187.5 6.3 %conv.1 = bf16[256,512]{1,0:T(8,128)(2,1)} custom-call(s32[3]{0:T(128)S(1)} %pad_add_fusion.place_ref, bf16[256,1024]{1,0:T(8,128)(2,1)S(1)} %get-tuple-element.42.mixed_ref, bf16[64,1024]{1,0:T(8,128)(2,1)S(1)} %collective-permute-done.14.top_ref, bf16[64,1024]{1,0:T(8,128)(2,1)S(1)} %collective-permute-done.15.bottom_ref, ...), custom_call_target="tpu_custom_call" | custom-call | tf_op jit(solution)/shard_map/conv/pallas_call | solution.py:161
  (87 shorter events, 33.8 us)
Async XLA Ops:
  0.0 150.9 %copy-start = (f32[1024,8]{0,1:T(8,128)S(1)}, f32[1024,8]{0,1:T(8,128)}, u32[]{:S(2)}) copy-start(f32[1024,8]{0,1:T(8,128)} %param.10) | copy-start | bytes 98308
  1.5 9.7 %collective-permute-start.16 = (bf16[1152,128]{1,0:T(8,128)(2,1)S(1)}, bf16[1152,128]{1,0:T(8,128)(2,1)S(1)}, u32[]{:S(2)}, u32[]{:S(2)}) collective-permute-start(bf16[1152,128]{1,0:T(8,128)(2,1)S(1)} %pad_maximum_fusion.refs_0_), channel_id=1, source_target_pairs={{0,2},{1,3},{2,4},{3,5},{4,6},{5,7},{8,10},{9,11},{10,12},{11,13},... | collective-permute-start | bytes 884744 | tf_op jit(solution)/shard_map/ppermute | solution.py:187
  5.6 9.8 %collective-permute-start.19 = (bf16[1152,128]{1,0:T(8,128)(2,1)S(1)}, bf16[1152,128]{1,0:T(8,128)(2,1)S(1)}, u32[]{:S(2)}, u32[]{:S(2)}) collective-permute-start(bf16[1152,128]{1,0:T(8,128)(2,1)S(1)} %pad_maximum_fusion.refs_0_), channel_id=1, source_target_pairs={{2,0},{3,1},{4,2},{5,3},{6,4},{7,5},{10,8},{11,9},{12,10},{13,11},... | collective-permute-start | bytes 884744 | tf_op jit(solution)/shard_map/ppermute | solution.py:188
  11.2 8.9 %collective-permute-start.17 = (bf16[1152,128]{1,0:T(8,128)(2,1)S(1)}, bf16[1152,128]{1,0:T(8,128)(2,1)S(1)}, u32[]{:S(2)}, u32[]{:S(2)}) collective-permute-start(bf16[1152,128]{1,0:T(8,128)(2,1)S(1)} %collective-permute-done.16.refs_1_), channel_id=1, source_target_pairs={{0,2},{1,3},{2,4},{3,5},{4,6},{5,7},{8,10},{9,11},{10,12},{11,13},... | collective-permute-start | bytes 884744 | tf_op jit(solution)/shard_map/ppermute | solution.py:187
  15.3 8.9 %collective-permute-start.20 = (bf16[1152,128]{1,0:T(8,128)(2,1)S(1)}, bf16[1152,128]{1,0:T(8,128)(2,1)S(1)}, u32[]{:S(2)}, u32[]{:S(2)}) collective-permute-start(bf16[1152,128]{1,0:T(8,128)(2,1)S(1)} %collective-permute-done.19.refs_4_), channel_id=1, source_target_pairs={{2,0},{3,1},{4,2},{5,3},{6,4},{7,5},{10,8},{11,9},{12,10},{13,11},... | collective-permute-start | bytes 884744 | tf_op jit(solution)/shard_map/ppermute | solution.py:188
  20.1 8.1 %collective-permute-start.18 = (bf16[1152,128]{1,0:T(8,128)(2,1)S(1)}, bf16[1152,128]{1,0:T(8,128)(2,1)S(1)}, u32[]{:S(2)}, u32[]{:S(2)}) collective-permute-start(bf16[1152,128]{1,0:T(8,128)(2,1)S(1)} %collective-permute-done.17.refs_2_), channel_id=1, source_target_pairs={{0,2},{1,3},{2,4},{3,5},{4,6},{5,7},{8,10},{9,11},{10,12},{11,13},... | collective-permute-start | bytes 884744 | tf_op jit(solution)/shard_map/ppermute | solution.py:187
  24.3 7.8 %collective-permute-start.21 = (bf16[1152,128]{1,0:T(8,128)(2,1)S(1)}, bf16[1152,128]{1,0:T(8,128)(2,1)S(1)}, u32[]{:S(2)}, u32[]{:S(2)}) collective-permute-start(bf16[1152,128]{1,0:T(8,128)(2,1)S(1)} %collective-permute-done.20.refs_5_), channel_id=1, source_target_pairs={{2,0},{3,1},{4,2},{5,3},{6,4},{7,5},{10,8},{11,9},{12,10},{13,11},... | collective-permute-start | bytes 884744 | tf_op jit(solution)/shard_map/ppermute | solution.py:188
  33.4 26.4 %copy-start.5 = (bf16[1,4,64,1024]{3,2,1,0:T(8,128)(2,1)S(1)}, bf16[1,4,64,1024]{3,2,1,0:T(8,128)(2,1)}, u32[]{:S(2)}) copy-start(bf16[1,4,64,1024]{3,2,1,0:T(8,128)(2,1)} %param.7) | copy-start | bytes 1572868
  33.4 24.2 %collective-permute-start.25 = (bf16[2304,256]{1,0:T(8,128)(2,1)S(1)}, bf16[2304,256]{1,0:T(8,128)(2,1)S(1)}, u32[]{:S(2)}, u32[]{:S(2)}) collective-permute-start(bf16[2304,256]{1,0:T(8,128)(2,1)S(1)} %assemble.1.refs_0_), channel_id=1, source_target_pairs={{0,16},{8,24},{16,0},{24,8},{1,17},{9,25},{17,1},{25,9},{2,18},{10... | collective-permute-start | bytes 3538952 | tf_op jit(solution)/shard_map/ppermute | solution.py:174
  34.7 32.5 %collective-permute-start.23 = (bf16[2304,256]{1,0:T(8,128)(2,1)S(1)}, bf16[2304,256]{1,0:T(8,128)(2,1)}, u32[]{:S(2)}, u32[]{:S(2)}) collective-permute-start(bf16[2304,256]{1,0:T(8,128)(2,1)S(1)} %assemble.1.refs_0_), channel_id=1, source_target_pairs={{0,8},{8,0},{16,24},{24,16},{1,9},{9,1},{17,25},{25,17},{2,10},{10... | collective-permute-start | bytes 3538952 | tf_op jit(solution)/shard_map/ppermute | solution.py:174
  58.4 66.9 %collective-permute-start.27 = (bf16[1152,256]{1,0:T(8,128)(2,1)}, bf16[1152,256]{1,0:T(8,128)(2,1)}, u32[]{:S(2)}, u32[]{:S(2)}) collective-permute-start(bf16[1152,256]{1,0:T(8,128)(2,1)} %slice.18), channel_id=1, source_target_pairs={{0,8},{8,0},{16,24},{24,16},{1,9},{9,1},{17,25},{25,17},{2,10},{10... | collective-permute-start | bytes 1769480 | tf_op jit(solution)/shard_map/ppermute | solution.py:174
  60.9 9.7 %collective-permute-start = (bf16[96,1024]{1,0:T(8,128)(2,1)S(1)}, bf16[96,1024]{1,0:T(8,128)(2,1)S(1)}, u32[]{:S(2)}, u32[]{:S(2)}) collective-permute-start(bf16[96,1024]{1,0:T(8,128)(2,1)S(1)} %get-tuple-element.27), channel_id=1, source_target_pairs={{0,1},{1,0},{2,3},{3,2},{4,5},{5,4},{6,7},{7,6},{8,9},{9,8},{10,11... | collective-permute-start | bytes 589832 | tf_op jit(solution)/shard_map/ppermute | solution.py:174
  65.5 10.6 %collective-permute-start.1 = (bf16[96,1024]{1,0:T(8,128)(2,1)S(1)}, bf16[96,1024]{1,0:T(8,128)(2,1)S(1)}, u32[]{:S(2)}, u32[]{:S(2)}) collective-permute-start(bf16[96,1024]{1,0:T(8,128)(2,1)S(1)} %get-tuple-element.28), channel_id=1, source_target_pairs={{0,2},{1,3},{2,0},{3,1},{4,6},{5,7},{6,4},{7,5},{8,10},{9,11},{10,... | collective-permute-start | bytes 589832 | tf_op jit(solution)/shard_map/ppermute | solution.py:174
  66.8 14.1 %collective-permute-start.2 = (bf16[96,1024]{1,0:T(8,128)(2,1)S(1)}, bf16[96,1024]{1,0:T(8,128)(2,1)S(1)}, u32[]{:S(2)}, u32[]{:S(2)}) collective-permute-start(bf16[96,1024]{1,0:T(8,128)(2,1)S(1)} %get-tuple-element.29), channel_id=1, source_target_pairs={{0,3},{1,2},{2,1},{3,0},{4,7},{5,6},{6,5},{7,4},{8,11},{9,10},{10,... | collective-permute-start | bytes 589832 | tf_op jit(solution)/shard_map/ppermute | solution.py:174
  67.2 15.7 %collective-permute-start.6 = (bf16[96,1024]{1,0:T(8,128)(2,1)S(1)}, bf16[96,1024]{1,0:T(8,128)(2,1)S(1)}, u32[]{:S(2)}, u32[]{:S(2)}) collective-permute-start(bf16[96,1024]{1,0:T(8,128)(2,1)S(1)} %get-tuple-element.34), channel_id=1, source_target_pairs={{0,4},{1,5},{2,6},{3,7},{4,0},{5,1},{6,2},{7,3},{8,12},{9,13},{10,... | collective-permute-start | bytes 589832 | tf_op jit(solution)/shard_map/ppermute | solution.py:174
  70.6 56.7 %collective-permute-start.28 = (bf16[1152,256]{1,0:T(8,128)(2,1)S(1)}, bf16[1152,256]{1,0:T(8,128)(2,1)S(1)}, u32[]{:S(2)}, u32[]{:S(2)}) collective-permute-start(bf16[1152,256]{1,0:T(8,128)(2,1)S(1)} %slice.19), channel_id=1, source_target_pairs={{0,16},{8,24},{16,0},{24,8},{1,17},{9,25},{17,1},{25,9},{2,18},{10... | collective-permute-start | bytes 1769480 | tf_op jit(solution)/shard_map/ppermute | solution.py:174
  76.1 24.0 %collective-permute-start.7 = (bf16[96,1024]{1,0:T(8,128)(2,1)S(1)}, bf16[96,1024]{1,0:T(8,128)(2,1)S(1)}, u32[]{:S(2)}, u32[]{:S(2)}) collective-permute-start(bf16[96,1024]{1,0:T(8,128)(2,1)S(1)} %get-tuple-element.35), channel_id=1, source_target_pairs={{0,5},{1,4},{2,7},{3,6},{4,1},{5,0},{6,3},{7,2},{8,13},{9,12},{10,... | collective-permute-start | bytes 589832 | tf_op jit(solution)/shard_map/ppermute | solution.py:174
  80.9 19.7 %collective-permute-start.8 = (bf16[96,1024]{1,0:T(8,128)(2,1)S(1)}, bf16[96,1024]{1,0:T(8,128)(2,1)S(1)}, u32[]{:S(2)}, u32[]{:S(2)}) collective-permute-start(bf16[96,1024]{1,0:T(8,128)(2,1)S(1)} %get-tuple-element.36), channel_id=1, source_target_pairs={{0,6},{1,7},{2,4},{3,5},{4,2},{5,3},{6,0},{7,1},{8,14},{9,15},{10,... | collective-permute-start | bytes 589832 | tf_op jit(solution)/shard_map/ppermute | solution.py:174
  82.9 21.2 %collective-permute-start.9 = (bf16[96,1024]{1,0:T(8,128)(2,1)S(1)}, bf16[96,1024]{1,0:T(8,128)(2,1)S(1)}, u32[]{:S(2)}, u32[]{:S(2)}) collective-permute-start(bf16[96,1024]{1,0:T(8,128)(2,1)S(1)} %get-tuple-element.37), channel_id=1, source_target_pairs={{0,7},{1,6},{2,5},{3,4},{4,3},{5,2},{6,1},{7,0},{8,15},{9,14},{10,... | collective-permute-start | bytes 589832 | tf_op jit(solution)/shard_map/ppermute | solution.py:174
  100.1 28.3 %collective-permute-start.3 = (bf16[96,1024]{1,0:T(8,128)(2,1)S(1)}, bf16[96,1024]{1,0:T(8,128)(2,1)S(1)}, u32[]{:S(2)}, u32[]{:S(2)}) collective-permute-start(bf16[96,1024]{1,0:T(8,128)(2,1)S(1)} %get-tuple-element.31), channel_id=1, source_target_pairs={{0,1},{1,0},{2,3},{3,2},{4,5},{5,4},{6,7},{7,6},{8,9},{9,8},{10,11... | collective-permute-start | bytes 589832 | tf_op jit(solution)/shard_map/ppermute | solution.py:174
  100.6 28.1 %collective-permute-start.4 = (bf16[96,1024]{1,0:T(8,128)(2,1)S(1)}, bf16[96,1024]{1,0:T(8,128)(2,1)S(1)}, u32[]{:S(2)}, u32[]{:S(2)}) collective-permute-start(bf16[96,1024]{1,0:T(8,128)(2,1)S(1)} %get-tuple-element.32), channel_id=1, source_target_pairs={{0,2},{1,3},{2,0},{3,1},{4,6},{5,7},{6,4},{7,5},{8,10},{9,11},{10,... | collective-permute-start | bytes 589832 | tf_op jit(solution)/shard_map/ppermute | solution.py:174
  104.1 24.8 %collective-permute-start.5 = (bf16[96,1024]{1,0:T(8,128)(2,1)S(1)}, bf16[96,1024]{1,0:T(8,128)(2,1)S(1)}, u32[]{:S(2)}, u32[]{:S(2)}) collective-permute-start(bf16[96,1024]{1,0:T(8,128)(2,1)S(1)} %get-tuple-element.33), channel_id=1, source_target_pairs={{0,3},{1,2},{2,1},{3,0},{4,7},{5,6},{6,5},{7,4},{8,11},{9,10},{10,... | collective-permute-start | bytes 589832 | tf_op jit(solution)/shard_map/ppermute | solution.py:174
  125.3 11.4 %collective-permute-start.10 = (bf16[96,1024]{1,0:T(8,128)(2,1)S(1)}, bf16[96,1024]{1,0:T(8,128)(2,1)S(1)}, u32[]{:S(2)}, u32[]{:S(2)}) collective-permute-start(bf16[96,1024]{1,0:T(8,128)(2,1)S(1)} %get-tuple-element.38), channel_id=1, source_target_pairs={{0,4},{1,5},{2,6},{3,7},{4,0},{5,1},{6,2},{7,3},{8,12},{9,13},{10,... | collective-permute-start | bytes 589832 | tf_op jit(solution)/shard_map/ppermute | solution.py:174
  127.3 60.2 %collective-permute-start.22 = (bf16[2304,256]{1,0:T(8,128)(2,1)S(1)}, bf16[2304,256]{1,0:T(8,128)(2,1)}, u32[]{:S(2)}, u32[]{:S(2)}) collective-permute-start(bf16[2304,256]{1,0:T(8,128)(2,1)S(1)} %assemble.1.refs_0_), channel_id=1, source_target_pairs={{0,1},{1,0},{2,3},{3,2},{4,5},{5,4},{6,7},{7,6},{8,9},{9,8},{10,11... | collective-permute-start | bytes 3538952 | tf_op jit(solution)/shard_map/ppermute | solution.py:174
  128.4 59.1 %collective-permute-start.24 = (bf16[2304,256]{1,0:T(8,128)(2,1)}, bf16[2304,256]{1,0:T(8,128)(2,1)}, u32[]{:S(2)}, u32[]{:S(2)}) collective-permute-start(bf16[2304,256]{1,0:T(8,128)(2,1)} %collective-permute-done.23.refs_2_), channel_id=1, source_target_pairs={{0,1},{1,0},{2,3},{3,2},{4,5},{5,4},{6,7},{7,6},{8,9},{9,8},{10,11... | collective-permute-start | bytes 3538952 | tf_op jit(solution)/shard_map/ppermute | solution.py:174
  128.7 58.8 %collective-permute-start.26 = (bf16[2304,256]{1,0:T(8,128)(2,1)S(1)}, bf16[2304,256]{1,0:T(8,128)(2,1)}, u32[]{:S(2)}, u32[]{:S(2)}) collective-permute-start(bf16[2304,256]{1,0:T(8,128)(2,1)S(1)} %collective-permute-done.25.refs_4_), channel_id=1, source_target_pairs={{0,1},{1,0},{2,3},{3,2},{4,5},{5,4},{6,7},{7,6},{8,9},{9,8},{10,11... | collective-permute-start | bytes 3538952 | tf_op jit(solution)/shard_map/ppermute | solution.py:174
  128.9 58.6 %collective-permute-start.29 = (bf16[2304,256]{1,0:T(8,128)(2,1)}, bf16[2304,256]{1,0:T(8,128)(2,1)}, u32[]{:S(2)}, u32[]{:S(2)}) collective-permute-start(bf16[2304,256]{1,0:T(8,128)(2,1)} %constant_dynamic-update-slice_fusion.refs_6_), channel_id=1, source_target_pairs={{0,1},{1,0},{2,3},{3,2},{4,5},{5,4},{6,7},{7,6},{8,9},{9,8},{10,11... | collective-permute-start | bytes 3538952 | tf_op jit(solution)/shard_map/ppermute | solution.py:174
  137.3 11.2 %collective-permute-start.11 = (bf16[96,1024]{1,0:T(8,128)(2,1)S(1)}, bf16[96,1024]{1,0:T(8,128)(2,1)S(1)}, u32[]{:S(2)}, u32[]{:S(2)}) collective-permute-start(bf16[96,1024]{1,0:T(8,128)(2,1)S(1)} %get-tuple-element.39), channel_id=1, source_target_pairs={{0,5},{1,4},{2,7},{3,6},{4,1},{5,0},{6,3},{7,2},{8,13},{9,12},{10,... | collective-permute-start | bytes 589832 | tf_op jit(solution)/shard_map/ppermute | solution.py:174
  149.2 8.2 %collective-permute-start.12 = (bf16[96,1024]{1,0:T(8,128)(2,1)}, bf16[96,1024]{1,0:T(8,128)(2,1)}, u32[]{:S(2)}, u32[]{:S(2)}) collective-permute-start(bf16[96,1024]{1,0:T(8,128)(2,1)} %get-tuple-element.40), channel_id=1, source_target_pairs={{0,6},{1,7},{2,4},{3,5},{4,2},{5,3},{6,0},{7,1},{8,14},{9,15},{10,... | collective-permute-start | bytes 589832 | tf_op jit(solution)/shard_map/ppermute | solution.py:174
  157.4 8.9 %collective-permute-start.13 = (bf16[96,1024]{1,0:T(8,128)(2,1)}, bf16[96,1024]{1,0:T(8,128)(2,1)S(1)}, u32[]{:S(2)}, u32[]{:S(2)}) collective-permute-start(bf16[96,1024]{1,0:T(8,128)(2,1)} %copy-done.14), channel_id=1, source_target_pairs={{0,7},{1,6},{2,5},{3,4},{4,3},{5,2},{6,1},{7,0},{8,15},{9,14},{10,... | collective-permute-start | bytes 589832 | tf_op jit(solution)/shard_map/ppermute | solution.py:174
  172.1 8.4 %collective-permute-start.14 = (bf16[64,1024]{1,0:T(8,128)(2,1)S(1)}, bf16[64,1024]{1,0:T(8,128)(2,1)S(1)}, u32[]{:S(2)}, u32[]{:S(2)}) collective-permute-start(bf16[64,1024]{1,0:T(8,128)(2,1)S(1)} %get-tuple-element.43), channel_id=1, source_target_pairs={{0,1},{1,2},{2,3},{3,4},{4,5},{5,6},{6,7},{8,9},{9,10},{10,11},{11... | collective-permute-start | bytes 393224 | tf_op jit(solution)/shard_map/ppermute | solution.py:224
  180.5 7.0 %collective-permute-start.15 = (bf16[64,1024]{1,0:T(8,128)(2,1)S(1)}, bf16[64,1024]{1,0:T(8,128)(2,1)S(1)}, u32[]{:S(2)}, u32[]{:S(2)}) collective-permute-start(bf16[64,1024]{1,0:T(8,128)(2,1)S(1)} %get-tuple-element.44), channel_id=1, source_target_pairs={{1,0},{2,1},{3,2},{4,3},{5,4},{6,5},{7,6},{9,8},{10,9},{11,10},{12... | collective-permute-start | bytes 393224 | tf_op jit(solution)/shard_map/ppermute | solution.py:225
  (16 other events, 111.1 us)
where the time goes:
time: 195 us; the launch traced here: 194 us
  waiting for transfers between devices  78.3 us (40%)
  starting transfers between devices  56.8 us (29%)
  Pallas kernels  29.8 us (15%)
  local copies, waits for them, and re-layouts  26.9 us (14%)
    ppermute x22, waiting for transfers between devices, flip(): lax.ppermute(value, axis, [(i, i ^ k) for i in range(lax.axis_size(axis))])  57.1 us
    ppermute x22, starting transfers between devices, flip(): lax.ppermute(value, axis, [(i, i ^ k) for i in range(lax.axis_size(axis))])  32.3 us
    unnamed x40, local copies, waits for them, and re-layouts  22.2 us
    pallas_call x2, Pallas kernels, mlp(): pl.pallas_call(kernel, in_specs=[VM] * (n + 2), out_specs=[VM] * n, out_s...  19.1 us
    ppermute x3, starting transfers between devices, gather_filters(): up = lax.ppermute(up, 'expert', [(i, i + 2) for i in range(size - 2)])  12.3 us
    ppermute x3, waiting for transfers between devices, gather_filters(): up = lax.ppermute(up, 'expert', [(i, i + 2) for i in range(size - 2)])  10.4 us
    ppermute x1, starting transfers between devices, shards(): top = lax.ppermute(high, 'expert', [(i, i + 1) for i in range(experts - 1)])  6.49 us
    pallas_call x1, Pallas kernels, conv(): pl.pallas_call(kernel, out_shape=jax.ShapeDtypeStruct((count, 2 * cols),...  6.33 us
  transfers between devices with their start and end apart: 30, of which 13 were waited for; matrix products, arithmetic and copies ran while one was open for 4% of the time, Pallas kernels for 11%

commit v1 on v0

--- a/solution.py
+++ b/solution.py
@@ -38,32 +38,53 @@
     return res[0], res[1:]
 
 
-def mlp(blocks, w_in, w_out, step=512):
+def mlp(blocks, w_in, w_out, stream=False, step=1024):
     n, (cap, width) = len(blocks), blocks[0].shape
     steps = w_in.shape[0] // step
 
     def kernel(*refs):
-        xs, (wi, wo), outs, (x_scr, acc) = refs[:n], refs[n : n + 2], refs[n + 2 : 2 * n + 2], refs[2 * n + 2 :]
+        xs, weights, outs = refs[:n], refs[n : n + 2], refs[n + 2 : 2 * n + 2]
+        x_scr, acc = refs[2 * n + 2 : 2 * n + 4]
+        copies = []
+        if stream:
+            held, sems = refs[2 * n + 4 : 2 * n + 6], refs[2 * n + 6]
+            for i in range(steps):
+                rows = slice(i * step, (i + 1) * step)
+                copies.append([
+                    pltpu.make_async_copy(w.at[rows], h.at[rows], sems.at[j, i])
+                    for j, (w, h) in enumerate(zip(weights, held))
+                ])
+            for pair in copies:
+                for c in pair:
+                    c.start()
+            weights = held
         for k in range(n):
             x_scr[k * cap : (k + 1) * cap, :] = xs[k][...]
-        acc[...] = jnp.zeros_like(acc)
-
-        def body(i, carry):
-            rows = pl.ds(pl.multiple_of(i * step, step), step)
-            h = lax.dot_general(x_scr[...], wi[rows, :], (((1,), (1,)), ((), ())), preferred_element_type=F32)
+        for i in range(steps):
+            rows = slice(i * step, (i + 1) * step)
+            if stream:
+                copies[i][0].wait()
+            h = lax.dot_general(
+                x_scr[...], weights[0][rows, :], (((1,), (1,)), ((), ())), preferred_element_type=F32
+            )
             act = (0.5 * h * (1.0 + lax.erf(h * 0.7071067811865476))).astype(BF16)
-            acc[...] += jnp.dot(act, wo[rows, :], preferred_element_type=F32)
-            return carry
-
-        lax.fori_loop(0, steps, body, 0)
+            if stream:
+                copies[i][1].wait()
+            part = jnp.dot(act, weights[1][rows, :], preferred_element_type=F32)
+            if i == 0:
+                acc[...] = part
+            else:
+                acc[...] += part
         for k in range(n):
             outs[k][...] = acc[k * cap : (k + 1) * cap, :].astype(BF16)
 
-    return pl.pallas_call(
-        kernel, in_specs=[VM] * (n + 2), out_specs=[VM] * n,
-        out_shape=[jax.ShapeDtypeStruct((cap, width), BF16)] * n,
-        scratch_shapes=[pltpu.VMEM((n * cap, width), BF16), pltpu.VMEM((n * cap, width), F32)],
-        compiler_params=pltpu.CompilerParams(vmem_limit_bytes=16 * 2**20),
+    scratch = [pltpu.VMEM((n * cap, width), BF16), pltpu.VMEM((n * cap, width), F32)]
+    if stream:
+        scratch += [pltpu.VMEM(w_in.shape, BF16), pltpu.VMEM(w_out.shape, BF16), pltpu.SemaphoreType.DMA((2, steps))]
+    return pl.pallas_call(
+        kernel, in_specs=[VM] * n + [ANY if stream else VM] * 2, out_specs=[VM] * n,
+        out_shape=[jax.ShapeDtypeStruct((cap, width), BF16)] * n, scratch_shapes=scratch,
+        compiler_params=pltpu.CompilerParams(vmem_limit_bytes=(32 if stream else 14) * 2**20),
     )(*blocks, w_in, w_out)
 
 
@@ -94,27 +115,23 @@
     )(tok, gates, cells, *results)
 
 
-def assemble(place, own, ups, downs, lanes):
-    rows, packed = own.shape
-    fold, n = packed // lanes, len(ups) + 1
+def assemble(place, pieces, lanes):
+    rows, packed = pieces[0].shape
+    fold, n = packed // lanes, len(pieces)
 
     def kernel(place_ref, *refs):
         z, out = place_ref[0], refs[-1]
-        share = [refs[0][...]] + [r[...] for r in refs[1:-1]]
         for p in range(n):
-            piece = share[0]
-            for k in range(1, n):
-                if p >= k:
-                    piece = jnp.where(z == p - k, share[n - 1 + k], piece)
-                if p + k < n:
-                    piece = jnp.where(z == p + k, share[k], piece)
+            piece = refs[0][...]
+            for j in range(1, n):
+                piece = jnp.where(z == p ^ j, refs[j][...], piece)
             for f in range(fold):
                 out[f * rows : (f + 1) * rows, p * lanes : (p + 1) * lanes] = piece[:, f * lanes : (f + 1) * lanes]
 
     return pl.pallas_call(
         kernel, out_shape=jax.ShapeDtypeStruct((rows * fold, lanes * n), BF16),
-        in_specs=[SM] + [VM] * (2 * n - 1), out_specs=VM, compiler_params=PARAMS, name="assemble",
-    )(place, own, *ups, *downs)
+        in_specs=[SM] + [VM] * n, out_specs=VM, compiler_params=PARAMS, name="assemble",
+    )(place, *pieces)
 
 
 def conv(place, mixed, top, bottom, mine, theirs, lanes):
@@ -181,14 +198,10 @@
     rows = 9 * chans // fold
     flat = conv_weight.reshape(9 * chans, lanes)
     own = jnp.concatenate([flat[f * rows : (f + 1) * rows] for f in range(fold)], axis=1)
-    up, down = own, own
-    ups, downs = [], []
-    for _ in range(1, size // 2):
-        up = lax.ppermute(up, "expert", [(i, i + 2) for i in range(size - 2)])
-        down = lax.ppermute(down, "expert", [(i + 2, i) for i in range(size - 2)])
-        ups.append(up)
-        downs.append(down)
-    column = assemble(place, own, ups, downs, lanes)
+    pieces = [own]
+    for k in range(1, size // 2):
+        pieces.append(flip(pieces[k & (k - 1)], "expert", 2 * (k & -k)))
+    column = assemble(place, pieces, lanes)
     if groups == 4:
         x, y = flip(column, "dp", 1), flip(column, "dp", 2)
         half = column.shape[0] // 2
@@ -213,9 +226,10 @@
     normed, blocks = prologue(tok, cells.T, experts, cap)
     received = [blocks[0]] + [flip(blocks[k], "expert", k) for k in range(1, experts)]
     mine, theirs = gather_filters(conv_weight, place)
-    half = experts // 2
-    produced = list(mlp(received[:half], expert_in[0], expert_out[0]))
-    produced += list(mlp(received[half:], expert_in[0], expert_out[0]))
+    half, mid = experts // 2, 3 * experts // 4
+    produced = []
+    for part in (slice(0, half), slice(half, mid), slice(mid, experts)):
+        produced += list(mlp(received[part], expert_in[0], expert_out[0]))
     returned = [produced[0]] + [flip(produced[k], "expert", k) for k in range(1, experts)]
     logits = jnp.dot(normed.astype(F32), router, precision=lax.Precision.HIGHEST)
     matches = routes[:, :, None] == lax.broadcasted_iota(jnp.int32, (1, 1, experts), 2)

time: 195 us -> 177 us (0.908)
  starting transfers between devices: 56.8 us -> 47.5 us
  waiting for transfers between devices: 78.3 us -> 72.5 us
  Pallas kernels: 29.8 us -> 27.5 us
    ppermute x6 -> x0, starting transfers between devices: 16.1 us -> none  [the longest x3 12.3 us: gather_filters(): up = lax.ppermute(up, 'expert', [(i, i + 2) for i in range(size - 2)])]
    ppermute x6 -> x0, waiting for transfers between devices: 14.2 us -> none  [the longest x3 10.4 us: gather_filters(): up = lax.ppermute(up, 'expert', [(i, i + 2) for i in range(size - 2)])]
    ppermute x22 -> x25, waiting for transfers between devices: 57.1 us -> 65.5 us  [flip(): lax.ppermute(value, axis, [(i, i ^ k) for i in range(lax.axis_size(axis))])]
    ppermute x22 -> x25, starting transfers between devices: 32.3 us -> 39.1 us  [flip(): lax.ppermute(value, axis, [(i, i ^ k) for i in range(lax.axis_size(axis))])]
    pallas_call x2 -> x3, Pallas kernels: 19.1 us -> 16.8 us  [mlp(): pl.pallas_call(kernel, in_specs=[VM] * n + [ANY if stream else VM] * 2, o...]
  transfers between devices with their start and end apart: 30 -> 27, of which waited for: 13 -> 12; matrix products, arithmetic and copies ran while one was open for 4% -> 5% of each run, Pallas kernels for 11% -> 11%
where the time goes in v1:
time: 177 us; the launch traced here: 176 us
  waiting for transfers between devices  72.5 us (41%)
  starting transfers between devices  47.5 us (27%)
  Pallas kernels  27.5 us (16%)
  local copies, waits for them, and re-layouts  26.8 us (15%)
    ppermute x25, waiting for transfers between devices, flip(): lax.ppermute(value, axis, [(i, i ^ k) for i in range(lax.axis_size(axis))])  65.5 us
    ppermute x25, starting transfers between devices, flip(): lax.ppermute(value, axis, [(i, i ^ k) for i in range(lax.axis_size(axis))])  39.1 us
    unnamed x40, local copies, waits for them, and re-layouts  22.1 us
    pallas_call x3, Pallas kernels, mlp(): pl.pallas_call(kernel, in_specs=[VM] * n + [ANY if stream else VM] * 2, o...  16.8 us
    ppermute x1, starting transfers between devices, shards(): top = lax.ppermute(high, 'expert', [(i, i + 1) for i in range(experts - 1)])  6.49 us
    pallas_call x1, Pallas kernels, conv(): pl.pallas_call(kernel, out_shape=jax.ShapeDtypeStruct((count, 2 * cols),...  6.33 us
    ppermute x1, waiting for transfers between devices, shards(): lax.ppermute(low, 'expert', [(i + 1, i) for i in range(experts - 1)])  5.07 us
  transfers between devices with their start and end apart: 27, of which 12 were waited for; matrix products, arithmetic and copies ran while one was open for 5% of the time, Pallas kernels for 11%

profile of v1, /device:TPU:1, one launch (start us, length us, event | category | flops | bytes accessed | tf_op | source)
XLA Modules:
  0.0 176.5 jit_solution(13953204958196665446)
XLA Ops:
  1.5 3.2 %collective-permute-start.17 = (bf16[1152,128]{1,0:T(8,128)(2,1)S(1)}, bf16[1152,128]{1,0:T(8,128)(2,1)S(1)}, u32[]{:S(2)}, u32[]{:S(2)}) collective-permute-start(bf16[1152,128]{1,0:T(8,128)(2,1)S(1)} %pad_maximum_fusion.refs_0_), channel_id=1, source_target_pairs={{0,4},{1,5},{2,6},{3,7},{4,0},{5,1},{6,2},{7,3},{8,12},{9,13},{10,... | collective-permute-start | bytes 884744 | tf_op jit(solution)/shard_map/ppermute | solution.py:191
  6.0 11.8 %collective-permute-done.17.refs_2_ = bf16[1152,128]{1,0:T(8,128)(2,1)S(1)} collective-permute-done((bf16[1152,128]{1,0:T(8,128)(2,1)S(1)}, bf16[1152,128]{1,0:T(8,128)(2,1)S(1)}, u32[]{:S(2)}, u32[]{:S(2)}) %collective-permute-start.17) | collective-permute-done | bytes 294944 | tf_op jit(solution)/shard_map/ppermute | solution.py:191
  19.0 6.0 %collective-permute-done.18.refs_3_ = bf16[1152,128]{1,0:T(8,128)(2,1)S(1)} collective-permute-done((bf16[1152,128]{1,0:T(8,128)(2,1)S(1)}, bf16[1152,128]{1,0:T(8,128)(2,1)S(1)}, u32[]{:S(2)}, u32[]{:S(2)}) %collective-permute-start.18) | collective-permute-done | bytes 294944 | tf_op jit(solution)/shard_map/ppermute | solution.py:191
  28.9 23.0 %collective-permute-done.22.refs_4_ = bf16[2304,256]{1,0:T(8,128)(2,1)S(1)} collective-permute-done((bf16[2304,256]{1,0:T(8,128)(2,1)S(1)}, bf16[2304,256]{1,0:T(8,128)(2,1)S(1)}, u32[]{:S(2)}, u32[]{:S(2)}) %collective-permute-start.22) | collective-permute-done | bytes 1179680 | tf_op jit(solution)/shard_map/ppermute | solution.py:191
  55.0 3.3 %collective-permute-start = (bf16[96,1024]{1,0:T(8,128)(2,1)S(1)}, bf16[96,1024]{1,0:T(8,128)(2,1)S(1)}, u32[]{:S(2)}, u32[]{:S(2)}) collective-permute-start(bf16[96,1024]{1,0:T(8,128)(2,1)S(1)} %get-tuple-element.27), channel_id=1, source_target_pairs={{0,1},{1,0},{2,3},{3,2},{4,5},{5,4},{6,7},{7,6},{8,9},{9,8},{10,11... | collective-permute-start | bytes 589832 | tf_op jit(solution)/shard_map/ppermute | solution.py:191
  58.2 2.2 %collective-permute-start.1 = (bf16[96,1024]{1,0:T(8,128)(2,1)S(1)}, bf16[96,1024]{1,0:T(8,128)(2,1)S(1)}, u32[]{:S(2)}, u32[]{:S(2)}) collective-permute-start(bf16[96,1024]{1,0:T(8,128)(2,1)S(1)} %get-tuple-element.28), channel_id=1, source_target_pairs={{0,2},{1,3},{2,0},{3,1},{4,6},{5,7},{6,4},{7,5},{8,10},{9,11},{10,... | collective-permute-start | bytes 589832 | tf_op jit(solution)/shard_map/ppermute | solution.py:191
  63.1 3.6 %collective-permute-start.6 = (bf16[96,1024]{1,0:T(8,128)(2,1)S(1)}, bf16[96,1024]{1,0:T(8,128)(2,1)S(1)}, u32[]{:S(2)}, u32[]{:S(2)}) collective-permute-start(bf16[96,1024]{1,0:T(8,128)(2,1)S(1)} %get-tuple-element.34), channel_id=1, source_target_pairs={{0,4},{1,5},{2,6},{3,7},{4,0},{5,1},{6,2},{7,3},{8,12},{9,13},{10,... | collective-permute-start | bytes 589832 | tf_op jit(solution)/shard_map/ppermute | solution.py:191
  66.8 2.9 %collective-permute-start.7 = (bf16[96,1024]{1,0:T(8,128)(2,1)S(1)}, bf16[96,1024]{1,0:T(8,128)(2,1)S(1)}, u32[]{:S(2)}, u32[]{:S(2)}) collective-permute-start(bf16[96,1024]{1,0:T(8,128)(2,1)S(1)} %get-tuple-element.35), channel_id=1, source_target_pairs={{0,5},{1,4},{2,7},{3,6},{4,1},{5,0},{6,3},{7,2},{8,13},{9,12},{10,... | collective-permute-start | bytes 589832 | tf_op jit(solution)/shard_map/ppermute | solution.py:191
  69.7 5.9 %collective-permute-done.2.refs_3_ = bf16[96,1024]{1,0:T(8,128)(2,1)S(1)} collective-permute-done((bf16[96,1024]{1,0:T(8,128)(2,1)S(1)}, bf16[96,1024]{1,0:T(8,128)(2,1)S(1)}, u32[]{:S(2)}, u32[]{:S(2)}) %collective-permute-start.2) | collective-permute-done | bytes 196640 | tf_op jit(solution)/shard_map/ppermute | solution.py:191
  76.6 3.4 %copy-done.1 = bf16[1,4096,1024]{2,1,0:T(8,128)(2,1)S(1)} copy-done((bf16[1,4096,1024]{2,1,0:T(8,128)(2,1)S(1)}, bf16[1,4096,1024]{2,1,0:T(8,128)(2,1)}, u32[]{:S(2)}) %copy-start.1) | copy-done | bytes 8388632
  79.9 3.4 %copy-done.3 = bf16[1,4096,1024]{2,1,0:T(8,128)(2,1)S(1)} copy-done((bf16[1,4096,1024]{2,1,0:T(8,128)(2,1)S(1)}, bf16[1,4096,1024]{2,1,0:T(8,128)(2,1)}, u32[]{:S(2)}) %copy-start.3) | copy-done | bytes 8388632
  83.3 6.8 %shard_map.73 = (bf16[96,1024]{1,0:T(8,128)(2,1)S(1)}, bf16[96,1024]{1,0:T(8,128)(2,1)S(1)}, bf16[96,1024]{1,0:T(8,128)(2,1)S(1)}, bf16[96,1024]{1,0:T(8,128)(2,1)S(1)}) custom-call(bf16[96,1024]{1,0:T(8,128)(2,1)S(1)} %get-tuple-element.26.refs_0_, bf16[96,1024]{1,0:T(8,128)(2,1)S(1)} %collective-permute-done.refs_1_, ...), custom_call_target="tpu_custom_call" | custom-call | tf_op jit(solution)/shard_map/pallas_call | solution.py:84
  90.1 2.8 %collective-permute-start.11 = (bf16[96,1024]{1,0:T(8,128)(2,1)S(1)}, bf16[96,1024]{1,0:T(8,128)(2,1)S(1)}, u32[]{:S(2)}, u32[]{:S(2)}) collective-permute-start(bf16[96,1024]{1,0:T(8,128)(2,1)S(1)} %get-tuple-element.39), channel_id=1, source_target_pairs={{0,7},{1,6},{2,5},{3,4},{4,3},{5,2},{6,1},{7,0},{8,15},{9,14},{10,... | collective-permute-start | bytes 589832 | tf_op jit(solution)/shard_map/ppermute | solution.py:191
  93.0 3.4 %copy-done.2 = bf16[1,4096,1024]{2,1,0:T(8,128)(2,1)S(1)} copy-done((bf16[1,4096,1024]{2,1,0:T(8,128)(2,1)S(1)}, bf16[1,4096,1024]{2,1,0:T(8,128)(2,1)}, u32[]{:S(2)}) %copy-start.2) | copy-done | bytes 8388632
  96.3 3.4 %copy-done.4 = bf16[1,4096,1024]{2,1,0:T(8,128)(2,1)S(1)} copy-done((bf16[1,4096,1024]{2,1,0:T(8,128)(2,1)S(1)}, bf16[1,4096,1024]{2,1,0:T(8,128)(2,1)}, u32[]{:S(2)}) %copy-start.4) | copy-done | bytes 8388632
  99.7 4.8 %shard_map.74 = (bf16[96,1024]{1,0:T(8,128)(2,1)S(1)}, bf16[96,1024]{1,0:T(8,128)(2,1)S(1)}) custom-call(bf16[96,1024]{1,0:T(8,128)(2,1)S(1)} %collective-permute-done.6.refs_0_, bf16[96,1024]{1,0:T(8,128)(2,1)S(1)} %collective-permute-done.7.refs_1_, bf16[4096,1024]{1,0:T(8,128)(2,1)S(1)} %bitcast.16, bf16[4096,1024]{1,0:T(8,128)(2,1)S(1)} %bitcast.19), custom_call_target="tpu_custom_call" | custom-call | tf_op jit(solution)/shard_map/pallas_call | solution.py:84
  104.6 1.9 %constant_dynamic-update-slice_fusion.1 = bf16[2304,256]{1,0:T(8,128)(2,1)} fusion(bf16[1152,256]{1,0:T(8,128)(2,1)} %collective-permute-done.24), kind=kLoop, calls=%fused_computation.6 | loop fusion | bytes 1179648
  106.5 2.1 %collective-permute-start.5 = (bf16[96,1024]{1,0:T(8,128)(2,1)S(1)}, bf16[96,1024]{1,0:T(8,128)(2,1)S(1)}, u32[]{:S(2)}, u32[]{:S(2)}) collective-permute-start(bf16[96,1024]{1,0:T(8,128)(2,1)S(1)} %get-tuple-element.33), channel_id=1, source_target_pairs={{0,3},{1,2},{2,1},{3,0},{4,7},{5,6},{6,5},{7,4},{8,11},{9,10},{10,... | collective-permute-start | bytes 589832 | tf_op jit(solution)/shard_map/ppermute | solution.py:191
  111.2 5.0 %collective-permute-start.23 = (bf16[2304,256]{1,0:T(8,128)(2,1)S(1)}, bf16[2304,256]{1,0:T(8,128)(2,1)}, u32[]{:S(2)}, u32[]{:S(2)}) collective-permute-start(bf16[2304,256]{1,0:T(8,128)(2,1)S(1)} %collective-permute-done.22.refs_4_), channel_id=1, source_target_pairs={{0,1},{1,0},{2,3},{3,2},{4,5},{5,4},{6,7},{7,6},{8,9},{9,8},{10,11... | collective-permute-start | bytes 3538952 | tf_op jit(solution)/shard_map/ppermute | solution.py:191
  116.2 2.4 %collective-permute-done.5.refs_3_ = bf16[96,1024]{1,0:T(8,128)(2,1)S(1)} collective-permute-done((bf16[96,1024]{1,0:T(8,128)(2,1)S(1)}, bf16[96,1024]{1,0:T(8,128)(2,1)S(1)}, u32[]{:S(2)}, u32[]{:S(2)}) %collective-permute-start.5) | collective-permute-done | bytes 196640 | tf_op jit(solution)/shard_map/ppermute | solution.py:191
  121.1 5.2 %shard_map.75 = (bf16[96,1024]{1,0:T(8,128)(2,1)}, bf16[96,1024]{1,0:T(8,128)(2,1)S(1)}) custom-call(bf16[96,1024]{1,0:T(8,128)(2,1)S(1)} %collective-permute-done.10.refs_0_, bf16[96,1024]{1,0:T(8,128)(2,1)S(1)} %collective-permute-done.11.refs_1_, bf16[4096,1024]{1,0:T(8,128)(2,1)S(1)} %bitcast.17, bf16[4096,1024]{1,0:T(8,128)(2,1)S(1)} %bitcast.20), custom_call_target="tpu_custom_call" | custom-call | tf_op jit(solution)/shard_map/pallas_call | solution.py:84
  126.3 5.3 %collective-permute-done.9.refs_5_ = bf16[96,1024]{1,0:T(8,128)(2,1)S(1)} collective-permute-done((bf16[96,1024]{1,0:T(8,128)(2,1)S(1)}, bf16[96,1024]{1,0:T(8,128)(2,1)S(1)}, u32[]{:S(2)}, u32[]{:S(2)}) %collective-permute-start.9) | collective-permute-done | bytes 196640 | tf_op jit(solution)/shard_map/ppermute | solution.py:191
  131.7 1.7 collective-permute-start.12
  135.7 4.2 %collective-permute-done.12.refs_6_ = bf16[96,1024]{1,0:T(8,128)(2,1)} collective-permute-done((bf16[96,1024]{1,0:T(8,128)(2,1)}, bf16[96,1024]{1,0:T(8,128)(2,1)}, u32[]{:S(2)}, u32[]{:S(2)}) %collective-permute-start.12) | collective-permute-done | bytes 196640 | tf_op jit(solution)/shard_map/ppermute | solution.py:191
  139.9 2.9 %collective-permute-start.13 = (bf16[96,1024]{1,0:T(8,128)(2,1)}, bf16[96,1024]{1,0:T(8,128)(2,1)S(1)}, u32[]{:S(2)}, u32[]{:S(2)}) collective-permute-start(bf16[96,1024]{1,0:T(8,128)(2,1)} %copy-done.14), channel_id=1, source_target_pairs={{0,7},{1,6},{2,5},{3,4},{4,3},{5,2},{6,1},{7,0},{8,15},{9,14},{10,... | collective-permute-start | bytes 589832 | tf_op jit(solution)/shard_map/ppermute | solution.py:191
  143.7 5.1 %collective-permute-done.13.refs_7_ = bf16[96,1024]{1,0:T(8,128)(2,1)S(1)} collective-permute-done((bf16[96,1024]{1,0:T(8,128)(2,1)}, bf16[96,1024]{1,0:T(8,128)(2,1)S(1)}, u32[]{:S(2)}, u32[]{:S(2)}) %collective-permute-start.13) | collective-permute-done | bytes 196640 | tf_op jit(solution)/shard_map/ppermute | solution.py:191
  152.5 2.0 %combine.1 = (bf16[256,1024]{1,0:T(8,128)(2,1)S(1)}, bf16[64,1024]{1,0:T(8,128)(2,1)S(1)}, bf16[64,1024]{1,0:T(8,128)(2,1)S(1)}) custom-call(bf16[256,1024]{1,0:T(8,128)(2,1)S(1)} %bitcast.22, f32[256,2]{1,0:T(8,128)S(1)} %add_divide_fusion.gates_ref, s32[256,2]{1,0:T(8,128)S(1)} %bitcast_add_fusion.cells_ref, ...), custom_call_target="tpu_custom_call" | custom-call | tf_op jit(solution)/shard_map/combine/pallas_call | solution.py:111
  154.6 6.5 %collective-permute-start.14 = (bf16[64,1024]{1,0:T(8,128)(2,1)S(1)}, bf16[64,1024]{1,0:T(8,128)(2,1)S(1)}, u32[]{:S(2)}, u32[]{:S(2)}) collective-permute-start(bf16[64,1024]{1,0:T(8,128)(2,1)S(1)} %get-tuple-element.43), channel_id=1, source_target_pairs={{0,1},{1,2},{2,3},{3,4},{4,5},{5,6},{6,7},{8,9},{9,10},{10,11},{11... | collective-permute-start | bytes 393224 | tf_op jit(solution)/shard_map/ppermute | solution.py:238
  161.0 1.9 %collective-permute-done.14.top_ref = bf16[64,1024]{1,0:T(8,128)(2,1)S(1)} collective-permute-done((bf16[64,1024]{1,0:T(8,128)(2,1)S(1)}, bf16[64,1024]{1,0:T(8,128)(2,1)S(1)}, u32[]{:S(2)}, u32[]{:S(2)}) %collective-permute-start.14) | collective-permute-done | bytes 131104 | tf_op jit(solution)/shard_map/ppermute | solution.py:238
  163.0 1.9 %collective-permute-start.15 = (bf16[64,1024]{1,0:T(8,128)(2,1)S(1)}, bf16[64,1024]{1,0:T(8,128)(2,1)S(1)}, u32[]{:S(2)}, u32[]{:S(2)}) collective-permute-start(bf16[64,1024]{1,0:T(8,128)(2,1)S(1)} %get-tuple-element.44), channel_id=1, source_target_pairs={{1,0},{2,1},{3,2},{4,3},{5,4},{6,5},{7,6},{9,8},{10,9},{11,10},{12... | collective-permute-start | bytes 393224 | tf_op jit(solution)/shard_map/ppermute | solution.py:239
  164.9 5.1 %collective-permute-done.15.bottom_ref = bf16[64,1024]{1,0:T(8,128)(2,1)S(1)} collective-permute-done((bf16[64,1024]{1,0:T(8,128)(2,1)S(1)}, bf16[64,1024]{1,0:T(8,128)(2,1)S(1)}, u32[]{:S(2)}, u32[]{:S(2)}) %collective-permute-start.15) | collective-permute-done | bytes 131104 | tf_op jit(solution)/shard_map/ppermute | solution.py:239
  170.0 6.3 %conv.1 = bf16[256,512]{1,0:T(8,128)(2,1)} custom-call(s32[3]{0:T(128)S(1)} %pad_add_fusion.place_ref, bf16[256,1024]{1,0:T(8,128)(2,1)S(1)} %get-tuple-element.42.mixed_ref, bf16[64,1024]{1,0:T(8,128)(2,1)S(1)} %collective-permute-done.14.top_ref, bf16[64,1024]{1,0:T(8,128)(2,1)S(1)} %collective-permute-done.15.bottom_ref, ...), custom_call_target="tpu_custom_call" | custom-call | tf_op jit(solution)/shard_map/conv/pallas_call | solution.py:178
  (82 shorter events, 26.7 us)
Async XLA Ops:
  0.0 133.4 %copy-start = (f32[1024,8]{0,1:T(8,128)S(1)}, f32[1024,8]{0,1:T(8,128)}, u32[]{:S(2)}) copy-start(f32[1024,8]{0,1:T(8,128)} %param.10) | copy-start | bytes 98308
  1.5 16.3 %collective-permute-start.17 = (bf16[1152,128]{1,0:T(8,128)(2,1)S(1)}, bf16[1152,128]{1,0:T(8,128)(2,1)S(1)}, u32[]{:S(2)}, u32[]{:S(2)}) collective-permute-start(bf16[1152,128]{1,0:T(8,128)(2,1)S(1)} %pad_maximum_fusion.refs_0_), channel_id=1, source_target_pairs={{0,4},{1,5},{2,6},{3,7},{4,0},{5,1},{6,2},{7,3},{8,12},{9,13},{10,... | collective-permute-start | bytes 884744 | tf_op jit(solution)/shard_map/ppermute | solution.py:191
  4.7 14.3 %collective-permute-start.16 = (bf16[1152,128]{1,0:T(8,128)(2,1)S(1)}, bf16[1152,128]{1,0:T(8,128)(2,1)S(1)}, u32[]{:S(2)}, u32[]{:S(2)}) collective-permute-start(bf16[1152,128]{1,0:T(8,128)(2,1)S(1)} %pad_maximum_fusion.refs_0_), channel_id=1, source_target_pairs={{0,2},{1,3},{2,0},{3,1},{4,6},{5,7},{6,4},{7,5},{8,10},{9,11},{10,... | collective-permute-start | bytes 884744 | tf_op jit(solution)/shard_map/ppermute | solution.py:191
  17.8 7.3 %collective-permute-start.18 = (bf16[1152,128]{1,0:T(8,128)(2,1)S(1)}, bf16[1152,128]{1,0:T(8,128)(2,1)S(1)}, u32[]{:S(2)}, u32[]{:S(2)}) collective-permute-start(bf16[1152,128]{1,0:T(8,128)(2,1)S(1)} %collective-permute-done.17.refs_2_), channel_id=1, source_target_pairs={{0,2},{1,3},{2,0},{3,1},{4,6},{5,7},{6,4},{7,5},{8,10},{9,11},{10,... | collective-permute-start | bytes 884744 | tf_op jit(solution)/shard_map/ppermute | solution.py:191
  19.0 9.6 %copy-start.16 = (s32[1,4,64,2]{2,3,1,0:T(2,128)S(1)}, s32[1,4,64,2]{2,3,1,0:T(2,128)}, u32[]{:S(2)}) copy-start(s32[1,4,64,2]{2,3,1,0:T(2,128)} %param.9) | copy-start | bytes 6148
  19.0 9.8 %copy-start.17 = (s32[1,4,64,2]{2,3,1,0:T(2,128)S(1)}, s32[1,4,64,2]{2,3,1,0:T(2,128)}, u32[]{:S(2)}) copy-start(s32[1,4,64,2]{2,3,1,0:T(2,128)} %param.8) | copy-start | bytes 6148
  26.4 27.5 %copy-start.5 = (bf16[1,4,64,1024]{3,2,1,0:T(8,128)(2,1)S(1)}, bf16[1,4,64,1024]{3,2,1,0:T(8,128)(2,1)}, u32[]{:S(2)}) copy-start(bf16[1,4,64,1024]{3,2,1,0:T(8,128)(2,1)} %param.7) | copy-start | bytes 1572868
  26.4 25.5 %collective-permute-start.22 = (bf16[2304,256]{1,0:T(8,128)(2,1)S(1)}, bf16[2304,256]{1,0:T(8,128)(2,1)S(1)}, u32[]{:S(2)}, u32[]{:S(2)}) collective-permute-start(bf16[2304,256]{1,0:T(8,128)(2,1)S(1)} %assemble.1.refs_0_), channel_id=1, source_target_pairs={{0,16},{8,24},{16,0},{24,8},{1,17},{9,25},{17,1},{25,9},{2,18},{10... | collective-permute-start | bytes 3538952 | tf_op jit(solution)/shard_map/ppermute | solution.py:191
  27.4 33.0 %collective-permute-start.20 = (bf16[2304,256]{1,0:T(8,128)(2,1)S(1)}, bf16[2304,256]{1,0:T(8,128)(2,1)}, u32[]{:S(2)}, u32[]{:S(2)}) collective-permute-start(bf16[2304,256]{1,0:T(8,128)(2,1)S(1)} %assemble.1.refs_0_), channel_id=1, source_target_pairs={{0,8},{8,0},{16,24},{24,16},{1,9},{9,1},{17,25},{25,17},{2,10},{10... | collective-permute-start | bytes 3538952 | tf_op jit(solution)/shard_map/ppermute | solution.py:191
  28.9 24.8 %copy-start.15 = (s32[1,4,64,2]{3,2,1,0:T(8,128)}, s32[1,4,64,2]{3,2,1,0:T(8,128)S(1)}, u32[]{:S(2)}) copy-start(s32[1,4,64,2]{3,2,1,0:T(8,128)S(1)} %copy.19) | copy-start | bytes 6148
  52.8 51.7 %collective-permute-start.24 = (bf16[1152,256]{1,0:T(8,128)(2,1)}, bf16[1152,256]{1,0:T(8,128)(2,1)}, u32[]{:S(2)}, u32[]{:S(2)}) collective-permute-start(bf16[1152,256]{1,0:T(8,128)(2,1)} %slice.18), channel_id=1, source_target_pairs={{0,8},{8,0},{16,24},{24,16},{1,9},{9,1},{17,25},{25,17},{2,10},{10... | collective-permute-start | bytes 1769480 | tf_op jit(solution)/shard_map/ppermute | solution.py:191
  55.0 8.2 %collective-permute-start = (bf16[96,1024]{1,0:T(8,128)(2,1)S(1)}, bf16[96,1024]{1,0:T(8,128)(2,1)S(1)}, u32[]{:S(2)}, u32[]{:S(2)}) collective-permute-start(bf16[96,1024]{1,0:T(8,128)(2,1)S(1)} %get-tuple-element.27), channel_id=1, source_target_pairs={{0,1},{1,0},{2,3},{3,2},{4,5},{5,4},{6,7},{7,6},{8,9},{9,8},{10,11... | collective-permute-start | bytes 589832 | tf_op jit(solution)/shard_map/ppermute | solution.py:191
  58.2 8.5 %collective-permute-start.1 = (bf16[96,1024]{1,0:T(8,128)(2,1)S(1)}, bf16[96,1024]{1,0:T(8,128)(2,1)S(1)}, u32[]{:S(2)}, u32[]{:S(2)}) collective-permute-start(bf16[96,1024]{1,0:T(8,128)(2,1)S(1)} %get-tuple-element.28), channel_id=1, source_target_pairs={{0,2},{1,3},{2,0},{3,1},{4,6},{5,7},{6,4},{7,5},{8,10},{9,11},{10,... | collective-permute-start | bytes 589832 | tf_op jit(solution)/shard_map/ppermute | solution.py:191
  61.6 47.1 %collective-permute-start.25 = (bf16[1152,256]{1,0:T(8,128)(2,1)S(1)}, bf16[1152,256]{1,0:T(8,128)(2,1)S(1)}, u32[]{:S(2)}, u32[]{:S(2)}) collective-permute-start(bf16[1152,256]{1,0:T(8,128)(2,1)S(1)} %slice.19), channel_id=1, source_target_pairs={{0,16},{8,24},{16,0},{24,8},{1,17},{9,25},{17,1},{25,9},{2,18},{10... | collective-permute-start | bytes 1769480 | tf_op jit(solution)/shard_map/ppermute | solution.py:191
  62.9 12.7 %collective-permute-start.2 = (bf16[96,1024]{1,0:T(8,128)(2,1)S(1)}, bf16[96,1024]{1,0:T(8,128)(2,1)S(1)}, u32[]{:S(2)}, u32[]{:S(2)}) collective-permute-start(bf16[96,1024]{1,0:T(8,128)(2,1)S(1)} %get-tuple-element.29), channel_id=1, source_target_pairs={{0,3},{1,2},{2,1},{3,0},{4,7},{5,6},{6,5},{7,4},{8,11},{9,10},{10,... | collective-permute-start | bytes 589832 | tf_op jit(solution)/shard_map/ppermute | solution.py:191
  63.1 27.0 %collective-permute-start.6 = (bf16[96,1024]{1,0:T(8,128)(2,1)S(1)}, bf16[96,1024]{1,0:T(8,128)(2,1)S(1)}, u32[]{:S(2)}, u32[]{:S(2)}) collective-permute-start(bf16[96,1024]{1,0:T(8,128)(2,1)S(1)} %get-tuple-element.34), channel_id=1, source_target_pairs={{0,4},{1,5},{2,6},{3,7},{4,0},{5,1},{6,2},{7,3},{8,12},{9,13},{10,... | collective-permute-start | bytes 589832 | tf_op jit(solution)/shard_map/ppermute | solution.py:191
  66.8 26.2 %collective-permute-start.7 = (bf16[96,1024]{1,0:T(8,128)(2,1)S(1)}, bf16[96,1024]{1,0:T(8,128)(2,1)S(1)}, u32[]{:S(2)}, u32[]{:S(2)}) collective-permute-start(bf16[96,1024]{1,0:T(8,128)(2,1)S(1)} %get-tuple-element.35), channel_id=1, source_target_pairs={{0,5},{1,4},{2,7},{3,6},{4,1},{5,0},{6,3},{7,2},{8,13},{9,12},{10,... | collective-permute-start | bytes 589832 | tf_op jit(solution)/shard_map/ppermute | solution.py:191
  75.6 31.0 %collective-permute-start.10 = (bf16[96,1024]{1,0:T(8,128)(2,1)S(1)}, bf16[96,1024]{1,0:T(8,128)(2,1)S(1)}, u32[]{:S(2)}, u32[]{:S(2)}) collective-permute-start(bf16[96,1024]{1,0:T(8,128)(2,1)S(1)} %get-tuple-element.38), channel_id=1, source_target_pairs={{0,6},{1,7},{2,4},{3,5},{4,2},{5,3},{6,0},{7,1},{8,14},{9,15},{10,... | collective-permute-start | bytes 589832 | tf_op jit(solution)/shard_map/ppermute | solution.py:191
  90.1 19.4 %collective-permute-start.11 = (bf16[96,1024]{1,0:T(8,128)(2,1)S(1)}, bf16[96,1024]{1,0:T(8,128)(2,1)S(1)}, u32[]{:S(2)}, u32[]{:S(2)}) collective-permute-start(bf16[96,1024]{1,0:T(8,128)(2,1)S(1)} %get-tuple-element.39), channel_id=1, source_target_pairs={{0,7},{1,6},{2,5},{3,4},{4,3},{5,2},{6,1},{7,0},{8,15},{9,14},{10,... | collective-permute-start | bytes 589832 | tf_op jit(solution)/shard_map/ppermute | solution.py:191
  93.0 16.6 %collective-permute-start.3 = (bf16[96,1024]{1,0:T(8,128)(2,1)S(1)}, bf16[96,1024]{1,0:T(8,128)(2,1)S(1)}, u32[]{:S(2)}, u32[]{:S(2)}) collective-permute-start(bf16[96,1024]{1,0:T(8,128)(2,1)S(1)} %get-tuple-element.31), channel_id=1, source_target_pairs={{0,1},{1,0},{2,3},{3,2},{4,5},{5,4},{6,7},{7,6},{8,9},{9,8},{10,11... | collective-permute-start | bytes 589832 | tf_op jit(solution)/shard_map/ppermute | solution.py:191
  104.5 6.0 %collective-permute-start.4 = (bf16[96,1024]{1,0:T(8,128)(2,1)S(1)}, bf16[96,1024]{1,0:T(8,128)(2,1)S(1)}, u32[]{:S(2)}, u32[]{:S(2)}) collective-permute-start(bf16[96,1024]{1,0:T(8,128)(2,1)S(1)} %get-tuple-element.32), channel_id=1, source_target_pairs={{0,2},{1,3},{2,0},{3,1},{4,6},{5,7},{6,4},{7,5},{8,10},{9,11},{10,... | collective-permute-start | bytes 589832 | tf_op jit(solution)/shard_map/ppermute | solution.py:191
  106.5 12.1 %collective-permute-start.5 = (bf16[96,1024]{1,0:T(8,128)(2,1)S(1)}, bf16[96,1024]{1,0:T(8,128)(2,1)S(1)}, u32[]{:S(2)}, u32[]{:S(2)}) collective-permute-start(bf16[96,1024]{1,0:T(8,128)(2,1)S(1)} %get-tuple-element.33), channel_id=1, source_target_pairs={{0,3},{1,2},{2,1},{3,0},{4,7},{5,6},{6,5},{7,4},{8,11},{9,10},{10,... | collective-permute-start | bytes 589832 | tf_op jit(solution)/shard_map/ppermute | solution.py:191
  108.7 11.9 %collective-permute-start.8 = (bf16[96,1024]{1,0:T(8,128)(2,1)S(1)}, bf16[96,1024]{1,0:T(8,128)(2,1)S(1)}, u32[]{:S(2)}, u32[]{:S(2)}) collective-permute-start(bf16[96,1024]{1,0:T(8,128)(2,1)S(1)} %get-tuple-element.36), channel_id=1, source_target_pairs={{0,4},{1,5},{2,6},{3,7},{4,0},{5,1},{6,2},{7,3},{8,12},{9,13},{10,... | collective-permute-start | bytes 589832 | tf_op jit(solution)/shard_map/ppermute | solution.py:191
  109.5 60.4 %collective-permute-start.19 = (bf16[2304,256]{1,0:T(8,128)(2,1)S(1)}, bf16[2304,256]{1,0:T(8,128)(2,1)}, u32[]{:S(2)}, u32[]{:S(2)}) collective-permute-start(bf16[2304,256]{1,0:T(8,128)(2,1)S(1)} %assemble.1.refs_0_), channel_id=1, source_target_pairs={{0,1},{1,0},{2,3},{3,2},{4,5},{5,4},{6,7},{7,6},{8,9},{9,8},{10,11... | collective-permute-start | bytes 3538952 | tf_op jit(solution)/shard_map/ppermute | solution.py:191
  109.5 60.4 %collective-permute-start.21 = (bf16[2304,256]{1,0:T(8,128)(2,1)}, bf16[2304,256]{1,0:T(8,128)(2,1)}, u32[]{:S(2)}, u32[]{:S(2)}) collective-permute-start(bf16[2304,256]{1,0:T(8,128)(2,1)} %collective-permute-done.20.refs_2_), channel_id=1, source_target_pairs={{0,1},{1,0},{2,3},{3,2},{4,5},{5,4},{6,7},{7,6},{8,9},{9,8},{10,11... | collective-permute-start | bytes 3538952 | tf_op jit(solution)/shard_map/ppermute | solution.py:191
  111.2 58.8 %collective-permute-start.23 = (bf16[2304,256]{1,0:T(8,128)(2,1)S(1)}, bf16[2304,256]{1,0:T(8,128)(2,1)}, u32[]{:S(2)}, u32[]{:S(2)}) collective-permute-start(bf16[2304,256]{1,0:T(8,128)(2,1)S(1)} %collective-permute-done.22.refs_4_), channel_id=1, source_target_pairs={{0,1},{1,0},{2,3},{3,2},{4,5},{5,4},{6,7},{7,6},{8,9},{9,8},{10,11... | collective-permute-start | bytes 3538952 | tf_op jit(solution)/shard_map/ppermute | solution.py:191
  119.3 50.7 %collective-permute-start.26 = (bf16[2304,256]{1,0:T(8,128)(2,1)}, bf16[2304,256]{1,0:T(8,128)(2,1)}, u32[]{:S(2)}, u32[]{:S(2)}) collective-permute-start(bf16[2304,256]{1,0:T(8,128)(2,1)} %constant_dynamic-update-slice_fusion.refs_6_), channel_id=1, source_target_pairs={{0,1},{1,0},{2,3},{3,2},{4,5},{5,4},{6,7},{7,6},{8,9},{9,8},{10,11... | collective-permute-start | bytes 3538952 | tf_op jit(solution)/shard_map/ppermute | solution.py:191
  120.6 11.1 %collective-permute-start.9 = (bf16[96,1024]{1,0:T(8,128)(2,1)S(1)}, bf16[96,1024]{1,0:T(8,128)(2,1)S(1)}, u32[]{:S(2)}, u32[]{:S(2)}) collective-permute-start(bf16[96,1024]{1,0:T(8,128)(2,1)S(1)} %get-tuple-element.37), channel_id=1, source_target_pairs={{0,5},{1,4},{2,7},{3,6},{4,1},{5,0},{6,3},{7,2},{8,13},{9,12},{10,... | collective-permute-start | bytes 589832 | tf_op jit(solution)/shard_map/ppermute | solution.py:191
  131.7 8.2 %collective-permute-start.12 = (bf16[96,1024]{1,0:T(8,128)(2,1)}, bf16[96,1024]{1,0:T(8,128)(2,1)}, u32[]{:S(2)}, u32[]{:S(2)}) collective-permute-start(bf16[96,1024]{1,0:T(8,128)(2,1)} %get-tuple-element.40), channel_id=1, source_target_pairs={{0,6},{1,7},{2,4},{3,5},{4,2},{5,3},{6,0},{7,1},{8,14},{9,15},{10,... | collective-permute-start | bytes 589832 | tf_op jit(solution)/shard_map/ppermute | solution.py:191
  139.9 8.9 %collective-permute-start.13 = (bf16[96,1024]{1,0:T(8,128)(2,1)}, bf16[96,1024]{1,0:T(8,128)(2,1)S(1)}, u32[]{:S(2)}, u32[]{:S(2)}) collective-permute-start(bf16[96,1024]{1,0:T(8,128)(2,1)} %copy-done.14), channel_id=1, source_target_pairs={{0,7},{1,6},{2,5},{3,4},{4,3},{5,2},{6,1},{7,0},{8,15},{9,14},{10,... | collective-permute-start | bytes 589832 | tf_op jit(solution)/shard_map/ppermute | solution.py:191
  154.6 8.4 %collective-permute-start.14 = (bf16[64,1024]{1,0:T(8,128)(2,1)S(1)}, bf16[64,1024]{1,0:T(8,128)(2,1)S(1)}, u32[]{:S(2)}, u32[]{:S(2)}) collective-permute-start(bf16[64,1024]{1,0:T(8,128)(2,1)S(1)} %get-tuple-element.43), channel_id=1, source_target_pairs={{0,1},{1,2},{2,3},{3,4},{4,5},{5,6},{6,7},{8,9},{9,10},{10,11},{11... | collective-permute-start | bytes 393224 | tf_op jit(solution)/shard_map/ppermute | solution.py:238
  163.0 7.0 %collective-permute-start.15 = (bf16[64,1024]{1,0:T(8,128)(2,1)S(1)}, bf16[64,1024]{1,0:T(8,128)(2,1)S(1)}, u32[]{:S(2)}, u32[]{:S(2)}) collective-permute-start(bf16[64,1024]{1,0:T(8,128)(2,1)S(1)} %get-tuple-element.44), channel_id=1, source_target_pairs={{1,0},{2,1},{3,2},{4,3},{5,4},{6,5},{7,6},{9,8},{10,9},{11,10},{12... | collective-permute-start | bytes 393224 | tf_op jit(solution)/shard_map/ppermute | solution.py:239
  (13 other events, 34.1 us)

commit v2 on v1

--- a/solution.py
+++ b/solution.py
@@ -88,12 +88,27 @@
     )(*blocks, w_in, w_out)
 
 
-def combine(tok, gates, cells, results, edge):
+def gate(logits, routes, w_in, w_out):
+    count, experts = logits.shape
+
+    def kernel(logits_ref, routes_ref, w_in_ref, w_out_ref, out):
+        col = lax.broadcasted_iota(jnp.int32, (count, experts), 1)
+        for k in range(2):
+            chosen = jnp.where(col == routes_ref[:, k : k + 1], logits_ref[...], 0.0)
+            out[:, k : k + 1] = jax.nn.sigmoid(jnp.sum(chosen, axis=1, keepdims=True))
+
+    return pl.pallas_call(
+        kernel, out_shape=jax.ShapeDtypeStruct((count, 2), F32), in_specs=[VM] * 4, out_specs=VM,
+        compiler_params=pltpu.CompilerParams(vmem_limit_bytes=4 * 2**20), name="gate",
+    )(logits, routes, w_in, w_out)
+
+
+def combine(place, tok, gates, cells, results, edge):
     count, width = tok.shape
     n, cap = len(results), results[0].shape[0]
 
-    def kernel(tok_ref, gates_ref, cells_ref, *refs):
-        res, (mixed_ref, low_ref, high_ref, scr) = refs[:n], refs[n:]
+    def kernel(place_ref, tok_ref, gates_ref, cells_ref, *refs):
+        res, (mixed_ref, inner_ref, outer_ref, scr) = refs[:n], refs[n:]
         for k in range(n):
             scr[k * cap : (k + 1) * cap, :] = res[k][...]
         cols = lax.broadcasted_iota(jnp.int32, (count, n * cap), 1)
@@ -104,15 +119,17 @@
             total = total + picked * gates_ref[:, k : k + 1]
         mixed = (tok_ref[...].astype(F32) + total).astype(BF16)
         mixed_ref[...] = mixed
-        low_ref[...] = mixed[:edge, :]
-        high_ref[...] = mixed[count - edge :, :]
+        first = place_ref[2] == 0
+        low, high = mixed[:edge, :], mixed[count - edge :, :]
+        inner_ref[...] = jnp.where(first, high, low)
+        outer_ref[...] = jnp.where(first, low, high)
 
     outs = [jax.ShapeDtypeStruct((r, width), BF16) for r in (count, edge, edge)]
     return pl.pallas_call(
-        kernel, out_shape=outs, in_specs=[VM] * (3 + n), out_specs=[VM] * 3,
+        kernel, out_shape=outs, in_specs=[SM] + [VM] * (3 + n), out_specs=[VM] * 3,
         scratch_shapes=[pltpu.VMEM((n * cap, width), BF16)],
         compiler_params=PARAMS, name="combine",
-    )(tok, gates, cells, *results)
+    )(place, tok, gates, cells, *results)
 
 
 def assemble(place, pieces, lanes):
@@ -134,22 +151,25 @@
     )(place, *pieces)
 
 
-def conv(place, mixed, top, bottom, mine, theirs, lanes):
+def conv(place, mixed, inner, outer, mine, theirs, lanes):
     count, _ = mixed.shape
-    edge = top.shape[0]
+    edge = inner.shape[0]
     quarters = len(mine)
     chans, cols = mine[0].shape[0] // 9, mine[0].shape[1]
     n = cols // lanes
 
-    def kernel(place_ref, mixed_ref, top_ref, bottom_ref, *refs):
+    def kernel(place_ref, mixed_ref, inner_ref, outer_ref, *refs):
         weights, (out, x_scr, w_scr, sems) = refs[: 2 * quarters], refs[2 * quarters :]
         copies = [pltpu.make_async_copy(w, w_scr.at[i], sems.at[i]) for i, w in enumerate(weights)]
         for c in copies:
             c.start()
+        first = place_ref[2] == 0
+        top = jnp.where(first, outer_ref[...], inner_ref[...])
+        bottom = jnp.where(first, inner_ref[...], outer_ref[...])
         for q in range(quarters):
-            x_scr[q, 0:edge, :] = top_ref[:, q * chans : (q + 1) * chans]
+            x_scr[q, 0:edge, :] = top[:, q * chans : (q + 1) * chans]
             x_scr[q, edge : edge + count, :] = mixed_ref[:, q * chans : (q + 1) * chans]
-            x_scr[q, edge + count :, :] = bottom_ref[:, q * chans : (q + 1) * chans]
+            x_scr[q, edge + count :, :] = bottom[:, q * chans : (q + 1) * chans]
         col = lax.broadcasted_iota(jnp.int32, (count, cols), 0) % edge
         accs = [[jnp.zeros((count, cols), F32) for _ in range(3)] for _ in range(2)]
         for k in range(quarters):
@@ -184,7 +204,7 @@
             pltpu.SemaphoreType.DMA((2 * quarters,)),
         ],
         compiler_params=PARAMS, name="conv",
-    )(place, mixed, top, bottom, *weights)
+    )(place, mixed, inner, outer, *weights)
 
 
 def flip(value, axis, k):
@@ -226,18 +246,18 @@
     normed, blocks = prologue(tok, cells.T, experts, cap)
     received = [blocks[0]] + [flip(blocks[k], "expert", k) for k in range(1, experts)]
     mine, theirs = gather_filters(conv_weight, place)
+    logits = jnp.dot(normed.astype(F32), router, precision=lax.Precision.HIGHEST)
+    gates = gate(logits, routes, expert_in[0], expert_out[0])
     half, mid = experts // 2, 3 * experts // 4
     produced = []
     for part in (slice(0, half), slice(half, mid), slice(mid, experts)):
         produced += list(mlp(received[part], expert_in[0], expert_out[0]))
     returned = [produced[0]] + [flip(produced[k], "expert", k) for k in range(1, experts)]
-    logits = jnp.dot(normed.astype(F32), router, precision=lax.Precision.HIGHEST)
-    matches = routes[:, :, None] == lax.broadcasted_iota(jnp.int32, (1, 1, experts), 2)
-    gates = jax.nn.sigmoid(jnp.sum(jnp.where(matches, logits[:, None, :], 0.0), axis=2))
-    mixed, low, high = combine(tok, gates, cells, returned, span_cols)
-    top = lax.ppermute(high, "expert", [(i, i + 1) for i in range(experts - 1)])
-    bottom = lax.ppermute(low, "expert", [(i + 1, i) for i in range(experts - 1)])
-    out = conv(place, mixed, top, bottom, mine, theirs, conv_weight.shape[3])
+    mixed, inner, outer = combine(place, tok, gates, cells, returned, span_cols)
+    joints = [(i, i + 1) for i in range(1, experts - 1, 2)]
+    outer = lax.ppermute(outer, "expert", joints + [(j, i) for i, j in joints])
+    inner = flip(inner, "expert", 1)
+    out = conv(place, mixed, inner, outer, mine, theirs, conv_weight.shape[3])
     return out.reshape(images, strip_rows, span_cols, out.shape[1])
 
 

time: 177 us -> 180 us (1.017)
  waiting for transfers between devices: 72.5 us -> 84.3 us
  local copies, waits for them, and re-layouts: 26.8 us -> 20.2 us
    ppermute x25 -> x26, waiting for transfers between devices: 65.5 us -> 81.7 us  [flip(): lax.ppermute(value, axis, [(i, i ^ k) for i in range(lax.axis_size(axis))])]
    unnamed x40 -> x24, local copies, waits for them, and re-layouts: 22.1 us -> 16.2 us
    ppermute x2 -> x1, waiting for transfers between devices: 7 us -> 2.64 us  [shards(): outer = lax.ppermute(outer, 'expert', joints + [(j, i) for i, j in joints])]
    ppermute x2 -> x1, starting transfers between devices: 8.4 us -> 6.4 us  [shards(): outer = lax.ppermute(outer, 'expert', joints + [(j, i) for i, j in joints])]
    ppermute x25 -> x26, starting transfers between devices: 39.1 us -> 39.6 us  [flip(): lax.ppermute(value, axis, [(i, i ^ k) for i in range(lax.axis_size(axis))])]
  transfers between devices with their start and end apart: 27 -> 27, of which waited for: 12 -> 13; matrix products, arithmetic and copies ran while one was open for 5% -> 3% of each run, Pallas kernels for 11% -> 11%
where the time goes in v2:
time: 180 us; the launch traced here: 179 us
  waiting for transfers between devices  84.3 us (47%)
  starting transfers between devices  46 us (26%)
  Pallas kernels  27.4 us (15%)
  local copies, waits for them, and re-layouts  20.2 us (11%)
    ppermute x26, waiting for transfers between devices, flip(): lax.ppermute(value, axis, [(i, i ^ k) for i in range(lax.axis_size(axis))])  81.7 us
    ppermute x26, starting transfers between devices, flip(): lax.ppermute(value, axis, [(i, i ^ k) for i in range(lax.axis_size(axis))])  39.6 us
    unnamed x24, local copies, waits for them, and re-layouts  16.2 us
    pallas_call x3, Pallas kernels, mlp(): pl.pallas_call(kernel, in_specs=[VM] * n + [ANY if stream else VM] * 2, o...  16.1 us
    pallas_call x1, Pallas kernels, conv(): pl.pallas_call(kernel, out_shape=jax.ShapeDtypeStruct((count, 2 * cols),...  7.01 us
    ppermute x1, starting transfers between devices, shards(): outer = lax.ppermute(outer, 'expert', joints + [(j, i) for i, j in joints])  6.4 us
  transfers between devices with their start and end apart: 27, of which 13 were waited for; matrix products, arithmetic and copies ran while one was open for 3% of the time, Pallas kernels for 11%

profile of v2, /device:TPU:1, one launch (start us, length us, event | category | flops | bytes accessed | tf_op | source)
XLA Modules:
  0.0 179.2 jit_solution(17804179530600408061)
XLA Ops:
  1.5 3.2 %collective-permute-start.17 = (bf16[1152,128]{1,0:T(8,128)(2,1)S(1)}, bf16[1152,128]{1,0:T(8,128)(2,1)S(1)}, u32[]{:S(2)}, u32[]{:S(2)}) collective-permute-start(bf16[1152,128]{1,0:T(8,128)(2,1)S(1)} %pad_maximum_fusion.refs_0_), channel_id=1, source_target_pairs={{0,4},{1,5},{2,6},{3,7},{4,0},{5,1},{6,2},{7,3},{8,12},{9,13},{10,... | collective-permute-start | bytes 884744 | tf_op jit(solution)/shard_map/ppermute | solution.py:211
  6.0 11.8 %collective-permute-done.17.refs_2_ = bf16[1152,128]{1,0:T(8,128)(2,1)S(1)} collective-permute-done((bf16[1152,128]{1,0:T(8,128)(2,1)S(1)}, bf16[1152,128]{1,0:T(8,128)(2,1)S(1)}, u32[]{:S(2)}, u32[]{:S(2)}) %collective-permute-start.17) | collective-permute-done | bytes 294944 | tf_op jit(solution)/shard_map/ppermute | solution.py:211
  19.0 6.0 %collective-permute-done.18.refs_3_ = bf16[1152,128]{1,0:T(8,128)(2,1)S(1)} collective-permute-done((bf16[1152,128]{1,0:T(8,128)(2,1)S(1)}, bf16[1152,128]{1,0:T(8,128)(2,1)S(1)}, u32[]{:S(2)}, u32[]{:S(2)}) %collective-permute-start.18) | collective-permute-done | bytes 294944 | tf_op jit(solution)/shard_map/ppermute | solution.py:211
  28.7 23.3 %collective-permute-done.22.refs_4_ = bf16[2304,256]{1,0:T(8,128)(2,1)S(1)} collective-permute-done((bf16[2304,256]{1,0:T(8,128)(2,1)S(1)}, bf16[2304,256]{1,0:T(8,128)(2,1)S(1)}, u32[]{:S(2)}, u32[]{:S(2)}) %collective-permute-start.22) | collective-permute-done | bytes 1179680 | tf_op jit(solution)/shard_map/ppermute | solution.py:211
  54.0 1.9 %slice.19 = bf16[1152,256]{1,0:T(8,128)(2,1)} slice(bf16[2304,256]{1,0:T(8,128)(2,1)} %collective-permute-done.20.refs_2_), slice={[1152:2304], [0:256]} | slice | bytes 1179648 | tf_op jit(solution)/shard_map/slice | solution.py:228
  58.4 3.6 %collective-permute-start = (bf16[96,1024]{1,0:T(8,128)(2,1)S(1)}, bf16[96,1024]{1,0:T(8,128)(2,1)S(1)}, u32[]{:S(2)}, u32[]{:S(2)}) collective-permute-start(bf16[96,1024]{1,0:T(8,128)(2,1)S(1)} %get-tuple-element.27), channel_id=1, source_target_pairs={{0,1},{1,0},{2,3},{3,2},{4,5},{5,4},{6,7},{7,6},{8,9},{9,8},{10,11... | collective-permute-start | bytes 589832 | tf_op jit(solution)/shard_map/ppermute | solution.py:211
  61.9 2.2 %collective-permute-start.1 = (bf16[96,1024]{1,0:T(8,128)(2,1)S(1)}, bf16[96,1024]{1,0:T(8,128)(2,1)S(1)}, u32[]{:S(2)}, u32[]{:S(2)}) collective-permute-start(bf16[96,1024]{1,0:T(8,128)(2,1)S(1)} %get-tuple-element.28), channel_id=1, source_target_pairs={{0,2},{1,3},{2,0},{3,1},{4,6},{5,7},{6,4},{7,5},{8,10},{9,11},{10,... | collective-permute-start | bytes 589832 | tf_op jit(solution)/shard_map/ppermute | solution.py:211
  64.2 3.6 %collective-permute-start.6 = (bf16[96,1024]{1,0:T(8,128)(2,1)S(1)}, bf16[96,1024]{1,0:T(8,128)(2,1)S(1)}, u32[]{:S(2)}, u32[]{:S(2)}) collective-permute-start(bf16[96,1024]{1,0:T(8,128)(2,1)S(1)} %get-tuple-element.34), channel_id=1, source_target_pairs={{0,4},{1,5},{2,6},{3,7},{4,0},{5,1},{6,2},{7,3},{8,12},{9,13},{10,... | collective-permute-start | bytes 589832 | tf_op jit(solution)/shard_map/ppermute | solution.py:211
  67.8 5.8 %collective-permute-done.1.refs_2_ = bf16[96,1024]{1,0:T(8,128)(2,1)S(1)} collective-permute-done((bf16[96,1024]{1,0:T(8,128)(2,1)S(1)}, bf16[96,1024]{1,0:T(8,128)(2,1)S(1)}, u32[]{:S(2)}, u32[]{:S(2)}) %collective-permute-start.1) | collective-permute-done | bytes 196640 | tf_op jit(solution)/shard_map/ppermute | solution.py:211
  73.5 3.4 %collective-permute-start.7 = (bf16[96,1024]{1,0:T(8,128)(2,1)S(1)}, bf16[96,1024]{1,0:T(8,128)(2,1)S(1)}, u32[]{:S(2)}, u32[]{:S(2)}) collective-permute-start(bf16[96,1024]{1,0:T(8,128)(2,1)S(1)} %get-tuple-element.35), channel_id=1, source_target_pairs={{0,5},{1,4},{2,7},{3,6},{4,1},{5,0},{6,3},{7,2},{8,13},{9,12},{10,... | collective-permute-start | bytes 589832 | tf_op jit(solution)/shard_map/ppermute | solution.py:211
  78.0 4.0 %collective-permute-start.10 = (bf16[96,1024]{1,0:T(8,128)(2,1)S(1)}, bf16[96,1024]{1,0:T(8,128)(2,1)S(1)}, u32[]{:S(2)}, u32[]{:S(2)}) collective-permute-start(bf16[96,1024]{1,0:T(8,128)(2,1)S(1)} %get-tuple-element.38), channel_id=1, source_target_pairs={{0,6},{1,7},{2,4},{3,5},{4,2},{5,3},{6,0},{7,1},{8,14},{9,15},{10,... | collective-permute-start | bytes 589832 | tf_op jit(solution)/shard_map/ppermute | solution.py:211
  82.1 3.4 %copy-done.1 = bf16[1,4096,1024]{2,1,0:T(8,128)(2,1)S(1)} copy-done((bf16[1,4096,1024]{2,1,0:T(8,128)(2,1)S(1)}, bf16[1,4096,1024]{2,1,0:T(8,128)(2,1)}, u32[]{:S(2)}) %copy-start.1) | copy-done | bytes 8388632
  85.4 3.4 %copy-done.3 = bf16[1,4096,1024]{2,1,0:T(8,128)(2,1)S(1)} copy-done((bf16[1,4096,1024]{2,1,0:T(8,128)(2,1)S(1)}, bf16[1,4096,1024]{2,1,0:T(8,128)(2,1)}, u32[]{:S(2)}) %copy-start.3) | copy-done | bytes 8388632
  88.8 6.8 %shard_map.73 = (bf16[96,1024]{1,0:T(8,128)(2,1)S(1)}, bf16[96,1024]{1,0:T(8,128)(2,1)S(1)}, bf16[96,1024]{1,0:T(8,128)(2,1)S(1)}, bf16[96,1024]{1,0:T(8,128)(2,1)S(1)}) custom-call(bf16[96,1024]{1,0:T(8,128)(2,1)S(1)} %get-tuple-element.26.refs_0_, bf16[96,1024]{1,0:T(8,128)(2,1)S(1)} %collective-permute-done.refs_1_, ...), custom_call_target="tpu_custom_call" | custom-call | tf_op jit(solution)/shard_map/pallas_call | solution.py:84
  97.3 1.8 collective-permute-start.5
  100.3 4.4 %collective-permute-done.11.refs_1_ = bf16[96,1024]{1,0:T(8,128)(2,1)S(1)} collective-permute-done((bf16[96,1024]{1,0:T(8,128)(2,1)S(1)}, bf16[96,1024]{1,0:T(8,128)(2,1)S(1)}, u32[]{:S(2)}, u32[]{:S(2)}) %collective-permute-start.11) | collective-permute-done | bytes 196640 | tf_op jit(solution)/shard_map/ppermute | solution.py:211
  105.2 2.6 %collective-permute-done.4.refs_2_ = bf16[96,1024]{1,0:T(8,128)(2,1)S(1)} collective-permute-done((bf16[96,1024]{1,0:T(8,128)(2,1)S(1)}, bf16[96,1024]{1,0:T(8,128)(2,1)S(1)}, u32[]{:S(2)}, u32[]{:S(2)}) %collective-permute-start.4) | collective-permute-done | bytes 196640 | tf_op jit(solution)/shard_map/ppermute | solution.py:211
  107.8 1.5 collective-permute-start.26
  109.4 3.4 %copy-done.2 = bf16[1,4096,1024]{2,1,0:T(8,128)(2,1)S(1)} copy-done((bf16[1,4096,1024]{2,1,0:T(8,128)(2,1)S(1)}, bf16[1,4096,1024]{2,1,0:T(8,128)(2,1)}, u32[]{:S(2)}) %copy-start.2) | copy-done | bytes 8388632
  112.8 3.4 %copy-done.4 = bf16[1,4096,1024]{2,1,0:T(8,128)(2,1)S(1)} copy-done((bf16[1,4096,1024]{2,1,0:T(8,128)(2,1)S(1)}, bf16[1,4096,1024]{2,1,0:T(8,128)(2,1)}, u32[]{:S(2)}) %copy-start.4) | copy-done | bytes 8388632
  116.1 4.7 %shard_map.74 = (bf16[96,1024]{1,0:T(8,128)(2,1)S(1)}, bf16[96,1024]{1,0:T(8,128)(2,1)S(1)}) custom-call(bf16[96,1024]{1,0:T(8,128)(2,1)S(1)} %collective-permute-done.6.refs_0_, bf16[96,1024]{1,0:T(8,128)(2,1)S(1)} %collective-permute-done.7.refs_1_, bf16[4096,1024]{1,0:T(8,128)(2,1)S(1)} %bitcast.16, bf16[4096,1024]{1,0:T(8,128)(2,1)S(1)} %bitcast.22), custom_call_target="tpu_custom_call" | custom-call | tf_op jit(solution)/shard_map/pallas_call | solution.py:84
  121.5 10.4 %collective-permute-done.8.refs_4_ = bf16[96,1024]{1,0:T(8,128)(2,1)S(1)} collective-permute-done((bf16[96,1024]{1,0:T(8,128)(2,1)S(1)}, bf16[96,1024]{1,0:T(8,128)(2,1)S(1)}, u32[]{:S(2)}, u32[]{:S(2)}) %collective-permute-start.8) | collective-permute-done | bytes 196640 | tf_op jit(solution)/shard_map/ppermute | solution.py:211
  131.9 4.6 %shard_map.75 = (bf16[96,1024]{1,0:T(8,128)(2,1)S(1)}, bf16[96,1024]{1,0:T(8,128)(2,1)S(1)}) custom-call(bf16[96,1024]{1,0:T(8,128)(2,1)S(1)} %collective-permute-done.10.refs_0_, bf16[96,1024]{1,0:T(8,128)(2,1)S(1)} %collective-permute-done.11.refs_1_, bf16[4096,1024]{1,0:T(8,128)(2,1)S(1)} %bitcast.17, bf16[4096,1024]{1,0:T(8,128)(2,1)S(1)} %bitcast.23), custom_call_target="tpu_custom_call" | custom-call | tf_op jit(solution)/shard_map/pallas_call | solution.py:84
  136.5 5.5 %collective-permute-done.9.refs_5_ = bf16[96,1024]{1,0:T(8,128)(2,1)S(1)} collective-permute-done((bf16[96,1024]{1,0:T(8,128)(2,1)S(1)}, bf16[96,1024]{1,0:T(8,128)(2,1)S(1)}, u32[]{:S(2)}, u32[]{:S(2)}) %collective-permute-start.9) | collective-permute-done | bytes 196640 | tf_op jit(solution)/shard_map/ppermute | solution.py:211
  142.0 2.8 %collective-permute-start.12 = (bf16[96,1024]{1,0:T(8,128)(2,1)S(1)}, bf16[96,1024]{1,0:T(8,128)(2,1)S(1)}, u32[]{:S(2)}, u32[]{:S(2)}) collective-permute-start(bf16[96,1024]{1,0:T(8,128)(2,1)S(1)} %get-tuple-element.40), channel_id=1, source_target_pairs={{0,6},{1,7},{2,4},{3,5},{4,2},{5,3},{6,0},{7,1},{8,14},{9,15},{10,... | collective-permute-start | bytes 589832 | tf_op jit(solution)/shard_map/ppermute | solution.py:211
  144.9 5.1 %collective-permute-done.12.refs_6_ = bf16[96,1024]{1,0:T(8,128)(2,1)S(1)} collective-permute-done((bf16[96,1024]{1,0:T(8,128)(2,1)S(1)}, bf16[96,1024]{1,0:T(8,128)(2,1)S(1)}, u32[]{:S(2)}, u32[]{:S(2)}) %collective-permute-start.12) | collective-permute-done | bytes 196640 | tf_op jit(solution)/shard_map/ppermute | solution.py:211
  149.9 4.0 %collective-permute-start.13 = (bf16[96,1024]{1,0:T(8,128)(2,1)S(1)}, bf16[96,1024]{1,0:T(8,128)(2,1)S(1)}, u32[]{:S(2)}, u32[]{:S(2)}) collective-permute-start(bf16[96,1024]{1,0:T(8,128)(2,1)S(1)} %get-tuple-element.41), channel_id=1, source_target_pairs={{0,7},{1,6},{2,5},{3,4},{4,3},{5,2},{6,1},{7,0},{8,15},{9,14},{10,... | collective-permute-start | bytes 589832 | tf_op jit(solution)/shard_map/ppermute | solution.py:211
  154.9 4.8 %collective-permute-done.13.refs_7_ = bf16[96,1024]{1,0:T(8,128)(2,1)S(1)} collective-permute-done((bf16[96,1024]{1,0:T(8,128)(2,1)S(1)}, bf16[96,1024]{1,0:T(8,128)(2,1)S(1)}, u32[]{:S(2)}, u32[]{:S(2)}) %collective-permute-start.13) | collective-permute-done | bytes 196640 | tf_op jit(solution)/shard_map/ppermute | solution.py:211
  159.6 1.6 combine.1
  162.9 6.4 %collective-permute-start.15 = (bf16[64,1024]{1,0:T(8,128)(2,1)S(1)}, bf16[64,1024]{1,0:T(8,128)(2,1)S(1)}, u32[]{:S(2)}, u32[]{:S(2)}) collective-permute-start(bf16[64,1024]{1,0:T(8,128)(2,1)S(1)} %get-tuple-element.44), channel_id=1, source_target_pairs={{1,2},{3,4},{5,6},{2,1},{4,3},{6,5},{9,10},{11,12},{13,14},{10,9},... | collective-permute-start | bytes 393224 | tf_op jit(solution)/shard_map/ppermute | solution.py:258
  169.3 2.6 %collective-permute-done.15.outer_ref = bf16[64,1024]{1,0:T(8,128)(2,1)S(1)} collective-permute-done((bf16[64,1024]{1,0:T(8,128)(2,1)S(1)}, bf16[64,1024]{1,0:T(8,128)(2,1)S(1)}, u32[]{:S(2)}, u32[]{:S(2)}) %collective-permute-start.15) | collective-permute-done | bytes 131104 | tf_op jit(solution)/shard_map/ppermute | solution.py:258
  172.0 7.0 %conv.1 = bf16[256,512]{1,0:T(8,128)(2,1)} custom-call(s32[3]{0:T(128)S(1)} %pad_add_fusion.place_ref, bf16[256,1024]{1,0:T(8,128)(2,1)S(1)} %get-tuple-element.42.mixed_ref, bf16[64,1024]{1,0:T(8,128)(2,1)S(1)} %collective-permute-done.14.inner_ref, bf16[64,1024]{1,0:T(8,128)(2,1)S(1)} %collective-permute-done.15.outer_ref, ...), custom_call_target="tpu_custom_call" | custom-call | tf_op jit(solution)/shard_map/conv/pallas_call | solution.py:198
  (64 shorter events, 19.8 us)
Async XLA Ops:
  0.0 154.0 %copy-start = (f32[1024,8]{0,1:T(8,128)S(1)}, f32[1024,8]{0,1:T(8,128)}, u32[]{:S(2)}) copy-start(f32[1024,8]{0,1:T(8,128)} %param.10) | copy-start | bytes 98308
  1.5 16.3 %collective-permute-start.17 = (bf16[1152,128]{1,0:T(8,128)(2,1)S(1)}, bf16[1152,128]{1,0:T(8,128)(2,1)S(1)}, u32[]{:S(2)}, u32[]{:S(2)}) collective-permute-start(bf16[1152,128]{1,0:T(8,128)(2,1)S(1)} %pad_maximum_fusion.refs_0_), channel_id=1, source_target_pairs={{0,4},{1,5},{2,6},{3,7},{4,0},{5,1},{6,2},{7,3},{8,12},{9,13},{10,... | collective-permute-start | bytes 884744 | tf_op jit(solution)/shard_map/ppermute | solution.py:211
  4.7 14.3 %collective-permute-start.16 = (bf16[1152,128]{1,0:T(8,128)(2,1)S(1)}, bf16[1152,128]{1,0:T(8,128)(2,1)S(1)}, u32[]{:S(2)}, u32[]{:S(2)}) collective-permute-start(bf16[1152,128]{1,0:T(8,128)(2,1)S(1)} %pad_maximum_fusion.refs_0_), channel_id=1, source_target_pairs={{0,2},{1,3},{2,0},{3,1},{4,6},{5,7},{6,4},{7,5},{8,10},{9,11},{10,... | collective-permute-start | bytes 884744 | tf_op jit(solution)/shard_map/ppermute | solution.py:211
  17.8 7.3 %collective-permute-start.18 = (bf16[1152,128]{1,0:T(8,128)(2,1)S(1)}, bf16[1152,128]{1,0:T(8,128)(2,1)S(1)}, u32[]{:S(2)}, u32[]{:S(2)}) collective-permute-start(bf16[1152,128]{1,0:T(8,128)(2,1)S(1)} %collective-permute-done.17.refs_2_), channel_id=1, source_target_pairs={{0,2},{1,3},{2,0},{3,1},{4,6},{5,7},{6,4},{7,5},{8,10},{9,11},{10,... | collective-permute-start | bytes 884744 | tf_op jit(solution)/shard_map/ppermute | solution.py:211
  26.3 27.4 %copy-start.6 = (s32[1,4,64,2]{2,3,1,0:T(2,128)S(1)}, s32[1,4,64,2]{2,3,1,0:T(2,128)}, u32[]{:S(2)}) copy-start(s32[1,4,64,2]{2,3,1,0:T(2,128)} %param.9) | copy-start | bytes 6148
  26.4 27.5 %copy-start.7 = (s32[1,4,64,2]{2,3,1,0:T(2,128)S(1)}, s32[1,4,64,2]{2,3,1,0:T(2,128)}, u32[]{:S(2)}) copy-start(s32[1,4,64,2]{2,3,1,0:T(2,128)} %param.8) | copy-start | bytes 6148
  26.4 25.5 %collective-permute-start.22 = (bf16[2304,256]{1,0:T(8,128)(2,1)S(1)}, bf16[2304,256]{1,0:T(8,128)(2,1)S(1)}, u32[]{:S(2)}, u32[]{:S(2)}) collective-permute-start(bf16[2304,256]{1,0:T(8,128)(2,1)S(1)} %assemble.1.refs_0_), channel_id=1, source_target_pairs={{0,16},{8,24},{16,0},{24,8},{1,17},{9,25},{17,1},{25,9},{2,18},{10... | collective-permute-start | bytes 3538952 | tf_op jit(solution)/shard_map/ppermute | solution.py:211
  27.4 26.5 %collective-permute-start.20 = (bf16[2304,256]{1,0:T(8,128)(2,1)S(1)}, bf16[2304,256]{1,0:T(8,128)(2,1)}, u32[]{:S(2)}, u32[]{:S(2)}) collective-permute-start(bf16[2304,256]{1,0:T(8,128)(2,1)S(1)} %assemble.1.refs_0_), channel_id=1, source_target_pairs={{0,8},{8,0},{16,24},{24,16},{1,9},{9,1},{17,25},{25,17},{2,10},{10... | collective-permute-start | bytes 3538952 | tf_op jit(solution)/shard_map/ppermute | solution.py:211
  52.8 42.8 %collective-permute-start.24 = (bf16[1152,256]{1,0:T(8,128)(2,1)}, bf16[1152,256]{1,0:T(8,128)(2,1)}, u32[]{:S(2)}, u32[]{:S(2)}) collective-permute-start(bf16[1152,256]{1,0:T(8,128)(2,1)} %slice.18), channel_id=1, source_target_pairs={{0,8},{8,0},{16,24},{24,16},{1,9},{9,1},{17,25},{25,17},{2,10},{10... | collective-permute-start | bytes 1769480 | tf_op jit(solution)/shard_map/ppermute | solution.py:211
  55.9 41.4 %collective-permute-start.25 = (bf16[1152,256]{1,0:T(8,128)(2,1)}, bf16[1152,256]{1,0:T(8,128)(2,1)}, u32[]{:S(2)}, u32[]{:S(2)}) collective-permute-start(bf16[1152,256]{1,0:T(8,128)(2,1)} %slice.19), channel_id=1, source_target_pairs={{0,16},{8,24},{16,0},{24,8},{1,17},{9,25},{17,1},{25,9},{2,18},{10... | collective-permute-start | bytes 1769480 | tf_op jit(solution)/shard_map/ppermute | solution.py:211
  58.4 5.8 %collective-permute-start = (bf16[96,1024]{1,0:T(8,128)(2,1)S(1)}, bf16[96,1024]{1,0:T(8,128)(2,1)S(1)}, u32[]{:S(2)}, u32[]{:S(2)}) collective-permute-start(bf16[96,1024]{1,0:T(8,128)(2,1)S(1)} %get-tuple-element.27), channel_id=1, source_target_pairs={{0,1},{1,0},{2,3},{3,2},{4,5},{5,4},{6,7},{7,6},{8,9},{9,8},{10,11... | collective-permute-start | bytes 589832 | tf_op jit(solution)/shard_map/ppermute | solution.py:211
  61.9 11.6 %collective-permute-start.1 = (bf16[96,1024]{1,0:T(8,128)(2,1)S(1)}, bf16[96,1024]{1,0:T(8,128)(2,1)S(1)}, u32[]{:S(2)}, u32[]{:S(2)}) collective-permute-start(bf16[96,1024]{1,0:T(8,128)(2,1)S(1)} %get-tuple-element.28), channel_id=1, source_target_pairs={{0,2},{1,3},{2,0},{3,1},{4,6},{5,7},{6,4},{7,5},{8,10},{9,11},{10,... | collective-permute-start | bytes 589832 | tf_op jit(solution)/shard_map/ppermute | solution.py:211
  64.1 13.9 %collective-permute-start.2 = (bf16[96,1024]{1,0:T(8,128)(2,1)S(1)}, bf16[96,1024]{1,0:T(8,128)(2,1)S(1)}, u32[]{:S(2)}, u32[]{:S(2)}) collective-permute-start(bf16[96,1024]{1,0:T(8,128)(2,1)S(1)} %get-tuple-element.29), channel_id=1, source_target_pairs={{0,3},{1,2},{2,1},{3,0},{4,7},{5,6},{6,5},{7,4},{8,11},{9,10},{10,... | collective-permute-start | bytes 589832 | tf_op jit(solution)/shard_map/ppermute | solution.py:211
  64.2 32.6 %collective-permute-start.6 = (bf16[96,1024]{1,0:T(8,128)(2,1)S(1)}, bf16[96,1024]{1,0:T(8,128)(2,1)S(1)}, u32[]{:S(2)}, u32[]{:S(2)}) collective-permute-start(bf16[96,1024]{1,0:T(8,128)(2,1)S(1)} %get-tuple-element.34), channel_id=1, source_target_pairs={{0,4},{1,5},{2,6},{3,7},{4,0},{5,1},{6,2},{7,3},{8,12},{9,13},{10,... | collective-permute-start | bytes 589832 | tf_op jit(solution)/shard_map/ppermute | solution.py:211
  73.5 23.7 %collective-permute-start.7 = (bf16[96,1024]{1,0:T(8,128)(2,1)S(1)}, bf16[96,1024]{1,0:T(8,128)(2,1)S(1)}, u32[]{:S(2)}, u32[]{:S(2)}) collective-permute-start(bf16[96,1024]{1,0:T(8,128)(2,1)S(1)} %get-tuple-element.35), channel_id=1, source_target_pairs={{0,5},{1,4},{2,7},{3,6},{4,1},{5,0},{6,3},{7,2},{8,13},{9,12},{10,... | collective-permute-start | bytes 589832 | tf_op jit(solution)/shard_map/ppermute | solution.py:211
  78.0 22.1 %collective-permute-start.10 = (bf16[96,1024]{1,0:T(8,128)(2,1)S(1)}, bf16[96,1024]{1,0:T(8,128)(2,1)S(1)}, u32[]{:S(2)}, u32[]{:S(2)}) collective-permute-start(bf16[96,1024]{1,0:T(8,128)(2,1)S(1)} %get-tuple-element.38), channel_id=1, source_target_pairs={{0,6},{1,7},{2,4},{3,5},{4,2},{5,3},{6,0},{7,1},{8,14},{9,15},{10,... | collective-permute-start | bytes 589832 | tf_op jit(solution)/shard_map/ppermute | solution.py:211
  95.6 9.1 %collective-permute-start.11 = (bf16[96,1024]{1,0:T(8,128)(2,1)S(1)}, bf16[96,1024]{1,0:T(8,128)(2,1)S(1)}, u32[]{:S(2)}, u32[]{:S(2)}) collective-permute-start(bf16[96,1024]{1,0:T(8,128)(2,1)S(1)} %get-tuple-element.39), channel_id=1, source_target_pairs={{0,7},{1,6},{2,5},{3,4},{4,3},{5,2},{6,1},{7,0},{8,15},{9,14},{10,... | collective-permute-start | bytes 589832 | tf_op jit(solution)/shard_map/ppermute | solution.py:211
  96.8 8.0 %collective-permute-start.3 = (bf16[96,1024]{1,0:T(8,128)(2,1)S(1)}, bf16[96,1024]{1,0:T(8,128)(2,1)S(1)}, u32[]{:S(2)}, u32[]{:S(2)}) collective-permute-start(bf16[96,1024]{1,0:T(8,128)(2,1)S(1)} %get-tuple-element.31), channel_id=1, source_target_pairs={{0,1},{1,0},{2,3},{3,2},{4,5},{5,4},{6,7},{7,6},{8,9},{9,8},{10,11... | collective-permute-start | bytes 589832 | tf_op jit(solution)/shard_map/ppermute | solution.py:211
  97.3 10.6 %collective-permute-start.4 = (bf16[96,1024]{1,0:T(8,128)(2,1)S(1)}, bf16[96,1024]{1,0:T(8,128)(2,1)S(1)}, u32[]{:S(2)}, u32[]{:S(2)}) collective-permute-start(bf16[96,1024]{1,0:T(8,128)(2,1)S(1)} %get-tuple-element.32), channel_id=1, source_target_pairs={{0,2},{1,3},{2,0},{3,1},{4,6},{5,7},{6,4},{7,5},{8,10},{9,11},{10,... | collective-permute-start | bytes 589832 | tf_op jit(solution)/shard_map/ppermute | solution.py:211
  97.3 23.6 %collective-permute-start.5 = (bf16[96,1024]{1,0:T(8,128)(2,1)S(1)}, bf16[96,1024]{1,0:T(8,128)(2,1)S(1)}, u32[]{:S(2)}, u32[]{:S(2)}) collective-permute-start(bf16[96,1024]{1,0:T(8,128)(2,1)S(1)} %get-tuple-element.33), channel_id=1, source_target_pairs={{0,3},{1,2},{2,1},{3,0},{4,7},{5,6},{6,5},{7,4},{8,11},{9,10},{10,... | collective-permute-start | bytes 589832 | tf_op jit(solution)/shard_map/ppermute | solution.py:211
  100.1 71.8 %collective-permute-start.19 = (bf16[2304,256]{1,0:T(8,128)(2,1)S(1)}, bf16[2304,256]{1,0:T(8,128)(2,1)S(1)}, u32[]{:S(2)}, u32[]{:S(2)}) collective-permute-start(bf16[2304,256]{1,0:T(8,128)(2,1)S(1)} %assemble.1.refs_0_), channel_id=1, source_target_pairs={{0,1},{1,0},{2,3},{3,2},{4,5},{5,4},{6,7},{7,6},{8,9},{9,8},{10,11... | collective-permute-start | bytes 3538952 | tf_op jit(solution)/shard_map/ppermute | solution.py:211
  104.7 67.2 %collective-permute-start.21 = (bf16[2304,256]{1,0:T(8,128)(2,1)}, bf16[2304,256]{1,0:T(8,128)(2,1)S(1)}, u32[]{:S(2)}, u32[]{:S(2)}) collective-permute-start(bf16[2304,256]{1,0:T(8,128)(2,1)} %collective-permute-done.20.refs_2_), channel_id=1, source_target_pairs={{0,1},{1,0},{2,3},{3,2},{4,5},{5,4},{6,7},{7,6},{8,9},{9,8},{10,11... | collective-permute-start | bytes 3538952 | tf_op jit(solution)/shard_map/ppermute | solution.py:211
  104.8 67.1 %collective-permute-start.23 = (bf16[2304,256]{1,0:T(8,128)(2,1)S(1)}, bf16[2304,256]{1,0:T(8,128)(2,1)S(1)}, u32[]{:S(2)}, u32[]{:S(2)}) collective-permute-start(bf16[2304,256]{1,0:T(8,128)(2,1)S(1)} %collective-permute-done.22.refs_4_), channel_id=1, source_target_pairs={{0,1},{1,0},{2,3},{3,2},{4,5},{5,4},{6,7},{7,6},{8,9},{9,8},{10,11... | collective-permute-start | bytes 3538952 | tf_op jit(solution)/shard_map/ppermute | solution.py:211
  107.8 64.1 %collective-permute-start.26 = (bf16[2304,256]{1,0:T(8,128)(2,1)S(1)}, bf16[2304,256]{1,0:T(8,128)(2,1)S(1)}, u32[]{:S(2)}, u32[]{:S(2)}) collective-permute-start(bf16[2304,256]{1,0:T(8,128)(2,1)S(1)} %constant_dynamic-update-slice_fusion.refs_6_), channel_id=1, source_target_pairs={{0,1},{1,0},{2,3},{3,2},{4,5},{5,4},{6,7},{7,6},{8,9},{9,8},{10,11... | collective-permute-start | bytes 3538952 | tf_op jit(solution)/shard_map/ppermute | solution.py:211
  120.9 11.0 %collective-permute-start.8 = (bf16[96,1024]{1,0:T(8,128)(2,1)S(1)}, bf16[96,1024]{1,0:T(8,128)(2,1)S(1)}, u32[]{:S(2)}, u32[]{:S(2)}) collective-permute-start(bf16[96,1024]{1,0:T(8,128)(2,1)S(1)} %get-tuple-element.36), channel_id=1, source_target_pairs={{0,4},{1,5},{2,6},{3,7},{4,0},{5,1},{6,2},{7,3},{8,12},{9,13},{10,... | collective-permute-start | bytes 589832 | tf_op jit(solution)/shard_map/ppermute | solution.py:211
  131.9 22.6 %slice-start = ((s8[8388608]{0:T(1024)(128)(4,1)}), s8[4194304]{0:T(1024)(128)(4,1)S(1)}, s32[]{:S(2)}) async-start(s8[8388608]{0:T(1024)(128)(4,1)} %bitcast.18), calls=%async_computation | async-start | bytes 8388608
  131.9 22.6 %slice-start.1 = ((s8[8388608]{0:T(1024)(128)(4,1)}), s8[4194304]{0:T(1024)(128)(4,1)S(1)}, s32[]{:S(2)}) async-start(s8[8388608]{0:T(1024)(128)(4,1)} %bitcast.18), calls=%async_computation.1 | async-start | bytes 8388608
  131.9 10.1 %collective-permute-start.9 = (bf16[96,1024]{1,0:T(8,128)(2,1)S(1)}, bf16[96,1024]{1,0:T(8,128)(2,1)S(1)}, u32[]{:S(2)}, u32[]{:S(2)}) collective-permute-start(bf16[96,1024]{1,0:T(8,128)(2,1)S(1)} %get-tuple-element.37), channel_id=1, source_target_pairs={{0,5},{1,4},{2,7},{3,6},{4,1},{5,0},{6,3},{7,2},{8,13},{9,12},{10,... | collective-permute-start | bytes 589832 | tf_op jit(solution)/shard_map/ppermute | solution.py:211
  142.0 7.9 %collective-permute-start.12 = (bf16[96,1024]{1,0:T(8,128)(2,1)S(1)}, bf16[96,1024]{1,0:T(8,128)(2,1)S(1)}, u32[]{:S(2)}, u32[]{:S(2)}) collective-permute-start(bf16[96,1024]{1,0:T(8,128)(2,1)S(1)} %get-tuple-element.40), channel_id=1, source_target_pairs={{0,6},{1,7},{2,4},{3,5},{4,2},{5,3},{6,0},{7,1},{8,14},{9,15},{10,... | collective-permute-start | bytes 589832 | tf_op jit(solution)/shard_map/ppermute | solution.py:211
  149.9 9.7 %collective-permute-start.13 = (bf16[96,1024]{1,0:T(8,128)(2,1)S(1)}, bf16[96,1024]{1,0:T(8,128)(2,1)S(1)}, u32[]{:S(2)}, u32[]{:S(2)}) collective-permute-start(bf16[96,1024]{1,0:T(8,128)(2,1)S(1)} %get-tuple-element.41), channel_id=1, source_target_pairs={{0,7},{1,6},{2,5},{3,4},{4,3},{5,2},{6,1},{7,0},{8,15},{9,14},{10,... | collective-permute-start | bytes 589832 | tf_op jit(solution)/shard_map/ppermute | solution.py:211
  161.3 1.6 collective-permute-start.14
  162.9 9.0 %collective-permute-start.15 = (bf16[64,1024]{1,0:T(8,128)(2,1)S(1)}, bf16[64,1024]{1,0:T(8,128)(2,1)S(1)}, u32[]{:S(2)}, u32[]{:S(2)}) collective-permute-start(bf16[64,1024]{1,0:T(8,128)(2,1)S(1)} %get-tuple-element.44), channel_id=1, source_target_pairs={{1,2},{3,4},{5,6},{2,1},{4,3},{6,5},{9,10},{11,12},{13,14},{10,9},... | collective-permute-start | bytes 393224 | tf_op jit(solution)/shard_map/ppermute | solution.py:258
  (5 other events, 18.0 us)

commit v3 on v2

--- a/solution.py
+++ b/solution.py
@@ -11,7 +11,7 @@
 VM = pl.BlockSpec(memory_space=pltpu.VMEM)
 SM = pl.BlockSpec(memory_space=pltpu.SMEM)
 ANY = pl.BlockSpec(memory_space=pl.ANY)
-PARAMS = pltpu.CompilerParams(vmem_limit_bytes=24 * 2**20)
+PARAMS = pltpu.CompilerParams(vmem_limit_bytes=10 * 2**20)
 
 
 def prologue(tok, cells, experts, cap):
@@ -84,7 +84,7 @@
     return pl.pallas_call(
         kernel, in_specs=[VM] * n + [ANY if stream else VM] * 2, out_specs=[VM] * n,
         out_shape=[jax.ShapeDtypeStruct((cap, width), BF16)] * n, scratch_shapes=scratch,
-        compiler_params=pltpu.CompilerParams(vmem_limit_bytes=(32 if stream else 14) * 2**20),
+        compiler_params=pltpu.CompilerParams(vmem_limit_bytes=(32 if stream else 9) * 2**20),
     )(*blocks, w_in, w_out)
 
 
@@ -159,10 +159,7 @@
     n = cols // lanes
 
     def kernel(place_ref, mixed_ref, inner_ref, outer_ref, *refs):
-        weights, (out, x_scr, w_scr, sems) = refs[: 2 * quarters], refs[2 * quarters :]
-        copies = [pltpu.make_async_copy(w, w_scr.at[i], sems.at[i]) for i, w in enumerate(weights)]
-        for c in copies:
-            c.start()
+        weights, (out, x_scr) = refs[: 2 * quarters], refs[2 * quarters :]
         first = place_ref[2] == 0
         top = jnp.where(first, outer_ref[...], inner_ref[...])
         bottom = jnp.where(first, inner_ref[...], outer_ref[...])
@@ -175,13 +172,12 @@
         for k in range(quarters):
             for r in range(2):
                 i = 2 * k + r
-                copies[i].wait()
                 for a in range(3):
                     x = x_scr[place_ref[1] ^ k, a * edge : a * edge + count, :]
                     for b in range(3):
                         t = 3 * a + b
                         accs[r][b] += jnp.dot(
-                            x, w_scr[i, t * chans : (t + 1) * chans, :], preferred_element_type=F32
+                            x, weights[i][t * chans : (t + 1) * chans, :], preferred_element_type=F32
                         )
         halves = []
         for r in range(2):
@@ -197,13 +193,9 @@
     weights = [w for pair in zip(mine, theirs) for w in pair]
     return pl.pallas_call(
         kernel, out_shape=jax.ShapeDtypeStruct((count, 2 * cols), BF16),
-        in_specs=[SM, VM, VM, VM] + [ANY] * (2 * quarters), out_specs=VM,
-        scratch_shapes=[
-            pltpu.VMEM((quarters, count + 2 * edge, chans), BF16),
-            pltpu.VMEM((2 * quarters, 9 * chans, cols), BF16),
-            pltpu.SemaphoreType.DMA((2 * quarters,)),
-        ],
-        compiler_params=PARAMS, name="conv",
+        in_specs=[SM, VM, VM, VM] + [VM] * (2 * quarters), out_specs=VM,
+        scratch_shapes=[pltpu.VMEM((quarters, count + 2 * edge, chans), BF16)],
+        compiler_params=pltpu.CompilerParams(vmem_limit_bytes=9 * 2**20), name="conv",
     )(place, mixed, inner, outer, *weights)
 
 
@@ -244,6 +236,7 @@
     routes = route_ids.reshape(count, 2)
     cells = (routes ^ me) * cap + slot_ids.reshape(count, 2)
     normed, blocks = prologue(tok, cells.T, experts, cap)
+    conv_weight, normed = lax.optimization_barrier((conv_weight, normed))
     received = [blocks[0]] + [flip(blocks[k], "expert", k) for k in range(1, experts)]
     mine, theirs = gather_filters(conv_weight, place)
     logits = jnp.dot(normed.astype(F32), router, precision=lax.Precision.HIGHEST)

time: 180 us -> 175 us (0.972)
  local copies, waits for them, and re-layouts: 20.2 us -> 17.1 us
  Pallas kernels: 27.4 us -> 24.5 us
    pallas_call x1, Pallas kernels: 7.01 us -> 4.03 us  [conv(): pl.pallas_call(kernel, out_shape=jax.ShapeDtypeStruct((count, 2 * cols),...]
    slice x2, local copies, waits for them, and re-layouts: 2.79 us -> 0.08 us  [gather_filters(): across = [flip(y[:half], 'dp', 1), flip(x[half:], 'dp', 2)]]
    ppermute x26, waiting for transfers between devices: 81.7 us -> 83.5 us  [flip(): lax.ppermute(value, axis, [(i, i ^ k) for i in range(lax.axis_size(axis))])]
    unnamed x24 -> x31, local copies, waits for them, and re-layouts: 16.2 us -> 16.6 us
  transfers between devices with their start and end apart: 27 -> 27, of which waited for: 13 -> 13; matrix products, arithmetic and copies ran while one was open for 3% -> 0% of each run, Pallas kernels for 11% -> 10%
where the time goes in v3:
time: 175 us; the launch traced here: 174 us
  waiting for transfers between devices  86.1 us (49%)
  starting transfers between devices  45.6 us (26%)
  Pallas kernels  24.5 us (14%)
  local copies, waits for them, and re-layouts  17.1 us (10%)
    ppermute x26, waiting for transfers between devices, flip(): lax.ppermute(value, axis, [(i, i ^ k) for i in range(lax.axis_size(axis))])  83.5 us
    ppermute x26, starting transfers between devices, flip(): lax.ppermute(value, axis, [(i, i ^ k) for i in range(lax.axis_size(axis))])  39.5 us
    unnamed x31, local copies, waits for them, and re-layouts  16.6 us
    pallas_call x3, Pallas kernels, mlp(): pl.pallas_call(kernel, in_specs=[VM] * n + [ANY if stream else VM] * 2, o...  16.1 us
    ppermute x1, starting transfers between devices, shards(): outer = lax.ppermute(outer, 'expert', joints + [(j, i) for i, j in joints])  6.13 us
    pallas_call x1, Pallas kernels, conv(): pl.pallas_call(kernel, out_shape=jax.ShapeDtypeStruct((count, 2 * cols),...  4.03 us
  transfers between devices with their start and end apart: 27, of which 13 were waited for; matrix products, arithmetic and copies ran while one was open for 0% of the time, Pallas kernels for 10%

profile of v3, /device:TPU:1, one launch (start us, length us, event | category | flops | bytes accessed | tf_op | source)
XLA Modules:
  0.0 174.4 jit_solution(5587454666151210820)
XLA Ops:
  4.8 3.2 %collective-permute-start.17 = (bf16[1152,128]{1,0:T(8,128)(2,1)S(1)}, bf16[1152,128]{1,0:T(8,128)(2,1)S(1)}, u32[]{:S(2)}, u32[]{:S(2)}) collective-permute-start(bf16[1152,128]{1,0:T(8,128)(2,1)S(1)} %pad_maximum_fusion.refs_0_), channel_id=1, source_target_pairs={{0,4},{1,5},{2,6},{3,7},{4,0},{5,1},{6,2},{7,3},{8,12},{9,13},{10,... | collective-permute-start | bytes 884744 | tf_op jit(solution)/shard_map/ppermute | solution.py:203
  9.3 11.8 %collective-permute-done.17.refs_2_ = bf16[1152,128]{1,0:T(8,128)(2,1)S(1)} collective-permute-done((bf16[1152,128]{1,0:T(8,128)(2,1)S(1)}, bf16[1152,128]{1,0:T(8,128)(2,1)S(1)}, u32[]{:S(2)}, u32[]{:S(2)}) %collective-permute-start.17) | collective-permute-done | bytes 294944 | tf_op jit(solution)/shard_map/ppermute | solution.py:203
  22.3 6.0 %collective-permute-done.18.refs_3_ = bf16[1152,128]{1,0:T(8,128)(2,1)S(1)} collective-permute-done((bf16[1152,128]{1,0:T(8,128)(2,1)S(1)}, bf16[1152,128]{1,0:T(8,128)(2,1)S(1)}, u32[]{:S(2)}, u32[]{:S(2)}) %collective-permute-start.18) | collective-permute-done | bytes 294944 | tf_op jit(solution)/shard_map/ppermute | solution.py:203
  31.9 23.1 %collective-permute-done.22.refs_4_ = bf16[2304,256]{1,0:T(8,128)(2,1)S(1)} collective-permute-done((bf16[2304,256]{1,0:T(8,128)(2,1)S(1)}, bf16[2304,256]{1,0:T(8,128)(2,1)S(1)}, u32[]{:S(2)}, u32[]{:S(2)}) %collective-permute-start.22) | collective-permute-done | bytes 1179680 | tf_op jit(solution)/shard_map/ppermute | solution.py:203
  57.5 3.6 %collective-permute-start = (bf16[96,1024]{1,0:T(8,128)(2,1)S(1)}, bf16[96,1024]{1,0:T(8,128)(2,1)S(1)}, u32[]{:S(2)}, u32[]{:S(2)}) collective-permute-start(bf16[96,1024]{1,0:T(8,128)(2,1)S(1)} %copy-done.8), channel_id=1, source_target_pairs={{0,1},{1,0},{2,3},{3,2},{4,5},{5,4},{6,7},{7,6},{8,9},{9,8},{10,11... | collective-permute-start | bytes 589832 | tf_op jit(solution)/shard_map/ppermute | solution.py:203
  61.1 2.2 %collective-permute-start.1 = (bf16[96,1024]{1,0:T(8,128)(2,1)S(1)}, bf16[96,1024]{1,0:T(8,128)(2,1)S(1)}, u32[]{:S(2)}, u32[]{:S(2)}) collective-permute-start(bf16[96,1024]{1,0:T(8,128)(2,1)S(1)} %get-tuple-element.31), channel_id=1, source_target_pairs={{0,2},{1,3},{2,0},{3,1},{4,6},{5,7},{6,4},{7,5},{8,10},{9,11},{10,... | collective-permute-start | bytes 589832 | tf_op jit(solution)/shard_map/ppermute | solution.py:203
  63.3 3.5 %collective-permute-start.6 = (bf16[96,1024]{1,0:T(8,128)(2,1)S(1)}, bf16[96,1024]{1,0:T(8,128)(2,1)S(1)}, u32[]{:S(2)}, u32[]{:S(2)}) collective-permute-start(bf16[96,1024]{1,0:T(8,128)(2,1)S(1)} %get-tuple-element.37), channel_id=1, source_target_pairs={{0,4},{1,5},{2,6},{3,7},{4,0},{5,1},{6,2},{7,3},{8,12},{9,13},{10,... | collective-permute-start | bytes 589832 | tf_op jit(solution)/shard_map/ppermute | solution.py:203
  66.8 5.9 %collective-permute-done.1.refs_2_ = bf16[96,1024]{1,0:T(8,128)(2,1)S(1)} collective-permute-done((bf16[96,1024]{1,0:T(8,128)(2,1)S(1)}, bf16[96,1024]{1,0:T(8,128)(2,1)S(1)}, u32[]{:S(2)}, u32[]{:S(2)}) %collective-permute-start.1) | collective-permute-done | bytes 196640 | tf_op jit(solution)/shard_map/ppermute | solution.py:203
  72.7 3.3 %collective-permute-start.7 = (bf16[96,1024]{1,0:T(8,128)(2,1)S(1)}, bf16[96,1024]{1,0:T(8,128)(2,1)S(1)}, u32[]{:S(2)}, u32[]{:S(2)}) collective-permute-start(bf16[96,1024]{1,0:T(8,128)(2,1)S(1)} %get-tuple-element.38), channel_id=1, source_target_pairs={{0,5},{1,4},{2,7},{3,6},{4,1},{5,0},{6,3},{7,2},{8,13},{9,12},{10,... | collective-permute-start | bytes 589832 | tf_op jit(solution)/shard_map/ppermute | solution.py:203
  77.2 4.0 %collective-permute-start.10 = (bf16[96,1024]{1,0:T(8,128)(2,1)S(1)}, bf16[96,1024]{1,0:T(8,128)(2,1)S(1)}, u32[]{:S(2)}, u32[]{:S(2)}) collective-permute-start(bf16[96,1024]{1,0:T(8,128)(2,1)S(1)} %get-tuple-element.41), channel_id=1, source_target_pairs={{0,6},{1,7},{2,4},{3,5},{4,2},{5,3},{6,0},{7,1},{8,14},{9,15},{10,... | collective-permute-start | bytes 589832 | tf_op jit(solution)/shard_map/ppermute | solution.py:203
  81.2 3.4 %copy-done.1 = bf16[1,4096,1024]{2,1,0:T(8,128)(2,1)S(1)} copy-done((bf16[1,4096,1024]{2,1,0:T(8,128)(2,1)S(1)}, bf16[1,4096,1024]{2,1,0:T(8,128)(2,1)}, u32[]{:S(2)}) %copy-start.1) | copy-done | bytes 8388632
  84.6 3.4 %copy-done.3 = bf16[1,4096,1024]{2,1,0:T(8,128)(2,1)S(1)} copy-done((bf16[1,4096,1024]{2,1,0:T(8,128)(2,1)S(1)}, bf16[1,4096,1024]{2,1,0:T(8,128)(2,1)}, u32[]{:S(2)}) %copy-start.3) | copy-done | bytes 8388632
  87.9 6.8 %shard_map.73 = (bf16[96,1024]{1,0:T(8,128)(2,1)S(1)}, bf16[96,1024]{1,0:T(8,128)(2,1)S(1)}, bf16[96,1024]{1,0:T(8,128)(2,1)S(1)}, bf16[96,1024]{1,0:T(8,128)(2,1)S(1)}) custom-call(bf16[96,1024]{1,0:T(8,128)(2,1)S(1)} %get-tuple-element.29.refs_0_, bf16[96,1024]{1,0:T(8,128)(2,1)S(1)} %collective-permute-done.refs_1_, ...), custom_call_target="tpu_custom_call" | custom-call | tf_op jit(solution)/shard_map/pallas_call | solution.py:84
  95.4 1.7 collective-permute-start.5
  97.4 6.5 %collective-permute-done.11.refs_1_ = bf16[96,1024]{1,0:T(8,128)(2,1)S(1)} collective-permute-done((bf16[96,1024]{1,0:T(8,128)(2,1)S(1)}, bf16[96,1024]{1,0:T(8,128)(2,1)S(1)}, u32[]{:S(2)}, u32[]{:S(2)}) %collective-permute-start.11) | collective-permute-done | bytes 196640 | tf_op jit(solution)/shard_map/ppermute | solution.py:203
  104.4 1.6 collective-permute-done.4.refs_2_
  106.0 1.5 collective-permute-start.26
  107.5 3.4 %copy-done.2 = bf16[1,4096,1024]{2,1,0:T(8,128)(2,1)S(1)} copy-done((bf16[1,4096,1024]{2,1,0:T(8,128)(2,1)S(1)}, bf16[1,4096,1024]{2,1,0:T(8,128)(2,1)}, u32[]{:S(2)}) %copy-start.2) | copy-done | bytes 8388632
  110.9 3.4 %copy-done.4 = bf16[1,4096,1024]{2,1,0:T(8,128)(2,1)S(1)} copy-done((bf16[1,4096,1024]{2,1,0:T(8,128)(2,1)S(1)}, bf16[1,4096,1024]{2,1,0:T(8,128)(2,1)}, u32[]{:S(2)}) %copy-start.4) | copy-done | bytes 8388632
  114.2 4.8 %shard_map.74 = (bf16[96,1024]{1,0:T(8,128)(2,1)S(1)}, bf16[96,1024]{1,0:T(8,128)(2,1)S(1)}) custom-call(bf16[96,1024]{1,0:T(8,128)(2,1)S(1)} %collective-permute-done.6.refs_0_, bf16[96,1024]{1,0:T(8,128)(2,1)S(1)} %collective-permute-done.7.refs_1_, bf16[4096,1024]{1,0:T(8,128)(2,1)S(1)} %bitcast.16, bf16[4096,1024]{1,0:T(8,128)(2,1)S(1)} %bitcast.22), custom_call_target="tpu_custom_call" | custom-call | tf_op jit(solution)/shard_map/pallas_call | solution.py:84
  119.0 1.6 collective-permute-start.8
  120.6 9.7 %collective-permute-done.8.refs_4_ = bf16[96,1024]{1,0:T(8,128)(2,1)S(1)} collective-permute-done((bf16[96,1024]{1,0:T(8,128)(2,1)S(1)}, bf16[96,1024]{1,0:T(8,128)(2,1)S(1)}, u32[]{:S(2)}, u32[]{:S(2)}) %collective-permute-start.8) | collective-permute-done | bytes 196640 | tf_op jit(solution)/shard_map/ppermute | solution.py:203
  130.3 4.6 %shard_map.75 = (bf16[96,1024]{1,0:T(8,128)(2,1)S(1)}, bf16[96,1024]{1,0:T(8,128)(2,1)S(1)}) custom-call(bf16[96,1024]{1,0:T(8,128)(2,1)S(1)} %collective-permute-done.10.refs_0_, bf16[96,1024]{1,0:T(8,128)(2,1)S(1)} %collective-permute-done.11.refs_1_, bf16[4096,1024]{1,0:T(8,128)(2,1)S(1)} %bitcast.17, bf16[4096,1024]{1,0:T(8,128)(2,1)S(1)} %bitcast.23), custom_call_target="tpu_custom_call" | custom-call | tf_op jit(solution)/shard_map/pallas_call | solution.py:84
  134.9 6.3 %collective-permute-done.9.refs_5_ = bf16[96,1024]{1,0:T(8,128)(2,1)S(1)} collective-permute-done((bf16[96,1024]{1,0:T(8,128)(2,1)S(1)}, bf16[96,1024]{1,0:T(8,128)(2,1)S(1)}, u32[]{:S(2)}, u32[]{:S(2)}) %collective-permute-start.9) | collective-permute-done | bytes 196640 | tf_op jit(solution)/shard_map/ppermute | solution.py:203
  141.2 2.0 %collective-permute-start.12 = (bf16[96,1024]{1,0:T(8,128)(2,1)S(1)}, bf16[96,1024]{1,0:T(8,128)(2,1)S(1)}, u32[]{:S(2)}, u32[]{:S(2)}) collective-permute-start(bf16[96,1024]{1,0:T(8,128)(2,1)S(1)} %get-tuple-element.43), channel_id=1, source_target_pairs={{0,6},{1,7},{2,4},{3,5},{4,2},{5,3},{6,0},{7,1},{8,14},{9,15},{10,... | collective-permute-start | bytes 589832 | tf_op jit(solution)/shard_map/ppermute | solution.py:203
  143.2 5.9 %collective-permute-done.12.refs_6_ = bf16[96,1024]{1,0:T(8,128)(2,1)S(1)} collective-permute-done((bf16[96,1024]{1,0:T(8,128)(2,1)S(1)}, bf16[96,1024]{1,0:T(8,128)(2,1)S(1)}, u32[]{:S(2)}, u32[]{:S(2)}) %collective-permute-start.12) | collective-permute-done | bytes 196640 | tf_op jit(solution)/shard_map/ppermute | solution.py:203
  149.1 3.2 %collective-permute-start.13 = (bf16[96,1024]{1,0:T(8,128)(2,1)S(1)}, bf16[96,1024]{1,0:T(8,128)(2,1)S(1)}, u32[]{:S(2)}, u32[]{:S(2)}) collective-permute-start(bf16[96,1024]{1,0:T(8,128)(2,1)S(1)} %get-tuple-element.44), channel_id=1, source_target_pairs={{0,7},{1,6},{2,5},{3,4},{4,3},{5,2},{6,1},{7,0},{8,15},{9,14},{10,... | collective-permute-start | bytes 589832 | tf_op jit(solution)/shard_map/ppermute | solution.py:203
  153.3 4.5 %collective-permute-done.13.refs_7_ = bf16[96,1024]{1,0:T(8,128)(2,1)S(1)} collective-permute-done((bf16[96,1024]{1,0:T(8,128)(2,1)S(1)}, bf16[96,1024]{1,0:T(8,128)(2,1)S(1)}, u32[]{:S(2)}, u32[]{:S(2)}) %collective-permute-start.13) | collective-permute-done | bytes 196640 | tf_op jit(solution)/shard_map/ppermute | solution.py:203
  157.8 1.6 combine.1
  161.6 6.1 %collective-permute-start.15 = (bf16[64,1024]{1,0:T(8,128)(2,1)S(1)}, bf16[64,1024]{1,0:T(8,128)(2,1)S(1)}, u32[]{:S(2)}, u32[]{:S(2)}) collective-permute-start(bf16[64,1024]{1,0:T(8,128)(2,1)S(1)} %get-tuple-element.47), channel_id=1, source_target_pairs={{1,2},{3,4},{5,6},{2,1},{4,3},{6,5},{9,10},{11,12},{13,14},{10,9},... | collective-permute-start | bytes 393224 | tf_op jit(solution)/shard_map/ppermute | solution.py:251
  167.7 2.6 %collective-permute-done.15.outer_ref = bf16[64,1024]{1,0:T(8,128)(2,1)S(1)} collective-permute-done((bf16[64,1024]{1,0:T(8,128)(2,1)S(1)}, bf16[64,1024]{1,0:T(8,128)(2,1)S(1)}, u32[]{:S(2)}, u32[]{:S(2)}) %collective-permute-start.15) | collective-permute-done | bytes 131104 | tf_op jit(solution)/shard_map/ppermute | solution.py:251
  170.4 4.0 %conv.1 = bf16[256,512]{1,0:T(8,128)(2,1)} custom-call(s32[3]{0:T(128)S(1)} %pad_add_fusion.place_ref, bf16[256,1024]{1,0:T(8,128)(2,1)S(1)} %get-tuple-element.45.mixed_ref, bf16[64,1024]{1,0:T(8,128)(2,1)S(1)} %collective-permute-done.14.inner_ref, bf16[64,1024]{1,0:T(8,128)(2,1)S(1)} %collective-permute-done.15.outer_ref, ...), custom_call_target="tpu_custom_call" | custom-call | tf_op jit(solution)/shard_map/conv/pallas_call | solution.py:194
  (73 shorter events, 18.8 us)
Async XLA Ops:
  0.0 152.3 %copy-start = (f32[1024,8]{0,1:T(8,128)S(1)}, f32[1024,8]{0,1:T(8,128)}, u32[]{:S(2)}) copy-start(f32[1024,8]{0,1:T(8,128)} %param.10) | copy-start | bytes 98308
  4.8 16.3 %collective-permute-start.17 = (bf16[1152,128]{1,0:T(8,128)(2,1)S(1)}, bf16[1152,128]{1,0:T(8,128)(2,1)S(1)}, u32[]{:S(2)}, u32[]{:S(2)}) collective-permute-start(bf16[1152,128]{1,0:T(8,128)(2,1)S(1)} %pad_maximum_fusion.refs_0_), channel_id=1, source_target_pairs={{0,4},{1,5},{2,6},{3,7},{4,0},{5,1},{6,2},{7,3},{8,12},{9,13},{10,... | collective-permute-start | bytes 884744 | tf_op jit(solution)/shard_map/ppermute | solution.py:203
  8.0 14.3 %collective-permute-start.16 = (bf16[1152,128]{1,0:T(8,128)(2,1)S(1)}, bf16[1152,128]{1,0:T(8,128)(2,1)S(1)}, u32[]{:S(2)}, u32[]{:S(2)}) collective-permute-start(bf16[1152,128]{1,0:T(8,128)(2,1)S(1)} %pad_maximum_fusion.refs_0_), channel_id=1, source_target_pairs={{0,2},{1,3},{2,0},{3,1},{4,6},{5,7},{6,4},{7,5},{8,10},{9,11},{10,... | collective-permute-start | bytes 884744 | tf_op jit(solution)/shard_map/ppermute | solution.py:203
  21.0 7.3 %collective-permute-start.18 = (bf16[1152,128]{1,0:T(8,128)(2,1)S(1)}, bf16[1152,128]{1,0:T(8,128)(2,1)S(1)}, u32[]{:S(2)}, u32[]{:S(2)}) collective-permute-start(bf16[1152,128]{1,0:T(8,128)(2,1)S(1)} %collective-permute-done.17.refs_2_), channel_id=1, source_target_pairs={{0,2},{1,3},{2,0},{3,1},{4,6},{5,7},{6,4},{7,5},{8,10},{9,11},{10,... | collective-permute-start | bytes 884744 | tf_op jit(solution)/shard_map/ppermute | solution.py:203
  29.6 27.9 %copy-start.8 = (bf16[96,1024]{1,0:T(8,128)(2,1)S(1)}, bf16[96,1024]{1,0:T(8,128)(2,1)}, u32[]{:S(2)}) copy-start(bf16[96,1024]{1,0:T(8,128)(2,1)} %copy-done.7) | copy-start | bytes 589828
  29.6 25.4 %collective-permute-start.22 = (bf16[2304,256]{1,0:T(8,128)(2,1)S(1)}, bf16[2304,256]{1,0:T(8,128)(2,1)S(1)}, u32[]{:S(2)}, u32[]{:S(2)}) collective-permute-start(bf16[2304,256]{1,0:T(8,128)(2,1)S(1)} %assemble.1.refs_0_), channel_id=1, source_target_pairs={{0,16},{8,24},{16,0},{24,8},{1,17},{9,25},{17,1},{25,9},{2,18},{10... | collective-permute-start | bytes 3538952 | tf_op jit(solution)/shard_map/ppermute | solution.py:203
  30.7 25.4 %collective-permute-start.20 = (bf16[2304,256]{1,0:T(8,128)(2,1)S(1)}, bf16[2304,256]{1,0:T(8,128)(2,1)S(1)}, u32[]{:S(2)}, u32[]{:S(2)}) collective-permute-start(bf16[2304,256]{1,0:T(8,128)(2,1)S(1)} %assemble.1.refs_0_), channel_id=1, source_target_pairs={{0,8},{8,0},{16,24},{24,16},{1,9},{9,1},{17,25},{25,17},{2,10},{10... | collective-permute-start | bytes 3538952 | tf_op jit(solution)/shard_map/ppermute | solution.py:203
  55.1 39.6 %collective-permute-start.24 = (bf16[1152,256]{1,0:T(8,128)(2,1)S(1)}, bf16[1152,256]{1,0:T(8,128)(2,1)S(1)}, u32[]{:S(2)}, u32[]{:S(2)}) collective-permute-start(bf16[1152,256]{1,0:T(8,128)(2,1)S(1)} %slice.18), channel_id=1, source_target_pairs={{0,8},{8,0},{16,24},{24,16},{1,9},{9,1},{17,25},{25,17},{2,10},{10... | collective-permute-start | bytes 1769480 | tf_op jit(solution)/shard_map/ppermute | solution.py:203
  56.1 39.3 %collective-permute-start.25 = (bf16[1152,256]{1,0:T(8,128)(2,1)S(1)}, bf16[1152,256]{1,0:T(8,128)(2,1)S(1)}, u32[]{:S(2)}, u32[]{:S(2)}) collective-permute-start(bf16[1152,256]{1,0:T(8,128)(2,1)S(1)} %slice.19), channel_id=1, source_target_pairs={{0,16},{8,24},{16,0},{24,8},{1,17},{9,25},{17,1},{25,9},{2,18},{10... | collective-permute-start | bytes 1769480 | tf_op jit(solution)/shard_map/ppermute | solution.py:203
  57.5 5.8 %collective-permute-start = (bf16[96,1024]{1,0:T(8,128)(2,1)S(1)}, bf16[96,1024]{1,0:T(8,128)(2,1)S(1)}, u32[]{:S(2)}, u32[]{:S(2)}) collective-permute-start(bf16[96,1024]{1,0:T(8,128)(2,1)S(1)} %copy-done.8), channel_id=1, source_target_pairs={{0,1},{1,0},{2,3},{3,2},{4,5},{5,4},{6,7},{7,6},{8,9},{9,8},{10,11... | collective-permute-start | bytes 589832 | tf_op jit(solution)/shard_map/ppermute | solution.py:203
  61.1 11.7 %collective-permute-start.1 = (bf16[96,1024]{1,0:T(8,128)(2,1)S(1)}, bf16[96,1024]{1,0:T(8,128)(2,1)S(1)}, u32[]{:S(2)}, u32[]{:S(2)}) collective-permute-start(bf16[96,1024]{1,0:T(8,128)(2,1)S(1)} %get-tuple-element.31), channel_id=1, source_target_pairs={{0,2},{1,3},{2,0},{3,1},{4,6},{5,7},{6,4},{7,5},{8,10},{9,11},{10,... | collective-permute-start | bytes 589832 | tf_op jit(solution)/shard_map/ppermute | solution.py:203
  63.3 13.9 %collective-permute-start.2 = (bf16[96,1024]{1,0:T(8,128)(2,1)S(1)}, bf16[96,1024]{1,0:T(8,128)(2,1)S(1)}, u32[]{:S(2)}, u32[]{:S(2)}) collective-permute-start(bf16[96,1024]{1,0:T(8,128)(2,1)S(1)} %get-tuple-element.32), channel_id=1, source_target_pairs={{0,3},{1,2},{2,1},{3,0},{4,7},{5,6},{6,5},{7,4},{8,11},{9,10},{10,... | collective-permute-start | bytes 589832 | tf_op jit(solution)/shard_map/ppermute | solution.py:203
  63.3 31.6 %collective-permute-start.6 = (bf16[96,1024]{1,0:T(8,128)(2,1)S(1)}, bf16[96,1024]{1,0:T(8,128)(2,1)S(1)}, u32[]{:S(2)}, u32[]{:S(2)}) collective-permute-start(bf16[96,1024]{1,0:T(8,128)(2,1)S(1)} %get-tuple-element.37), channel_id=1, source_target_pairs={{0,4},{1,5},{2,6},{3,7},{4,0},{5,1},{6,2},{7,3},{8,12},{9,13},{10,... | collective-permute-start | bytes 589832 | tf_op jit(solution)/shard_map/ppermute | solution.py:203
  72.7 22.6 %collective-permute-start.7 = (bf16[96,1024]{1,0:T(8,128)(2,1)S(1)}, bf16[96,1024]{1,0:T(8,128)(2,1)S(1)}, u32[]{:S(2)}, u32[]{:S(2)}) collective-permute-start(bf16[96,1024]{1,0:T(8,128)(2,1)S(1)} %get-tuple-element.38), channel_id=1, source_target_pairs={{0,5},{1,4},{2,7},{3,6},{4,1},{5,0},{6,3},{7,2},{8,13},{9,12},{10,... | collective-permute-start | bytes 589832 | tf_op jit(solution)/shard_map/ppermute | solution.py:203
  77.2 20.0 %collective-permute-start.10 = (bf16[96,1024]{1,0:T(8,128)(2,1)S(1)}, bf16[96,1024]{1,0:T(8,128)(2,1)S(1)}, u32[]{:S(2)}, u32[]{:S(2)}) collective-permute-start(bf16[96,1024]{1,0:T(8,128)(2,1)S(1)} %get-tuple-element.41), channel_id=1, source_target_pairs={{0,6},{1,7},{2,4},{3,5},{4,2},{5,3},{6,0},{7,1},{8,14},{9,15},{10,... | collective-permute-start | bytes 589832 | tf_op jit(solution)/shard_map/ppermute | solution.py:203
  94.7 9.1 %collective-permute-start.11 = (bf16[96,1024]{1,0:T(8,128)(2,1)S(1)}, bf16[96,1024]{1,0:T(8,128)(2,1)S(1)}, u32[]{:S(2)}, u32[]{:S(2)}) collective-permute-start(bf16[96,1024]{1,0:T(8,128)(2,1)S(1)} %get-tuple-element.42), channel_id=1, source_target_pairs={{0,7},{1,6},{2,5},{3,4},{4,3},{5,2},{6,1},{7,0},{8,15},{9,14},{10,... | collective-permute-start | bytes 589832 | tf_op jit(solution)/shard_map/ppermute | solution.py:203
  94.9 9.2 %collective-permute-start.3 = (bf16[96,1024]{1,0:T(8,128)(2,1)S(1)}, bf16[96,1024]{1,0:T(8,128)(2,1)S(1)}, u32[]{:S(2)}, u32[]{:S(2)}) collective-permute-start(bf16[96,1024]{1,0:T(8,128)(2,1)S(1)} %get-tuple-element.34), channel_id=1, source_target_pairs={{0,1},{1,0},{2,3},{3,2},{4,5},{5,4},{6,7},{7,6},{8,9},{9,8},{10,11... | collective-permute-start | bytes 589832 | tf_op jit(solution)/shard_map/ppermute | solution.py:203
  95.4 10.6 %collective-permute-start.4 = (bf16[96,1024]{1,0:T(8,128)(2,1)S(1)}, bf16[96,1024]{1,0:T(8,128)(2,1)S(1)}, u32[]{:S(2)}, u32[]{:S(2)}) collective-permute-start(bf16[96,1024]{1,0:T(8,128)(2,1)S(1)} %get-tuple-element.35), channel_id=1, source_target_pairs={{0,2},{1,3},{2,0},{3,1},{4,6},{5,7},{6,4},{7,5},{8,10},{9,11},{10,... | collective-permute-start | bytes 589832 | tf_op jit(solution)/shard_map/ppermute | solution.py:203
  95.4 23.6 %collective-permute-start.5 = (bf16[96,1024]{1,0:T(8,128)(2,1)S(1)}, bf16[96,1024]{1,0:T(8,128)(2,1)S(1)}, u32[]{:S(2)}, u32[]{:S(2)}) collective-permute-start(bf16[96,1024]{1,0:T(8,128)(2,1)S(1)} %get-tuple-element.36), channel_id=1, source_target_pairs={{0,3},{1,2},{2,1},{3,0},{4,7},{5,6},{6,5},{7,4},{8,11},{9,10},{10,... | collective-permute-start | bytes 589832 | tf_op jit(solution)/shard_map/ppermute | solution.py:203
  97.2 73.2 %collective-permute-start.19 = (bf16[2304,256]{1,0:T(8,128)(2,1)S(1)}, bf16[2304,256]{1,0:T(8,128)(2,1)S(1)}, u32[]{:S(2)}, u32[]{:S(2)}) collective-permute-start(bf16[2304,256]{1,0:T(8,128)(2,1)S(1)} %assemble.1.refs_0_), channel_id=1, source_target_pairs={{0,1},{1,0},{2,3},{3,2},{4,5},{5,4},{6,7},{7,6},{8,9},{9,8},{10,11... | collective-permute-start | bytes 3538952 | tf_op jit(solution)/shard_map/ppermute | solution.py:203
  103.8 66.5 %collective-permute-start.23 = (bf16[2304,256]{1,0:T(8,128)(2,1)S(1)}, bf16[2304,256]{1,0:T(8,128)(2,1)S(1)}, u32[]{:S(2)}, u32[]{:S(2)}) collective-permute-start(bf16[2304,256]{1,0:T(8,128)(2,1)S(1)} %collective-permute-done.22.refs_4_), channel_id=1, source_target_pairs={{0,1},{1,0},{2,3},{3,2},{4,5},{5,4},{6,7},{7,6},{8,9},{9,8},{10,11... | collective-permute-start | bytes 3538952 | tf_op jit(solution)/shard_map/ppermute | solution.py:203
  104.1 66.2 %collective-permute-start.21 = (bf16[2304,256]{1,0:T(8,128)(2,1)S(1)}, bf16[2304,256]{1,0:T(8,128)(2,1)S(1)}, u32[]{:S(2)}, u32[]{:S(2)}) collective-permute-start(bf16[2304,256]{1,0:T(8,128)(2,1)S(1)} %collective-permute-done.20.refs_2_), channel_id=1, source_target_pairs={{0,1},{1,0},{2,3},{3,2},{4,5},{5,4},{6,7},{7,6},{8,9},{9,8},{10,11... | collective-permute-start | bytes 3538952 | tf_op jit(solution)/shard_map/ppermute | solution.py:203
  106.0 64.4 %collective-permute-start.26 = (bf16[2304,256]{1,0:T(8,128)(2,1)S(1)}, bf16[2304,256]{1,0:T(8,128)(2,1)S(1)}, u32[]{:S(2)}, u32[]{:S(2)}) collective-permute-start(bf16[2304,256]{1,0:T(8,128)(2,1)S(1)} %constant_dynamic-update-slice_fusion.refs_6_), channel_id=1, source_target_pairs={{0,1},{1,0},{2,3},{3,2},{4,5},{5,4},{6,7},{7,6},{8,9},{9,8},{10,11... | collective-permute-start | bytes 3538952 | tf_op jit(solution)/shard_map/ppermute | solution.py:203
  114.2 38.7 %slice-start.2 = ((s8[8388608]{0:T(1024)(128)(4,1)}), s8[4194304]{0:T(1024)(128)(4,1)S(1)}, s32[]{:S(2)}) async-start(s8[8388608]{0:T(1024)(128)(4,1)} %bitcast.24), calls=%async_computation.2 | async-start | bytes 8388608
  119.0 11.3 %collective-permute-start.8 = (bf16[96,1024]{1,0:T(8,128)(2,1)S(1)}, bf16[96,1024]{1,0:T(8,128)(2,1)S(1)}, u32[]{:S(2)}, u32[]{:S(2)}) collective-permute-start(bf16[96,1024]{1,0:T(8,128)(2,1)S(1)} %get-tuple-element.39), channel_id=1, source_target_pairs={{0,4},{1,5},{2,6},{3,7},{4,0},{5,1},{6,2},{7,3},{8,12},{9,13},{10,... | collective-permute-start | bytes 589832 | tf_op jit(solution)/shard_map/ppermute | solution.py:203
  130.3 22.6 %slice-start.1 = ((s8[8388608]{0:T(1024)(128)(4,1)}), s8[4194304]{0:T(1024)(128)(4,1)S(1)}, s32[]{:S(2)}) async-start(s8[8388608]{0:T(1024)(128)(4,1)} %bitcast.18), calls=%async_computation.1 | async-start | bytes 8388608
  130.3 22.6 %slice-start.3 = ((s8[8388608]{0:T(1024)(128)(4,1)}), s8[4194304]{0:T(1024)(128)(4,1)S(1)}, s32[]{:S(2)}) async-start(s8[8388608]{0:T(1024)(128)(4,1)} %bitcast.24), calls=%async_computation.3 | async-start | bytes 8388608
  130.3 10.9 %collective-permute-start.9 = (bf16[96,1024]{1,0:T(8,128)(2,1)S(1)}, bf16[96,1024]{1,0:T(8,128)(2,1)S(1)}, u32[]{:S(2)}, u32[]{:S(2)}) collective-permute-start(bf16[96,1024]{1,0:T(8,128)(2,1)S(1)} %get-tuple-element.40), channel_id=1, source_target_pairs={{0,5},{1,4},{2,7},{3,6},{4,1},{5,0},{6,3},{7,2},{8,13},{9,12},{10,... | collective-permute-start | bytes 589832 | tf_op jit(solution)/shard_map/ppermute | solution.py:203
  141.2 7.9 %collective-permute-start.12 = (bf16[96,1024]{1,0:T(8,128)(2,1)S(1)}, bf16[96,1024]{1,0:T(8,128)(2,1)S(1)}, u32[]{:S(2)}, u32[]{:S(2)}) collective-permute-start(bf16[96,1024]{1,0:T(8,128)(2,1)S(1)} %get-tuple-element.43), channel_id=1, source_target_pairs={{0,6},{1,7},{2,4},{3,5},{4,2},{5,3},{6,0},{7,1},{8,14},{9,15},{10,... | collective-permute-start | bytes 589832 | tf_op jit(solution)/shard_map/ppermute | solution.py:203
  149.1 8.7 %collective-permute-start.13 = (bf16[96,1024]{1,0:T(8,128)(2,1)S(1)}, bf16[96,1024]{1,0:T(8,128)(2,1)S(1)}, u32[]{:S(2)}, u32[]{:S(2)}) collective-permute-start(bf16[96,1024]{1,0:T(8,128)(2,1)S(1)} %get-tuple-element.44), channel_id=1, source_target_pairs={{0,7},{1,6},{2,5},{3,4},{4,3},{5,2},{6,1},{7,0},{8,15},{9,14},{10,... | collective-permute-start | bytes 589832 | tf_op jit(solution)/shard_map/ppermute | solution.py:203
  159.5 2.1 %collective-permute-start.14 = (bf16[64,1024]{1,0:T(8,128)(2,1)S(1)}, bf16[64,1024]{1,0:T(8,128)(2,1)S(1)}, u32[]{:S(2)}, u32[]{:S(2)}) collective-permute-start(bf16[64,1024]{1,0:T(8,128)(2,1)S(1)} %get-tuple-element.46), channel_id=1, source_target_pairs={{0,1},{1,0},{2,3},{3,2},{4,5},{5,4},{6,7},{7,6},{8,9},{9,8},{10,11... | collective-permute-start | bytes 393224 | tf_op jit(solution)/shard_map/ppermute | solution.py:203
  161.6 8.8 %collective-permute-start.15 = (bf16[64,1024]{1,0:T(8,128)(2,1)S(1)}, bf16[64,1024]{1,0:T(8,128)(2,1)S(1)}, u32[]{:S(2)}, u32[]{:S(2)}) collective-permute-start(bf16[64,1024]{1,0:T(8,128)(2,1)S(1)} %get-tuple-element.47), channel_id=1, source_target_pairs={{1,2},{3,4},{5,6},{2,1},{4,3},{6,5},{9,10},{11,12},{13,14},{10,9},... | collective-permute-start | bytes 393224 | tf_op jit(solution)/shard_map/ppermute | solution.py:251
  (9 other events, 46.7 us)

commit v4 on v3

--- a/solution.py
+++ b/solution.py
@@ -14,27 +14,54 @@
 PARAMS = pltpu.CompilerParams(vmem_limit_bytes=10 * 2**20)
 
 
-def prologue(tok, cells, experts, cap):
+def prologue(place, tok, routes, slots, experts, cap, late):
     count, width = tok.shape
-
-    def kernel(tok_ref, cells_ref, normed_ref, *blocks):
+    strips = routes.shape[0]
+
+    def kernel(place_ref, tok_any, routes_any, slots_any, normed_ref, *refs):
+        blocks, held, sems, tok_ref, routes_ref, slots_ref, loads = refs[:experts], *refs[experts:]
+        fetches = [
+            pltpu.make_async_copy(src, dst, loads.at[i])
+            for i, (src, dst) in enumerate(((tok_any, tok_ref), (routes_any, routes_ref), (slots_any, slots_ref)))
+        ]
+        for c in fetches:
+            c.start()
+        for c in fetches:
+            c.wait()
         x = tok_ref[...].astype(F32)
         centred = x - jnp.mean(x, axis=-1, keepdims=True)
         var = jnp.mean(centred * centred, axis=-1, keepdims=True)
         normed = (centred * lax.rsqrt(var + 1e-06)).astype(BF16)
         normed_ref[...] = normed
-        first, second = cells_ref[0:1, :], cells_ref[1:2, :]
-        for k in range(experts):
+        cells = (routes_ref[...] ^ (2 * place_ref[0] + place_ref[2])) * cap + slots_ref[...]
+        first, second = (jnp.concatenate([cells[i, k : k + 1, :] for i in range(strips)], axis=1) for k in range(2))
+        copies = [
+            pltpu.make_async_copy(held.at[k - late], blocks[k], sems.at[k - late]) for k in range(late, experts)
+        ]
+        for k in [*range(late, experts), *range(late)]:
             rows = lax.broadcasted_iota(jnp.int32, (cap, count), 0) + k * cap
             hot = ((rows == first) | (rows == second)).astype(F32).astype(BF16)
-            blocks[k][...] = jnp.dot(hot, normed, preferred_element_type=F32).astype(BF16)
+            block = jnp.dot(hot, normed, preferred_element_type=F32).astype(BF16)
+            if k >= late:
+                held[k - late] = block
+                copies[k - late].start()
+            else:
+                blocks[k][...] = block
+        for c in copies:
+            c.wait()
 
     outs = [jax.ShapeDtypeStruct((count, width), BF16)]
     outs += [jax.ShapeDtypeStruct((cap, width), BF16)] * experts
     res = pl.pallas_call(
-        kernel, out_shape=outs, in_specs=[VM, VM], out_specs=[VM] * len(outs),
+        kernel, out_shape=outs, in_specs=[SM, ANY, ANY, ANY],
+        out_specs=[VM] * (1 + late) + [ANY] * (experts - late),
+        scratch_shapes=[
+            pltpu.VMEM((experts - late, cap, width), BF16), pltpu.SemaphoreType.DMA((experts - late,)),
+            pltpu.VMEM(tok.shape, BF16), pltpu.VMEM(routes.shape, jnp.int32), pltpu.VMEM(slots.shape, jnp.int32),
+            pltpu.SemaphoreType.DMA((3,)),
+        ],
         compiler_params=PARAMS, name="prologue",
-    )(tok, cells)
+    )(place, tok, routes, slots)
     return res[0], res[1:]
 
 
@@ -235,7 +262,8 @@
     tok = tokens.reshape(count, width)
     routes = route_ids.reshape(count, 2)
     cells = (routes ^ me) * cap + slot_ids.reshape(count, 2)
-    normed, blocks = prologue(tok, cells.T, experts, cap)
+    turned = [ids.reshape(-1, span_cols, 2).transpose(0, 2, 1) for ids in (route_ids, slot_ids)]
+    normed, blocks = prologue(place, tok, *turned, experts, cap, 3 * experts // 4)
     conv_weight, normed = lax.optimization_barrier((conv_weight, normed))
     received = [blocks[0]] + [flip(blocks[k], "expert", k) for k in range(1, experts)]
     mine, theirs = gather_filters(conv_weight, place)

time: 175 us -> 188 us (1.074)
  local copies, waits for them, and re-layouts: 17.1 us -> 38.2 us
  waiting for transfers between devices: 86.1 us -> 75.1 us
  Pallas kernels: 24.5 us -> 29.5 us
  starting transfers between devices: 45.6 us -> 43.6 us
    unnamed x31 -> x83, local copies, waits for them, and re-layouts: 16.6 us -> 34.7 us
    ppermute x26, waiting for transfers between devices: 83.5 us -> 72.5 us  [flip(): lax.ppermute(value, axis, [(i, i ^ k) for i in range(lax.axis_size(axis))])]
    pallas_call x1, Pallas kernels: 4.03 us -> 6.55 us  [conv(): pl.pallas_call(kernel, out_shape=jax.ShapeDtypeStruct((count, 2 * cols),...]
    ppermute x26, starting transfers between devices: 39.5 us -> 37.1 us  [flip(): lax.ppermute(value, axis, [(i, i ^ k) for i in range(lax.axis_size(axis))])]
  transfers between devices with their start and end apart: 27 -> 27, of which waited for: 13 -> 11; matrix products, arithmetic and copies ran while one was open for 0% -> 2% of each run, Pallas kernels for 10% -> 10%
where the time goes in v4:
time: 188 us
  waiting for transfers between devices  75.1 us (40%)
  starting transfers between devices  43.6 us (23%)
  local copies, waits for them, and re-layouts  38.2 us (20%)
  Pallas kernels  29.5 us (16%)
    ppermute x26, waiting for transfers between devices, flip(): lax.ppermute(value, axis, [(i, i ^ k) for i in range(lax.axis_size(axis))])  72.5 us
    ppermute x26, starting transfers between devices, flip(): lax.ppermute(value, axis, [(i, i ^ k) for i in range(lax.axis_size(axis))])  37.1 us
    unnamed x83, local copies, waits for them, and re-layouts  34.7 us
    pallas_call x3, Pallas kernels, mlp(): pl.pallas_call(kernel, in_specs=[VM] * n + [ANY if stream else VM] * 2, o...  16.8 us
    pallas_call x1, Pallas kernels, conv(): pl.pallas_call(kernel, out_shape=jax.ShapeDtypeStruct((count, 2 * cols),...  6.55 us
    ppermute x1, starting transfers between devices, shards(): outer = lax.ppermute(outer, 'expert', joints + [(j, i) for i, j in joints])  6.51 us
  transfers between devices with their start and end apart: 27, of which 11 were waited for; matrix products, arithmetic and copies ran while one was open for 2% of the time, Pallas kernels for 10%

profile of v4, /device:TPU:1, one launch (start us, length us, event | category | flops | bytes accessed | tf_op | source)
XLA Modules:
  0.0 187.6 jit_solution(15972375340864475587)
XLA Ops:
  2.5 2.5 %prologue.1 = (bf16[256,1024]{1,0:T(8,128)(2,1)S(1)}, bf16[96,1024]{1,0:T(8,128)(2,1)S(1)}, bf16[96,1024]{1,0:T(8,128)(2,1)S(1)}, bf16[96,1024]{1,0:T(8,128)(2,1...) custom-call(s32[3]{0:T(128)S(1)} %pad_add_fusion.place_ref, ...), custom_call_target="tpu_custom_call" | custom-call | tf_op jit(solution)/shard_map/prologue/pallas_call | solution.py:55
  8.8 3.2 %collective-permute-start.17 = (bf16[1152,128]{1,0:T(8,128)(2,1)S(1)}, bf16[1152,128]{1,0:T(8,128)(2,1)S(1)}, u32[]{:S(2)}, u32[]{:S(2)}) collective-permute-start(bf16[1152,128]{1,0:T(8,128)(2,1)S(1)} %pad_maximum_fusion.refs_0_), channel_id=1, source_target_pairs={{0,4},{1,5},{2,6},{3,7},{4,0},{5,1},{6,2},{7,3},{8,12},{9,13},{10,... | collective-permute-start | bytes 884744 | tf_op jit(solution)/shard_map/ppermute | solution.py:230
  13.3 11.8 %collective-permute-done.17.refs_2_ = bf16[1152,128]{1,0:T(8,128)(2,1)S(1)} collective-permute-done((bf16[1152,128]{1,0:T(8,128)(2,1)S(1)}, bf16[1152,128]{1,0:T(8,128)(2,1)S(1)}, u32[]{:S(2)}, u32[]{:S(2)}) %collective-permute-start.17) | collective-permute-done | bytes 294944 | tf_op jit(solution)/shard_map/ppermute | solution.py:230
  26.2 6.1 %collective-permute-done.18.refs_3_ = bf16[1152,128]{1,0:T(8,128)(2,1)S(1)} collective-permute-done((bf16[1152,128]{1,0:T(8,128)(2,1)S(1)}, bf16[1152,128]{1,0:T(8,128)(2,1)S(1)}, u32[]{:S(2)}, u32[]{:S(2)}) %collective-permute-start.18) | collective-permute-done | bytes 294944 | tf_op jit(solution)/shard_map/ppermute | solution.py:230
  36.0 23.3 %collective-permute-done.22.refs_4_ = bf16[2304,256]{1,0:T(8,128)(2,1)S(1)} collective-permute-done((bf16[2304,256]{1,0:T(8,128)(2,1)S(1)}, bf16[2304,256]{1,0:T(8,128)(2,1)S(1)}, u32[]{:S(2)}, u32[]{:S(2)}) %collective-permute-start.22) | collective-permute-done | bytes 1179680 | tf_op jit(solution)/shard_map/ppermute | solution.py:230
  62.7 3.5 %collective-permute-start = (bf16[96,1024]{1,0:T(8,128)(2,1)S(1)}, bf16[96,1024]{1,0:T(8,128)(2,1)S(1)}, u32[]{:S(2)}, u32[]{:S(2)}) collective-permute-start(bf16[96,1024]{1,0:T(8,128)(2,1)S(1)} %copy-done.38), channel_id=1, source_target_pairs={{0,1},{1,0},{2,3},{3,2},{4,5},{5,4},{6,7},{7,6},{8,9},{9,8},{10,11... | collective-permute-start | bytes 589832 | tf_op jit(solution)/shard_map/ppermute | solution.py:230
  66.2 2.2 %collective-permute-start.1 = (bf16[96,1024]{1,0:T(8,128)(2,1)S(1)}, bf16[96,1024]{1,0:T(8,128)(2,1)S(1)}, u32[]{:S(2)}, u32[]{:S(2)}) collective-permute-start(bf16[96,1024]{1,0:T(8,128)(2,1)S(1)} %copy-done.36), channel_id=1, source_target_pairs={{0,2},{1,3},{2,0},{3,1},{4,6},{5,7},{6,4},{7,5},{8,10},{9,11},{10,... | collective-permute-start | bytes 589832 | tf_op jit(solution)/shard_map/ppermute | solution.py:230
  68.5 3.6 %collective-permute-start.6 = (bf16[96,1024]{1,0:T(8,128)(2,1)S(1)}, bf16[96,1024]{1,0:T(8,128)(2,1)S(1)}, u32[]{:S(2)}, u32[]{:S(2)}) collective-permute-start(bf16[96,1024]{1,0:T(8,128)(2,1)S(1)} %copy-done.32), channel_id=1, source_target_pairs={{0,4},{1,5},{2,6},{3,7},{4,0},{5,1},{6,2},{7,3},{8,12},{9,13},{10,... | collective-permute-start | bytes 589832 | tf_op jit(solution)/shard_map/ppermute | solution.py:230
  72.1 5.8 %collective-permute-done.1.refs_2_ = bf16[96,1024]{1,0:T(8,128)(2,1)S(1)} collective-permute-done((bf16[96,1024]{1,0:T(8,128)(2,1)S(1)}, bf16[96,1024]{1,0:T(8,128)(2,1)S(1)}, u32[]{:S(2)}, u32[]{:S(2)}) %collective-permute-start.1) | collective-permute-done | bytes 196640 | tf_op jit(solution)/shard_map/ppermute | solution.py:230
  77.8 3.4 %collective-permute-start.7 = (bf16[96,1024]{1,0:T(8,128)(2,1)S(1)}, bf16[96,1024]{1,0:T(8,128)(2,1)S(1)}, u32[]{:S(2)}, u32[]{:S(2)}) collective-permute-start(bf16[96,1024]{1,0:T(8,128)(2,1)S(1)} %copy-done.30), channel_id=1, source_target_pairs={{0,5},{1,4},{2,7},{3,6},{4,1},{5,0},{6,3},{7,2},{8,13},{9,12},{10,... | collective-permute-start | bytes 589832 | tf_op jit(solution)/shard_map/ppermute | solution.py:230
  82.3 4.0 %collective-permute-start.10 = (bf16[96,1024]{1,0:T(8,128)(2,1)S(1)}, bf16[96,1024]{1,0:T(8,128)(2,1)S(1)}, u32[]{:S(2)}, u32[]{:S(2)}) collective-permute-start(bf16[96,1024]{1,0:T(8,128)(2,1)S(1)} %copy-done.28), channel_id=1, source_target_pairs={{0,6},{1,7},{2,4},{3,5},{4,2},{5,3},{6,0},{7,1},{8,14},{9,15},{10,... | collective-permute-start | bytes 589832 | tf_op jit(solution)/shard_map/ppermute | solution.py:230
  86.4 3.4 %copy-done.1 = bf16[1,4096,1024]{2,1,0:T(8,128)(2,1)S(1)} copy-done((bf16[1,4096,1024]{2,1,0:T(8,128)(2,1)S(1)}, bf16[1,4096,1024]{2,1,0:T(8,128)(2,1)}, u32[]{:S(2)}) %copy-start.1) | copy-done | bytes 8388632
  89.7 3.4 %copy-done.5 = bf16[1,4096,1024]{2,1,0:T(8,128)(2,1)S(1)} copy-done((bf16[1,4096,1024]{2,1,0:T(8,128)(2,1)S(1)}, bf16[1,4096,1024]{2,1,0:T(8,128)(2,1)}, u32[]{:S(2)}) %copy-start.5) | copy-done | bytes 8388632
  93.1 6.8 %shard_map.73 = (bf16[96,1024]{1,0:T(8,128)(2,1)S(1)}, bf16[96,1024]{1,0:T(8,128)(2,1)S(1)}, bf16[96,1024]{1,0:T(8,128)(2,1)S(1)}, bf16[96,1024]{1,0:T(8,128)(2,1)S(1)}) custom-call(bf16[96,1024]{1,0:T(8,128)(2,1)S(1)} %get-tuple-element.29.refs_0_, bf16[96,1024]{1,0:T(8,128)(2,1)S(1)} %collective-permute-done.refs_1_, ...), custom_call_target="tpu_custom_call" | custom-call | tf_op jit(solution)/shard_map/pallas_call | solution.py:111
  101.3 1.8 collective-permute-start.5
  104.0 5.0 %collective-permute-done.11.refs_1_ = bf16[96,1024]{1,0:T(8,128)(2,1)S(1)} collective-permute-done((bf16[96,1024]{1,0:T(8,128)(2,1)S(1)}, bf16[96,1024]{1,0:T(8,128)(2,1)S(1)}, u32[]{:S(2)}, u32[]{:S(2)}) %collective-permute-start.11) | collective-permute-done | bytes 196640 | tf_op jit(solution)/shard_map/ppermute | solution.py:230
  109.6 2.3 %collective-permute-done.4.refs_2_ = bf16[96,1024]{1,0:T(8,128)(2,1)S(1)} collective-permute-done((bf16[96,1024]{1,0:T(8,128)(2,1)S(1)}, bf16[96,1024]{1,0:T(8,128)(2,1)S(1)}, u32[]{:S(2)}, u32[]{:S(2)}) %collective-permute-start.4) | collective-permute-done | bytes 196640 | tf_op jit(solution)/shard_map/ppermute | solution.py:230
  113.4 3.4 %copy-done.2 = bf16[1,4096,1024]{2,1,0:T(8,128)(2,1)S(1)} copy-done((bf16[1,4096,1024]{2,1,0:T(8,128)(2,1)S(1)}, bf16[1,4096,1024]{2,1,0:T(8,128)(2,1)}, u32[]{:S(2)}) %copy-start.2) | copy-done | bytes 8388632
  116.8 3.4 %copy-done.6 = bf16[1,4096,1024]{2,1,0:T(8,128)(2,1)S(1)} copy-done((bf16[1,4096,1024]{2,1,0:T(8,128)(2,1)S(1)}, bf16[1,4096,1024]{2,1,0:T(8,128)(2,1)}, u32[]{:S(2)}) %copy-start.6) | copy-done | bytes 8388632
  120.2 5.4 %shard_map.74 = (bf16[96,1024]{1,0:T(8,128)(2,1)S(1)}, bf16[96,1024]{1,0:T(8,128)(2,1)}) custom-call(bf16[96,1024]{1,0:T(8,128)(2,1)S(1)} %collective-permute-done.6.refs_0_, bf16[96,1024]{1,0:T(8,128)(2,1)S(1)} %collective-permute-done.7.refs_1_, bf16[4096,1024]{1,0:T(8,128)(2,1)S(1)} %bitcast.21, bf16[4096,1024]{1,0:T(8,128)(2,1)S(1)} %bitcast.25), custom_call_target="tpu_custom_call" | custom-call | tf_op jit(solution)/shard_map/pallas_call | solution.py:111
  127.1 10.1 %collective-permute-done.8.refs_4_ = bf16[96,1024]{1,0:T(8,128)(2,1)S(1)} collective-permute-done((bf16[96,1024]{1,0:T(8,128)(2,1)S(1)}, bf16[96,1024]{1,0:T(8,128)(2,1)S(1)}, u32[]{:S(2)}, u32[]{:S(2)}) %collective-permute-start.8) | collective-permute-done | bytes 196640 | tf_op jit(solution)/shard_map/ppermute | solution.py:230
  138.9 3.4 %copy-done.3 = bf16[1,4096,1024]{2,1,0:T(8,128)(2,1)S(1)} copy-done((bf16[1,4096,1024]{2,1,0:T(8,128)(2,1)S(1)}, bf16[1,4096,1024]{2,1,0:T(8,128)(2,1)}, u32[]{:S(2)}) %copy-start.3) | copy-done | bytes 8388632
  142.2 3.4 %copy-done.7 = bf16[1,4096,1024]{2,1,0:T(8,128)(2,1)S(1)} copy-done((bf16[1,4096,1024]{2,1,0:T(8,128)(2,1)S(1)}, bf16[1,4096,1024]{2,1,0:T(8,128)(2,1)}, u32[]{:S(2)}) %copy-start.7) | copy-done | bytes 8388632
  145.6 4.6 %shard_map.75 = (bf16[96,1024]{1,0:T(8,128)(2,1)S(1)}, bf16[96,1024]{1,0:T(8,128)(2,1)S(1)}) custom-call(bf16[96,1024]{1,0:T(8,128)(2,1)S(1)} %collective-permute-done.10.refs_0_, bf16[96,1024]{1,0:T(8,128)(2,1)S(1)} %collective-permute-done.11.refs_1_, bf16[4096,1024]{1,0:T(8,128)(2,1)S(1)} %bitcast.22, bf16[4096,1024]{1,0:T(8,128)(2,1)S(1)} %bitcast.26), custom_call_target="tpu_custom_call" | custom-call | tf_op jit(solution)/shard_map/pallas_call | solution.py:111
  151.7 3.4 %copy-done.4 = bf16[1,4096,1024]{2,1,0:T(8,128)(2,1)S(1)} copy-done((bf16[1,4096,1024]{2,1,0:T(8,128)(2,1)S(1)}, bf16[1,4096,1024]{2,1,0:T(8,128)(2,1)}, u32[]{:S(2)}) %copy-start.4) | copy-done | bytes 8388632
  155.1 3.4 %copy-done.8 = bf16[1,4096,1024]{2,1,0:T(8,128)(2,1)S(1)} copy-done((bf16[1,4096,1024]{2,1,0:T(8,128)(2,1)S(1)}, bf16[1,4096,1024]{2,1,0:T(8,128)(2,1)}, u32[]{:S(2)}) %copy-start.8) | copy-done | bytes 8388632
  158.8 3.0 %collective-permute-start.13 = (bf16[96,1024]{1,0:T(8,128)(2,1)S(1)}, bf16[96,1024]{1,0:T(8,128)(2,1)S(1)}, u32[]{:S(2)}, u32[]{:S(2)}) collective-permute-start(bf16[96,1024]{1,0:T(8,128)(2,1)S(1)} %get-tuple-element.44), channel_id=1, source_target_pairs={{0,7},{1,6},{2,5},{3,4},{4,3},{5,2},{6,1},{7,0},{8,15},{9,14},{10,... | collective-permute-start | bytes 589832 | tf_op jit(solution)/shard_map/ppermute | solution.py:230
  161.9 6.0 %collective-permute-done.13.refs_7_ = bf16[96,1024]{1,0:T(8,128)(2,1)S(1)} collective-permute-done((bf16[96,1024]{1,0:T(8,128)(2,1)S(1)}, bf16[96,1024]{1,0:T(8,128)(2,1)S(1)}, u32[]{:S(2)}, u32[]{:S(2)}) %collective-permute-start.13) | collective-permute-done | bytes 196640 | tf_op jit(solution)/shard_map/ppermute | solution.py:230
  168.0 2.0 %combine.1 = (bf16[256,1024]{1,0:T(8,128)(2,1)S(1)}, bf16[64,1024]{1,0:T(8,128)(2,1)S(1)}, bf16[64,1024]{1,0:T(8,128)(2,1)S(1)}) custom-call(s32[3]{0:T(128)S(1)} %pad_add_fusion.place_ref, bf16[256,1024]{1,0:T(8,128)(2,1)S(1)} %bitcast.29, f32[256,2]{1,0:T(8,128)S(1)} %gate.1.gates_ref, s32[256,2]{1,0:T(8,128)S(1)} %bitcast_add_fusion.cells_ref, ...), custom_call_target="tpu_custom_call" | custom-call | tf_op jit(solution)/shard_map/combine/pallas_call | solution.py:155
  171.8 6.5 %collective-permute-start.15 = (bf16[64,1024]{1,0:T(8,128)(2,1)S(1)}, bf16[64,1024]{1,0:T(8,128)(2,1)S(1)}, u32[]{:S(2)}, u32[]{:S(2)}) collective-permute-start(bf16[64,1024]{1,0:T(8,128)(2,1)S(1)} %get-tuple-element.47), channel_id=1, source_target_pairs={{1,2},{3,4},{5,6},{2,1},{4,3},{6,5},{9,10},{11,12},{13,14},{10,9},... | collective-permute-start | bytes 393224 | tf_op jit(solution)/shard_map/ppermute | solution.py:279
  178.4 2.6 %collective-permute-done.15.outer_ref = bf16[64,1024]{1,0:T(8,128)(2,1)S(1)} collective-permute-done((bf16[64,1024]{1,0:T(8,128)(2,1)S(1)}, bf16[64,1024]{1,0:T(8,128)(2,1)S(1)}, u32[]{:S(2)}, u32[]{:S(2)}) %collective-permute-start.15) | collective-permute-done | bytes 131104 | tf_op jit(solution)/shard_map/ppermute | solution.py:279
  181.0 6.5 %conv.1 = bf16[256,512]{1,0:T(8,128)(2,1)} custom-call(s32[3]{0:T(128)S(1)} %pad_add_fusion.place_ref, bf16[256,1024]{1,0:T(8,128)(2,1)S(1)} %get-tuple-element.45.mixed_ref, bf16[64,1024]{1,0:T(8,128)(2,1)S(1)} %collective-permute-done.14.inner_ref, bf16[64,1024]{1,0:T(8,128)(2,1)S(1)} %collective-permute-done.15.outer_ref, ...), custom_call_target="tpu_custom_call" | custom-call | tf_op jit(solution)/shard_map/conv/pallas_call | solution.py:221
  (122 shorter events, 28.0 us)
Async XLA Ops:
  0.0 151.2 %copy-start = (f32[1024,8]{0,1:T(8,128)S(1)}, f32[1024,8]{0,1:T(8,128)}, u32[]{:S(2)}) copy-start(f32[1024,8]{0,1:T(8,128)} %param.10) | copy-start | bytes 98308
  8.8 16.3 %collective-permute-start.17 = (bf16[1152,128]{1,0:T(8,128)(2,1)S(1)}, bf16[1152,128]{1,0:T(8,128)(2,1)S(1)}, u32[]{:S(2)}, u32[]{:S(2)}) collective-permute-start(bf16[1152,128]{1,0:T(8,128)(2,1)S(1)} %pad_maximum_fusion.refs_0_), channel_id=1, source_target_pairs={{0,4},{1,5},{2,6},{3,7},{4,0},{5,1},{6,2},{7,3},{8,12},{9,13},{10,... | collective-permute-start | bytes 884744 | tf_op jit(solution)/shard_map/ppermute | solution.py:230
  12.0 14.2 %collective-permute-start.16 = (bf16[1152,128]{1,0:T(8,128)(2,1)S(1)}, bf16[1152,128]{1,0:T(8,128)(2,1)S(1)}, u32[]{:S(2)}, u32[]{:S(2)}) collective-permute-start(bf16[1152,128]{1,0:T(8,128)(2,1)S(1)} %pad_maximum_fusion.refs_0_), channel_id=1, source_target_pairs={{0,2},{1,3},{2,0},{3,1},{4,6},{5,7},{6,4},{7,5},{8,10},{9,11},{10,... | collective-permute-start | bytes 884744 | tf_op jit(solution)/shard_map/ppermute | solution.py:230
  25.1 7.3 %collective-permute-start.18 = (bf16[1152,128]{1,0:T(8,128)(2,1)S(1)}, bf16[1152,128]{1,0:T(8,128)(2,1)S(1)}, u32[]{:S(2)}, u32[]{:S(2)}) collective-permute-start(bf16[1152,128]{1,0:T(8,128)(2,1)S(1)} %collective-permute-done.17.refs_2_), channel_id=1, source_target_pairs={{0,2},{1,3},{2,0},{3,1},{4,6},{5,7},{6,4},{7,5},{8,10},{9,11},{10,... | collective-permute-start | bytes 884744 | tf_op jit(solution)/shard_map/ppermute | solution.py:230
  33.7 44.2 %copy-start.30 = (bf16[96,1024]{1,0:T(8,128)(2,1)S(1)}, bf16[96,1024]{1,0:T(8,128)(2,1)}, u32[]{:S(2)}) copy-start(bf16[96,1024]{1,0:T(8,128)(2,1)} %copy-done.29) | copy-start | bytes 589828
  33.7 48.6 %copy-start.28 = (bf16[96,1024]{1,0:T(8,128)(2,1)S(1)}, bf16[96,1024]{1,0:T(8,128)(2,1)}, u32[]{:S(2)}) copy-start(bf16[96,1024]{1,0:T(8,128)(2,1)} %copy-done.27) | copy-start | bytes 589828
  33.7 25.5 %collective-permute-start.22 = (bf16[2304,256]{1,0:T(8,128)(2,1)S(1)}, bf16[2304,256]{1,0:T(8,128)(2,1)S(1)}, u32[]{:S(2)}, u32[]{:S(2)}) collective-permute-start(bf16[2304,256]{1,0:T(8,128)(2,1)S(1)} %assemble.1.refs_0_), channel_id=1, source_target_pairs={{0,16},{8,24},{16,0},{24,8},{1,17},{9,25},{17,1},{25,9},{2,18},{10... | collective-permute-start | bytes 3538952 | tf_op jit(solution)/shard_map/ppermute | solution.py:230
  34.8 25.5 %collective-permute-start.20 = (bf16[2304,256]{1,0:T(8,128)(2,1)S(1)}, bf16[2304,256]{1,0:T(8,128)(2,1)}, u32[]{:S(2)}, u32[]{:S(2)}) collective-permute-start(bf16[2304,256]{1,0:T(8,128)(2,1)S(1)} %assemble.1.refs_0_), channel_id=1, source_target_pairs={{0,8},{8,0},{16,24},{24,16},{1,9},{9,1},{17,25},{25,17},{2,10},{10... | collective-permute-start | bytes 3538952 | tf_op jit(solution)/shard_map/ppermute | solution.py:230
  59.3 40.6 %collective-permute-start.24 = (bf16[1152,256]{1,0:T(8,128)(2,1)S(1)}, bf16[1152,256]{1,0:T(8,128)(2,1)S(1)}, u32[]{:S(2)}, u32[]{:S(2)}) collective-permute-start(bf16[1152,256]{1,0:T(8,128)(2,1)S(1)} %slice.18), channel_id=1, source_target_pairs={{0,8},{8,0},{16,24},{24,16},{1,9},{9,1},{17,25},{25,17},{2,10},{10... | collective-permute-start | bytes 1769480 | tf_op jit(solution)/shard_map/ppermute | solution.py:230
  61.4 39.9 %collective-permute-start.25 = (bf16[1152,256]{1,0:T(8,128)(2,1)S(1)}, bf16[1152,256]{1,0:T(8,128)(2,1)S(1)}, u32[]{:S(2)}, u32[]{:S(2)}) collective-permute-start(bf16[1152,256]{1,0:T(8,128)(2,1)S(1)} %slice.19), channel_id=1, source_target_pairs={{0,16},{8,24},{16,0},{24,8},{1,17},{9,25},{17,1},{25,9},{2,18},{10... | collective-permute-start | bytes 1769480 | tf_op jit(solution)/shard_map/ppermute | solution.py:230
  62.7 5.8 %collective-permute-start = (bf16[96,1024]{1,0:T(8,128)(2,1)S(1)}, bf16[96,1024]{1,0:T(8,128)(2,1)S(1)}, u32[]{:S(2)}, u32[]{:S(2)}) collective-permute-start(bf16[96,1024]{1,0:T(8,128)(2,1)S(1)} %copy-done.38), channel_id=1, source_target_pairs={{0,1},{1,0},{2,3},{3,2},{4,5},{5,4},{6,7},{7,6},{8,9},{9,8},{10,11... | collective-permute-start | bytes 589832 | tf_op jit(solution)/shard_map/ppermute | solution.py:230
  66.2 11.6 %collective-permute-start.1 = (bf16[96,1024]{1,0:T(8,128)(2,1)S(1)}, bf16[96,1024]{1,0:T(8,128)(2,1)S(1)}, u32[]{:S(2)}, u32[]{:S(2)}) collective-permute-start(bf16[96,1024]{1,0:T(8,128)(2,1)S(1)} %copy-done.36), channel_id=1, source_target_pairs={{0,2},{1,3},{2,0},{3,1},{4,6},{5,7},{6,4},{7,5},{8,10},{9,11},{10,... | collective-permute-start | bytes 589832 | tf_op jit(solution)/shard_map/ppermute | solution.py:230
  68.4 13.9 %collective-permute-start.2 = (bf16[96,1024]{1,0:T(8,128)(2,1)S(1)}, bf16[96,1024]{1,0:T(8,128)(2,1)S(1)}, u32[]{:S(2)}, u32[]{:S(2)}) collective-permute-start(bf16[96,1024]{1,0:T(8,128)(2,1)S(1)} %copy-done.34), channel_id=1, source_target_pairs={{0,3},{1,2},{2,1},{3,0},{4,7},{5,6},{6,5},{7,4},{8,11},{9,10},{10,... | collective-permute-start | bytes 589832 | tf_op jit(solution)/shard_map/ppermute | solution.py:230
  68.5 32.4 %collective-permute-start.6 = (bf16[96,1024]{1,0:T(8,128)(2,1)S(1)}, bf16[96,1024]{1,0:T(8,128)(2,1)S(1)}, u32[]{:S(2)}, u32[]{:S(2)}) collective-permute-start(bf16[96,1024]{1,0:T(8,128)(2,1)S(1)} %copy-done.32), channel_id=1, source_target_pairs={{0,4},{1,5},{2,6},{3,7},{4,0},{5,1},{6,2},{7,3},{8,12},{9,13},{10,... | collective-permute-start | bytes 589832 | tf_op jit(solution)/shard_map/ppermute | solution.py:230
  77.8 23.4 %collective-permute-start.7 = (bf16[96,1024]{1,0:T(8,128)(2,1)S(1)}, bf16[96,1024]{1,0:T(8,128)(2,1)S(1)}, u32[]{:S(2)}, u32[]{:S(2)}) collective-permute-start(bf16[96,1024]{1,0:T(8,128)(2,1)S(1)} %copy-done.30), channel_id=1, source_target_pairs={{0,5},{1,4},{2,7},{3,6},{4,1},{5,0},{6,3},{7,2},{8,13},{9,12},{10,... | collective-permute-start | bytes 589832 | tf_op jit(solution)/shard_map/ppermute | solution.py:230
  82.3 21.6 %collective-permute-start.10 = (bf16[96,1024]{1,0:T(8,128)(2,1)S(1)}, bf16[96,1024]{1,0:T(8,128)(2,1)S(1)}, u32[]{:S(2)}, u32[]{:S(2)}) collective-permute-start(bf16[96,1024]{1,0:T(8,128)(2,1)S(1)} %copy-done.28), channel_id=1, source_target_pairs={{0,6},{1,7},{2,4},{3,5},{4,2},{5,3},{6,0},{7,1},{8,14},{9,15},{10,... | collective-permute-start | bytes 589832 | tf_op jit(solution)/shard_map/ppermute | solution.py:230
  99.9 9.1 %collective-permute-start.11 = (bf16[96,1024]{1,0:T(8,128)(2,1)S(1)}, bf16[96,1024]{1,0:T(8,128)(2,1)S(1)}, u32[]{:S(2)}, u32[]{:S(2)}) collective-permute-start(bf16[96,1024]{1,0:T(8,128)(2,1)S(1)} %copy-done.26), channel_id=1, source_target_pairs={{0,7},{1,6},{2,5},{3,4},{4,3},{5,2},{6,1},{7,0},{8,15},{9,14},{10,... | collective-permute-start | bytes 589832 | tf_op jit(solution)/shard_map/ppermute | solution.py:230
  100.9 8.3 %collective-permute-start.3 = (bf16[96,1024]{1,0:T(8,128)(2,1)S(1)}, bf16[96,1024]{1,0:T(8,128)(2,1)S(1)}, u32[]{:S(2)}, u32[]{:S(2)}) collective-permute-start(bf16[96,1024]{1,0:T(8,128)(2,1)S(1)} %get-tuple-element.34), channel_id=1, source_target_pairs={{0,1},{1,0},{2,3},{3,2},{4,5},{5,4},{6,7},{7,6},{8,9},{9,8},{10,11... | collective-permute-start | bytes 589832 | tf_op jit(solution)/shard_map/ppermute | solution.py:230
  101.3 10.5 %collective-permute-start.4 = (bf16[96,1024]{1,0:T(8,128)(2,1)S(1)}, bf16[96,1024]{1,0:T(8,128)(2,1)S(1)}, u32[]{:S(2)}, u32[]{:S(2)}) collective-permute-start(bf16[96,1024]{1,0:T(8,128)(2,1)S(1)} %get-tuple-element.35), channel_id=1, source_target_pairs={{0,2},{1,3},{2,0},{3,1},{4,6},{5,7},{6,4},{7,5},{8,10},{9,11},{10,... | collective-permute-start | bytes 589832 | tf_op jit(solution)/shard_map/ppermute | solution.py:230
  101.3 24.3 %collective-permute-start.5 = (bf16[96,1024]{1,0:T(8,128)(2,1)S(1)}, bf16[96,1024]{1,0:T(8,128)(2,1)S(1)}, u32[]{:S(2)}, u32[]{:S(2)}) collective-permute-start(bf16[96,1024]{1,0:T(8,128)(2,1)S(1)} %get-tuple-element.36), channel_id=1, source_target_pairs={{0,3},{1,2},{2,1},{3,0},{4,7},{5,6},{6,5},{7,4},{8,11},{9,10},{10,... | collective-permute-start | bytes 589832 | tf_op jit(solution)/shard_map/ppermute | solution.py:230
  103.0 34.9 %copy-start.22 = (s32[1,4,64,2]{2,3,1,0:T(2,128)S(1)}, s32[1,4,64,2]{2,3,1,0:T(2,128)}, u32[]{:S(2)}) copy-start(s32[1,4,64,2]{2,3,1,0:T(2,128)} %param.8) | copy-start | bytes 6148
  103.0 35.0 %copy-start.24 = (s32[1,4,64,2]{2,3,1,0:T(2,128)S(1)}, s32[1,4,64,2]{2,3,1,0:T(2,128)}, u32[]{:S(2)}) copy-start(s32[1,4,64,2]{2,3,1,0:T(2,128)} %param.9) | copy-start | bytes 6148
  103.9 77.1 %collective-permute-start.19 = (bf16[2304,256]{1,0:T(8,128)(2,1)S(1)}, bf16[2304,256]{1,0:T(8,128)(2,1)}, u32[]{:S(2)}, u32[]{:S(2)}) collective-permute-start(bf16[2304,256]{1,0:T(8,128)(2,1)S(1)} %assemble.1.refs_0_), channel_id=1, source_target_pairs={{0,1},{1,0},{2,3},{3,2},{4,5},{5,4},{6,7},{7,6},{8,9},{9,8},{10,11... | collective-permute-start | bytes 3538952 | tf_op jit(solution)/shard_map/ppermute | solution.py:230
  109.0 72.0 %collective-permute-start.23 = (bf16[2304,256]{1,0:T(8,128)(2,1)S(1)}, bf16[2304,256]{1,0:T(8,128)(2,1)}, u32[]{:S(2)}, u32[]{:S(2)}) collective-permute-start(bf16[2304,256]{1,0:T(8,128)(2,1)S(1)} %collective-permute-done.22.refs_4_), channel_id=1, source_target_pairs={{0,1},{1,0},{2,3},{3,2},{4,5},{5,4},{6,7},{7,6},{8,9},{9,8},{10,11... | collective-permute-start | bytes 3538952 | tf_op jit(solution)/shard_map/ppermute | solution.py:230
  109.2 71.8 %collective-permute-start.21 = (bf16[2304,256]{1,0:T(8,128)(2,1)}, bf16[2304,256]{1,0:T(8,128)(2,1)}, u32[]{:S(2)}, u32[]{:S(2)}) collective-permute-start(bf16[2304,256]{1,0:T(8,128)(2,1)} %collective-permute-done.20.refs_2_), channel_id=1, source_target_pairs={{0,1},{1,0},{2,3},{3,2},{4,5},{5,4},{6,7},{7,6},{8,9},{9,8},{10,11... | collective-permute-start | bytes 3538952 | tf_op jit(solution)/shard_map/ppermute | solution.py:230
  111.8 69.2 %collective-permute-start.26 = (bf16[2304,256]{1,0:T(8,128)(2,1)}, bf16[2304,256]{1,0:T(8,128)(2,1)}, u32[]{:S(2)}, u32[]{:S(2)}) collective-permute-start(bf16[2304,256]{1,0:T(8,128)(2,1)} %constant_dynamic-update-slice_fusion.refs_6_), channel_id=1, source_target_pairs={{0,1},{1,0},{2,3},{3,2},{4,5},{5,4},{6,7},{7,6},{8,9},{9,8},{10,11... | collective-permute-start | bytes 3538952 | tf_op jit(solution)/shard_map/ppermute | solution.py:230
  126.3 11.0 %collective-permute-start.8 = (bf16[96,1024]{1,0:T(8,128)(2,1)S(1)}, bf16[96,1024]{1,0:T(8,128)(2,1)S(1)}, u32[]{:S(2)}, u32[]{:S(2)}) collective-permute-start(bf16[96,1024]{1,0:T(8,128)(2,1)S(1)} %get-tuple-element.39), channel_id=1, source_target_pairs={{0,4},{1,5},{2,6},{3,7},{4,0},{5,1},{6,2},{7,3},{8,12},{9,13},{10,... | collective-permute-start | bytes 589832 | tf_op jit(solution)/shard_map/ppermute | solution.py:230
  137.9 12.3 %collective-permute-start.9 = (bf16[96,1024]{1,0:T(8,128)(2,1)}, bf16[96,1024]{1,0:T(8,128)(2,1)}, u32[]{:S(2)}, u32[]{:S(2)}) collective-permute-start(bf16[96,1024]{1,0:T(8,128)(2,1)} %get-tuple-element.40), channel_id=1, source_target_pairs={{0,5},{1,4},{2,7},{3,6},{4,1},{5,0},{6,3},{7,2},{8,13},{9,12},{10,... | collective-permute-start | bytes 589832 | tf_op jit(solution)/shard_map/ppermute | solution.py:230
  150.2 8.6 %collective-permute-start.12 = (bf16[96,1024]{1,0:T(8,128)(2,1)S(1)}, bf16[96,1024]{1,0:T(8,128)(2,1)S(1)}, u32[]{:S(2)}, u32[]{:S(2)}) collective-permute-start(bf16[96,1024]{1,0:T(8,128)(2,1)S(1)} %get-tuple-element.43), channel_id=1, source_target_pairs={{0,6},{1,7},{2,4},{3,5},{4,2},{5,3},{6,0},{7,1},{8,14},{9,15},{10,... | collective-permute-start | bytes 589832 | tf_op jit(solution)/shard_map/ppermute | solution.py:230
  158.8 9.1 %collective-permute-start.13 = (bf16[96,1024]{1,0:T(8,128)(2,1)S(1)}, bf16[96,1024]{1,0:T(8,128)(2,1)S(1)}, u32[]{:S(2)}, u32[]{:S(2)}) collective-permute-start(bf16[96,1024]{1,0:T(8,128)(2,1)S(1)} %get-tuple-element.44), channel_id=1, source_target_pairs={{0,7},{1,6},{2,5},{3,4},{4,3},{5,2},{6,1},{7,0},{8,15},{9,14},{10,... | collective-permute-start | bytes 589832 | tf_op jit(solution)/shard_map/ppermute | solution.py:230
  170.1 1.8 collective-permute-start.14
  171.8 9.2 %collective-permute-start.15 = (bf16[64,1024]{1,0:T(8,128)(2,1)S(1)}, bf16[64,1024]{1,0:T(8,128)(2,1)S(1)}, u32[]{:S(2)}, u32[]{:S(2)}) collective-permute-start(bf16[64,1024]{1,0:T(8,128)(2,1)S(1)} %get-tuple-element.47), channel_id=1, source_target_pairs={{1,2},{3,4},{5,6},{2,1},{4,3},{6,5},{9,10},{11,12},{13,14},{10,9},... | collective-permute-start | bytes 393224 | tf_op jit(solution)/shard_map/ppermute | solution.py:279
  (35 other events, 272.3 us)
